TPU v7x, 32 devices: a whole 2x2x4 slice. The times are simulated.
32 devices in a mesh: dp: 8 (over z, y), chan: 4 (over x, core).
Axes of the slice: x: 2, y: 2, z: 4, core: 2. Of those that a mesh axis runs over, the one named last changes fastest.
Arguments:
- tokens: bfloat16 [640, 65536], P('chan', 'dp'), may hold values from -6 to 6
- weights: bfloat16 [3, 640, 1280], P(None, 'chan', 'dp'), may hold values from -0.15625 to 0.15625
- bias: float32 [3, 640], P(None, 'chan'), may hold values from -3 to 8
- segment_ids: int32 [65536], P('dp'), may hold values from 0 to 191, never falling along the last dimension, each value on 1 to 1024 neighbouring positions
- cotangent: bfloat16 [640, 65536], P('chan', 'dp'), may hold values from -6 to 6
Outputs:
- hidden: bfloat16 [640, 65536], P('chan', 'dp')
- input_grad: bfloat16 [640, 65536], P('chan', 'dp')
- weight_grad: float32 [3, 640, 1280], P(None, 'chan', 'dp')
- bias_grad: float32 [3, 640], P(None, 'chan')
All inputs are finite; a program needn't handle non-finite values.
Results may differ from a plain program's by a relative error of at most 0.0051.
Values may be sent and summed in bfloat16 or wider, within the bound.
No kernel may reach another device: no remote copies, remote signals or barrier semaphores. Data moves between devices by JAX's collectives and lax.ppermute only.
A program may use at most 320 MiB of HBM per device.

v0:
```python
import jax
import jax.numpy as jnp
from jax import lax
from jax.sharding import PartitionSpec as P

LEN = 1024
MICRO = 4


def combine(earlier, later):
    return (earlier[0] * later[0], later[0] * earlier[1] + later[1])


def local(tokens, weights, bias, segment_ids, cotangent):
    width_part, total_rows = tokens.shape
    batch_rows = total_rows // MICRO
    grad_shard = jnp.zeros(weights.shape, jnp.float32)
    bias_total = jnp.zeros(bias.shape, jnp.float32)
    position = jnp.arange(batch_rows) % LEN
    hidden_parts = []
    input_parts = []
    for micro in range(MICRO):
        lower = micro * batch_rows
        upper = lower + batch_rows
        part_in = tokens[:, lower:upper]
        ids = segment_ids[lower:upper]
        cot = cotangent[:, lower:upper].astype(jnp.float32)
        before = jnp.concatenate([ids[:1], ids[:-1]], 0)
        carry_flag = (position > 0) & (ids == before)
        carry_on = jnp.where(carry_flag, 1.0, 0.0).astype(jnp.float32)
        gathered = lax.all_gather(part_in, "chan", axis=0, tiled=True)
        width = gathered.shape[0]
        shifted = jnp.concatenate([jnp.zeros((width, 1), jnp.bfloat16), gathered[:, :-1]], 1)
        previous = jnp.where(carry_flag[None, :], shifted, jnp.zeros((), jnp.bfloat16))
        joined_inputs = jnp.concatenate([gathered, previous], 0)
        preactivation = jnp.einsum(
            "gcr,rl->gcl",
            lax.all_gather(weights, "dp", axis=2, tiled=True),
            joined_inputs,
            preferred_element_type=jnp.float32,
        )
        preactivation = preactivation + bias[:, :, None]
        gate_z = jnp.tanh(preactivation[0])
        forget = jax.nn.sigmoid(preactivation[1])
        output_gate = jax.nn.sigmoid(preactivation[2])
        decay = forget * carry_on[None, :]
        source = (1.0 - forget) * gate_z
        cell = lax.associative_scan(combine, (decay, source), axis=1)[1]
        hidden_parts.append((output_gate * cell).astype(jnp.bfloat16))
        decay_next = jnp.concatenate([decay[:, 1:], jnp.zeros((width_part, 1), jnp.float32)], 1)
        dcell = lax.associative_scan(
            combine, (decay_next, cot * output_gate), reverse=True, axis=1
        )[1]
        cell_before = (
            jnp.concatenate([jnp.zeros((width_part, 1), jnp.float32), cell[:, :-1]], 1)
            * carry_on[None, :]
        )
        grad_z = dcell * (1.0 - forget) * (1.0 - gate_z * gate_z)
        grad_f = dcell * (cell_before - gate_z) * forget * (1.0 - forget)
        grad_o = cot * cell * output_gate * (1.0 - output_gate)
        dpre_low = jnp.stack([grad_z, grad_f, grad_o], 0).astype(jnp.bfloat16)
        bias_total = bias_total + jnp.sum(dpre_low.astype(jnp.float32), axis=2)
        weight_term = jnp.einsum(
            "gcl,rl->gcr", dpre_low, joined_inputs, preferred_element_type=jnp.float32
        )
        djoined = jnp.einsum(
            "gcl,gcr->rl",
            dpre_low,
            lax.all_gather(weights, "dp", axis=2, tiled=True),
            preferred_element_type=jnp.float32,
        )
        later = djoined[width:] * carry_on[None, :]
        later = jnp.concatenate([later[:, 1:], jnp.zeros((width, 1), jnp.float32)], 1)
        term = djoined[:width] + later
        input_parts.append(
            lax.psum_scatter(term, "chan", scatter_dimension=0, tiled=True).astype(jnp.bfloat16)
        )
        grad_shard = grad_shard + lax.psum_scatter(
            weight_term, "dp", scatter_dimension=2, tiled=True
        )
    bias_grad = lax.psum(bias_total, "dp")
    hidden = jnp.concatenate(hidden_parts, 1)
    input_grad = jnp.concatenate(input_parts, 1)
    return (hidden, input_grad, grad_shard, bias_grad)


def solution(mesh):
    in_specs = (P("chan", "dp"), P(None, "chan", "dp"), P(None, "chan"), P("dp"), P("chan", "dp"))
    out_specs = (P("chan", "dp"), P("chan", "dp"), P(None, "chan", "dp"), P(None, "chan"))
    return jax.shard_map(local, mesh=mesh, in_specs=in_specs, out_specs=out_specs, check_vma=False)
```

profile of v0, /device:TPU:0, one launch (start us, length us, event | category | flops | bytes accessed | tf_op | source)
XLA Modules:
  0.0 4457.5 jit_solution(5522663903721280229)
XLA Ops:
  17.6 50.5 %all-gather.8.cloned.1.call-done = bf16[3,160,1280]{1,0,2:T(4,128)(2,1)} async-done(((bf16[3,160,160]{1,0,2:T(4,128)(2,1)}), bf16[3,160,1280]{1,0,2:T(4,128)(2,1)}) %all-gather.8.cloned.1.call-update) | async-done | bytes 1228816 | tf_op jit(solution)/shard_map/all_gather | solution.py:38
  97.7 24.5 all-gather.6.cloned.1.call-done
  499.0 23.6 slice.2303
  932.6 26.7 pad.595
  961.3 24.7 pad.594
  1049.3 26.7 pad.573
  1078.0 24.6 pad.572
  1899.6 23.6 slice.2576
  2702.4 26.4 pad.639
  2730.8 24.9 pad.638
  2819.7 26.5 pad.617
  2848.2 24.6 pad.616
  3205.2 23.7 slice.2935
  3634.2 24.2 pad.683
  3759.8 26.5 pad.661
  3803.1 24.9 pad.660
  3894.3 26.5 pad.705
  3937.6 24.7 pad.704
  4028.7 26.5 pad.727
  4072.0 24.8 pad.726
  4243.3 33.6 reduce-scatter.16.cloned.1.call-done
  4278.3 52.6 %reduce-scatter.18.cloned.1.call-done = f32[160,2048]{1,0:T(8,128)} async-done(((f32[640,2048]{1,0:T(8,128)}), f32[160,2048]{1,0:T(8,128)}) %reduce-scatter.18.cloned.1.call-update) | async-done | bytes 1310736
  4332.5 52.4 %reduce-scatter.20.cloned.1.call-done = f32[160,2048]{1,0:T(8,128)} async-done(((f32[640,2048]{1,0:T(8,128)}), f32[160,2048]{1,0:T(8,128)}) %reduce-scatter.20.cloned.1.call-update) | async-done | bytes 1310736
  4386.4 52.4 %reduce-scatter.22.cloned.1.call-done = f32[160,2048]{1,0:T(8,128)} async-done(((f32[640,2048]{1,0:T(8,128)}), f32[160,2048]{1,0:T(8,128)}) %reduce-scatter.22.cloned.1.call-update) | async-done | bytes 1310736
  (1681 shorter events, 3716.6 us)
Async XLA Ops:
  7.2 61.0 %all-gather.8.cloned.1.call-start = ((), (), s32[]{:S(2)}) async-start(), calls=%async_computation.6 | async-start | bytes 2949120 | tf_op jit(solution)/shard_map/all_gather | solution.py:38
  9.1 85.3 %all-gather.10.cloned.1.call-start = ((), (), s32[]{:S(2)}) async-start(), calls=%async_computation.7 | async-start | bytes 3276800 | tf_op jit(solution)/shard_map/all_gather | solution.py:31
  12.5 109.7 %all-gather.6.cloned.1.call-start = ((), (), s32[]{:S(2)}) async-start(), calls=%async_computation.5 | async-start | bytes 3276800 | tf_op jit(solution)/shard_map/all_gather | solution.py:31
  13.2 1866.7 %all-gather.14.cloned.1.call-start = ((), (), s32[]{:S(2)}) async-start(), calls=%async_computation.9 | async-start | bytes 3276800 | tf_op jit(solution)/shard_map/all_gather | solution.py:31
  13.8 1873.9 %all-gather.12.cloned.1.call-start = ((), (), s32[]{:S(2)}) async-start(), calls=%async_computation.8 | async-start | bytes 3276800 | tf_op jit(solution)/shard_map/all_gather | solution.py:31
  14.4 4226.5 %reduce-scatter.24.cloned.1.call-start = ((), (), s32[]{:S(2)}) async-start(), calls=%async_computation.14 | async-start | bytes 2949120
  17.6 113.8 %copy-start.285 = (f32[2048]{0:T(1024)}, f32[2048]{0:T(1024)S(1)}, u32[]{:S(2)}) copy-start(f32[2048]{0:T(1024)S(1)} %get-tuple-element.242) | copy-start | bytes 24580
  17.6 113.8 %copy-start.287 = (f32[2048]{0:T(1024)}, f32[2048]{0:T(1024)S(1)}, u32[]{:S(2)}) copy-start(f32[2048]{0:T(1024)S(1)} %get-tuple-element.16) | copy-start | bytes 24580
  811.1 61.6 %copy-start.180 = (f32[160,1]{1,0:T(8,128)S(1)}, f32[160,1]{1,0:T(8,128)}, u32[]{:S(2)}) copy-start(f32[160,1]{1,0:T(8,128)} %get-tuple-element.190) | copy-start | bytes 1924
  825.2 49.8 %copy-start.120 = (f32[160,8]{1,0:T(8,128)S(1)}, f32[160,8]{1,0:T(8,128)}, u32[]{:S(2)}) copy-start(f32[160,8]{1,0:T(8,128)} %get-tuple-element.197) | copy-start | bytes 15364
  1156.5 60.0 %copy-start.17 = (f32[160,2048]{1,0:T(8,128)}, f32[160,2048]{1,0:T(8,128)S(1)}, u32[]{:S(2)}) copy-start(f32[160,2048]{1,0:T(8,128)S(1)} %concatenate.384) | copy-start | bytes 3932164
  1284.9 50.9 %copy-start.129 = (f32[160,512]{1,0:T(8,128)}, f32[160,512]{1,0:T(8,128)S(1)}, u32[]{:S(2)}) copy-start(f32[160,512]{1,0:T(8,128)S(1)} %get-tuple-element.80) | copy-start | bytes 983044
  1414.0 61.4 %copy-start.14 = (f32[160,2048]{1,0:T(8,128)S(1)}, f32[160,2048]{1,0:T(8,128)}, u32[]{:S(2)}) copy-start(f32[160,2048]{1,0:T(8,128)} %get-tuple-element.24) | copy-start | bytes 3932164
  2580.2 61.4 %copy-start.182 = (f32[160,1]{1,0:T(8,128)S(1)}, f32[160,1]{1,0:T(8,128)}, u32[]{:S(2)}) copy-start(f32[160,1]{1,0:T(8,128)} %get-tuple-element.222) | copy-start | bytes 1924
  2926.7 60.2 %copy-start.15 = (f32[160,2048]{1,0:T(8,128)}, f32[160,2048]{1,0:T(8,128)S(1)}, u32[]{:S(2)}) copy-start(f32[160,2048]{1,0:T(8,128)S(1)} %concatenate.397) | copy-start | bytes 3932164
  3055.1 49.6 %copy-start.128 = (f32[160,512]{1,0:T(8,128)}, f32[160,512]{1,0:T(8,128)S(1)}, u32[]{:S(2)}) copy-start(f32[160,512]{1,0:T(8,128)S(1)} %get-tuple-element.82) | copy-start | bytes 983044
  3192.3 61.6 %copy-start.6 = (f32[160,2048]{1,0:T(8,128)S(1)}, f32[160,2048]{1,0:T(8,128)}, u32[]{:S(2)}) copy-start(f32[160,2048]{1,0:T(8,128)} %pad.617) | copy-start | bytes 3932164
  3302.7 56.3 %copy-start.16 = (f32[160,2048]{1,0:T(8,128)}, f32[160,2048]{1,0:T(8,128)S(1)}, u32[]{:S(2)}) copy-start(f32[160,2048]{1,0:T(8,128)S(1)} %concatenate.410) | copy-start | bytes 3932164
  3523.2 61.6 %copy-start.1 = (f32[160,2048]{1,0:T(8,128)S(1)}, f32[160,2048]{1,0:T(8,128)}, u32[]{:S(2)}) copy-start(f32[160,2048]{1,0:T(8,128)} %pad.639) | copy-start | bytes 3932164
  3523.2 61.6 %copy-start.3 = (f32[160,2048]{1,0:T(8,128)S(1)}, f32[160,2048]{1,0:T(8,128)}, u32[]{:S(2)}) copy-start(f32[160,2048]{1,0:T(8,128)} %pad.638) | copy-start | bytes 3932164
  4153.4 123.4 %reduce-scatter.16.cloned.1.call-start = ((), (), s32[]{:S(2)}) async-start(), calls=%async_computation.10 | async-start | bytes 6553600
  4167.7 163.2 %reduce-scatter.18.cloned.1.call-start = ((), (), s32[]{:S(2)}) async-start(), calls=%async_computation.11 | async-start | bytes 6553600
  4183.0 201.9 %reduce-scatter.20.cloned.1.call-start = ((), (), s32[]{:S(2)}) async-start(), calls=%async_computation.12 | async-start | bytes 6553600
  4197.8 241.1 %reduce-scatter.22.cloned.1.call-start = ((), (), s32[]{:S(2)}) async-start(), calls=%async_computation.13 | async-start | bytes 6553600
  (276 other events, 3249.4 us)
Sparse Core Ops, SparseCore 0:
  10.8 57.3 all-gather.7
  70.3 24.1 all-gather.9
  96.6 25.5 all-gather.5
  123.6 25.5 all-gather.13
  150.6 25.5 all-gather.11
  4153.5 70.4 reduce-scatter.23
  4226.5 50.2 reduce-scatter.15
  4279.5 51.3 reduce-scatter.17
  4333.5 51.3 reduce-scatter.19
  4387.4 51.3 reduce-scatter.21
where the time goes:
time: 4490 us; the launch traced here: 4460 us
  local copies, waits for them, and re-layouts  3790 us (84%)
  other arithmetic  295 us (7%)
  waiting for transfers between devices  289 us (6%)
    slice x264, local copies, waits for them, and re-layouts, local(): lax.associative_scan(combine, (decay_next, cot * output_gate), reverse=Tr...  1410 us
    slice x248, local copies, waits for them, and re-layouts, local(): cell = lax.associative_scan(combine, (decay, source), axis=1)[1]  1400 us
    pad x80, local copies, waits for them, and re-layouts, local(): cell = lax.associative_scan(combine, (decay, source), axis=1)[1]  402 us
    pad x80, local copies, waits for them, and re-layouts, local(): lax.associative_scan(combine, (decay_next, cot * output_gate), reverse=Tr...  377 us
    unnamed x15, waiting for transfers between devices  193 us
    unnamed x602, local copies, waits for them, and re-layouts  129 us
    mul x72, other arithmetic, combine(): return (earlier[0] * later[0], later[0] * earlier[1] + later[1])  112 us
  transfers between devices with their start and end apart: 10, of which 7 were waited for; matrix products, arithmetic and copies ran while one was open for 41% of the time, Pallas kernels for 0%

commit v1 on v0

--- a/solution.py
+++ b/solution.py
@@ -1,17 +1,583 @@
+import functools
+
 import jax
 import jax.numpy as jnp
 from jax import lax
+from jax.experimental import pallas as pl
+from jax.experimental.pallas import tpu as pltpu
 from jax.sharding import PartitionSpec as P
 
 LEN = 1024
 MICRO = 4
+LANES = 128
+SEGS = 8
+PAD = 8
+TILE = 256
+UNROLL = 16
+f32 = jnp.float32
+bf16 = jnp.bfloat16
+ANY = pl.BlockSpec(memory_space=pl.ANY)
+VMEM = pl.BlockSpec(memory_space=pltpu.VMEM)
+SMEM = pl.BlockSpec(memory_space=pltpu.SMEM)
+
+
+def dot(a, b, ca, cb):
+    return lax.dot_general(a, b, (((ca,), (cb,)), ((), ())), preferred_element_type=f32)
+
+
+def sigmoid(v):
+    return 0.5 * jnp.tanh(0.5 * v) + 0.5
+
+
+def layer_kernel(k, first, last, parts, C, n, *refs):
+    refs = list(refs)
+    me_ref, tok, sib, px, pd, cot, scot, carry_l, carry_t, bias = refs[:10]
+    refs = refs[10:]
+    if first:
+        w_in, refs = refs[: 2 * parts], refs[2 * parts :]
+    else:
+        w_in, acc_in, refs = refs[0], refs[1], refs[3:]
+    hid, hid_sib, dx_own, dx_sib, dx_px, dx_pd, bsum = refs[:7]
+    refs = refs[7:]
+    if last:
+        acc_own, acc_sib, refs = refs[0], refs[1], refs[2:]
+    else:
+        acc_out, refs = refs[0], refs[1:]
+    if first:
+        w_out, refs = refs[0], refs[1:]
+    (xb, wb, cb, pre, zs, fs, os_, cbs, ct, hs, hb, dp, dxb, accb, ab, small, nxt, cl, ca_t, sem) = refs
+    D = 4 * C
+    tl = C - LANES
+    steps = n // SEGS
+    sp = steps + PAD
+    me, row, place = me_ref[0], me_ref[1], me_ref[2]
+    col = pl.multiple_of(row * n, n)
+    half = 4 * LANES
+
+    def go(src, dst, i):
+        copy = pltpu.make_async_copy(src, dst, sem.at[i])
+        copy.start()
+        return copy
+
+    def block(j):
+        return pl.ds(pl.multiple_of((me ^ j) * C, 32), C)
+
+    def nat(o, h):
+        return pl.ds(pl.multiple_of((o // steps + h) * sp, 8), steps)
+
+    here = pl.ds(col, n)
+    x_copies = [
+        go(px, xb.at[block(2), :], 2),
+        go(pd, xb.at[block(3), :], 3),
+        go(tok.at[:, here], xb.at[block(0), :], 0),
+        go(sib.at[:, here], xb.at[block(1), :], 1),
+        go(carry_l.at[k], cl, 10),
+    ]
+    if first:
+        w_copies = []
+        for j in range(parts):
+            at = pl.ds(pl.multiple_of((place ^ j) * C, 32), C)
+            w_copies.append(go(w_in[j], wb.at[at, 0:half], 12 + j))
+            w_copies.append(go(w_in[parts + j], wb.at[at, half : 2 * half], 12 + parts + j))
+    else:
+        w_copies = [go(w_in, wb, 4)]
+    c_copies = [
+        go(cot.at[0:LANES, here], cb.at[0:LANES], 5),
+        go(scot.at[0:LANES, here], cb.at[LANES : 2 * LANES], 6),
+        go(cot.at[LANES:C, here], cb.at[2 * LANES : 2 * LANES + tl], 7),
+        go(scot.at[LANES:C, here], cb.at[2 * LANES + tl : 2 * LANES + 2 * tl], 8),
+        go(carry_t.at[k], ca_t, 11),
+    ]
+    for copy in x_copies:
+        copy.wait()
+    mask = cl[0:1, :]
+    rb = 32
+
+    def prev_step(i, _):
+        o = pl.multiple_of(i * rb, rb)
+        v = xb[pl.ds(o, rb), :].astype(f32)
+        xb[pl.ds(D + o, rb), :] = (pltpu.roll(v, 1, 1) * mask).astype(bf16)
+        return 0
+
+    lax.fori_loop(0, D // rb, prev_step, 0, unroll=2)
+    for copy in w_copies:
+        copy.wait()
+    if first:
+        w_save = go(wb, w_out, 4)
+    else:
+        acc_copy = go(acc_in, accb, 9)
+
+    def forward_step(i, _):
+        o = pl.multiple_of(i * TILE, TILE)
+        v = dot(xb[:, pl.ds(o, TILE)], wb[...], 0, 0)
+        for q in range(8):
+            for h in range(TILE // steps):
+                pre[q, nat(o, h), :] = v[h * steps : (h + 1) * steps, q * LANES : (q + 1) * LANES]
+        return 0
+
+    lax.fori_loop(0, n // TILE, forward_step, 0)
+    for copy in c_copies:
+        copy.wait()
+
+    def cot_step(i, _):
+        o = pl.multiple_of(i * TILE, TILE)
+        v = cb[:, pl.ds(o, TILE)].astype(f32).T
+        for q in range(3):
+            for h in range(TILE // steps):
+                ct[q, nat(o, h), :] = v[h * steps : (h + 1) * steps, q * LANES : (q + 1) * LANES]
+        return 0
+
+    lax.fori_loop(0, n // TILE, cot_step, 0)
+    lane = lax.broadcasted_iota(jnp.int32, (SEGS, LANES), 1)
+    b_all = bias[...]
+    b = [jnp.broadcast_to(b_all[:, q * LANES : (q + 1) * LANES], (SEGS, LANES)) for q in range(8)]
+    cols = [slice(q * LANES, (q + 1) * LANES) for q in range(3)]
+    one = jnp.ones((SEGS, LANES), f32)
+    zero = jnp.zeros((SEGS, LANES), f32)
+
+    def strided(ref, t, q):
+        return ref[q, pl.ds(t, SEGS, stride=sp), :]
+
+    def now(t):
+        return pl.ds(pl.multiple_of(t * SEGS, SEGS), SEGS)
+
+    def gates_step(t, state):
+        gain, total = state
+        v = [strided(pre, t, q) + b[q] for q in range(8)]
+        u, w = v[3], v[7]
+        tz = jnp.where(lane < tl, u, pltpu.roll(w, tl, 1))
+        tf = jnp.where(lane < tl, pltpu.roll(u, LANES - tl, 1), w)
+        to = jnp.where(lane < tl, pltpu.roll(u, LANES - 2 * tl, 1), pltpu.roll(w, LANES - tl, 1))
+        z = [jnp.tanh(g) for g in (v[0], v[4], tz)]
+        f = [sigmoid(g) for g in (v[1], v[5], tf)]
+        o = [sigmoid(g) for g in (v[2], v[6], to)]
+        r = now(t)
+        ca = ca_t[r, :]
+        gains, totals = [], []
+        for q in range(3):
+            zs[r, cols[q]] = z[q]
+            fs[r, cols[q]] = f[q]
+            os_[r, cols[q]] = o[q]
+            gains.append(gain[q] * (f[q] * ca))
+            totals.append(z[q] + f[q] * (ca * total[q] - z[q]))
+        return tuple(gains), tuple(totals)
+
+    gain, total = lax.fori_loop(0, steps, gates_step, ((one,) * 3, (zero,) * 3), unroll=UNROLL)
+    for q in range(3):
+        small[0, :, cols[q]] = gain[q]
+        small[1, :, cols[q]] = total[q]
+    run = jnp.zeros((1, 3 * LANES), f32)
+    for s in range(SEGS):
+        small[2, s : s + 1, :] = run
+        run = small[0, s : s + 1, :] * run + small[1, s : s + 1, :]
+    cell = tuple(small[2, :, cols[q]] for q in range(3))
+
+    def cell_step(t, state):
+        cell, back, gain = state
+        r = now(t)
+        ca = ca_t[r, :]
+        cells, backs, gains = [], [], []
+        for q in range(3):
+            z, f, o = zs[r, cols[q]], fs[r, cols[q]], os_[r, cols[q]]
+            prev = ca * cell[q]
+            cbs[r, cols[q]] = prev
+            new = z + f * (prev - z)
+            hs[q, pl.ds(t, SEGS, stride=sp), :] = o * new
+            g = jnp.where(t == 0, one, gain[q] * (f * ca))
+            cells.append(new)
+            gains.append(g)
+            backs.append(back[q] + g * (strided(ct, t, q) * o))
+        return tuple(cells), tuple(backs), tuple(gains)
+
+    cell, back, gain = lax.fori_loop(0, steps, cell_step, (cell, (zero,) * 3, (one,) * 3), unroll=UNROLL)
+    for q in range(3):
+        small[0, :, cols[q]] = back[q]
+        small[1, :, cols[q]] = gain[q]
+        small[3, :, cols[q]] = fs[0:SEGS, cols[q]] * ca_t[0:SEGS, :]
+    run = jnp.zeros((1, 3 * LANES), f32)
+    for s in range(SEGS - 1, -1, -1):
+        small[2, s : s + 1, :] = run
+        run = small[3, s : s + 1, :] * (small[0, s : s + 1, :] + small[1, s : s + 1, :] * run)
+    later = tuple(small[2, :, cols[q]] for q in range(3))
+
+    def hidden_step(i, _):
+        o = pl.multiple_of(i * TILE, TILE)
+        for q in range(3):
+            e = LANES if q < 2 else 2 * tl
+            for h in range(TILE // steps):
+                v = hs[q, nat(o, h), :].T.astype(bf16)
+                hb[q * LANES : q * LANES + e, pl.ds(pl.multiple_of(o + h * steps, LANES), steps)] = v[0:e]
+        return 0
+
+    lax.fori_loop(0, n // TILE, hidden_step, 0)
+    out_copies = [
+        go(hb.at[0:LANES], hid.at[0:LANES, here], 5),
+        go(hb.at[LANES : 2 * LANES], hid_sib.at[0:LANES], 6),
+        go(hb.at[2 * LANES : 2 * LANES + tl], hid.at[LANES:C, here], 7),
+        go(hb.at[2 * LANES + tl : 2 * LANES + 2 * tl], hid_sib.at[LANES:C], 8),
+    ]
+
+    def grad_step(i, later):
+        t = steps - 1 - i
+        r = now(t)
+        ca = ca_t[r, :]
+        gz, gf, go_, laters = [], [], [], []
+        for q in range(3):
+            z, f, o, prev = zs[r, cols[q]], fs[r, cols[q]], os_[r, cols[q]], cbs[r, cols[q]]
+            c = strided(ct, t, q)
+            dc = c * o + later[q]
+            laters.append((f * ca) * dc)
+            d = prev - z
+            u = dc * (1.0 - f)
+            gz.append(u * (1.0 - z * z))
+            gf.append(u * (f * d))
+            go_.append(c * (z + f * d) * (o * (1.0 - o)))
+        z, f, o = gz[2], gf[2], go_[2]
+        u = jnp.where(
+            lane < tl,
+            z,
+            jnp.where(
+                lane < 2 * tl,
+                pltpu.roll(f, tl, 1),
+                jnp.where(lane < 3 * tl, pltpu.roll(o, 2 * tl, 1), 0.0),
+            ),
+        )
+        w = jnp.where(
+            lane < tl,
+            pltpu.roll(z, LANES - tl, 1),
+            jnp.where(lane < 2 * tl, f, jnp.where(lane < 3 * tl, pltpu.roll(o, tl, 1), 0.0)),
+        )
+        for q, v in enumerate((gz[0], gf[0], go_[0], u, gz[1], gf[1], go_[1], w)):
+            pre[q, pl.ds(t, SEGS, stride=sp), :] = v
+        return tuple(laters)
+
+    lax.fori_loop(0, steps, grad_step, later, unroll=UNROLL)
+    ck = 64
+
+    def cast_step(i, sums):
+        o = pl.multiple_of(i * ck, ck)
+        at = pl.ds(pl.multiple_of(o // steps * sp + o % steps, 8), ck)
+        out = []
+        for q in range(8):
+            v = pre[q, at, :].astype(bf16)
+            dp[pl.ds(o, ck), q * LANES : (q + 1) * LANES] = v
+            w = v.astype(f32)
+            a = sums[q]
+            for h in range(ck // SEGS):
+                a = a + w[h * SEGS : (h + 1) * SEGS]
+            out.append(a)
+        return tuple(out)
+
+    sums = lax.fori_loop(0, n // ck, cast_step, (zero,) * 8)
+    for q in range(8):
+        bsum[:, q * LANES : (q + 1) * LANES] = sums[q]
+    if not first:
+        acc_copy.wait()
+
+    def weight_step(j, _):
+        o = pl.multiple_of(j * TILE, TILE)
+        v = dot(xb[...], dp[:, pl.ds(o, TILE)], 1, 0)
+        if not first:
+            v = v + accb[:, pl.ds(o, TILE)]
+        accb[:, pl.ds(o, TILE)] = v
+        return 0
+
+    def weight_sib_step(j, _):
+        o = pl.multiple_of(j * TILE, TILE)
+        v = dot(xb[...], dp[:, pl.ds(half + o, TILE)], 1, 0)
+        if not first:
+            v = v + accb[:, pl.ds(half + o, TILE)]
+        ab[:, pl.ds(o, TILE)] = v.astype(bf16)
+        return 0
+
+    if last:
+        lax.fori_loop(0, half // TILE, weight_sib_step, 0)
+        out_copies.append(go(ab, acc_sib, 10))
+        lax.fori_loop(0, half // TILE, weight_step, 0)
+        out_copies.append(go(accb.at[:, 0:half], acc_own, 9))
+    else:
+        lax.fori_loop(0, 2 * half // TILE, weight_step, 0)
+        out_copies.append(go(accb, acc_out, 9))
+    nxt[...] = jnp.zeros_like(nxt)
+    lane2 = lax.broadcasted_iota(jnp.int32, (D, LANES), 1)
+
+    def input_step(i, _):
+        o = pl.multiple_of((n // TILE - 1 - i) * TILE, TILE)
+        dj = dot(wb[...], dp[pl.ds(o, TILE), :], 1, 1)
+        rolled = [
+            pltpu.roll(
+                dj[D:, h * LANES : (h + 1) * LANES] * cl[0:1, pl.ds(o + h * LANES, LANES)], LANES - 1, 1
+            )
+            for h in range(2)
+        ]
+        after = nxt[...]
+        nxt[...] = rolled[0]
+        edge = lane2 == LANES - 1
+        dxb[:, pl.ds(o, LANES)] = (dj[:D, 0:LANES] + jnp.where(edge, rolled[1], rolled[0])).astype(bf16)
+        dxb[:, pl.ds(o + LANES, LANES)] = (
+            dj[:D, LANES : 2 * LANES] + jnp.where(edge, after, rolled[1])
+        ).astype(bf16)
+        return 0
+
+    lax.fori_loop(0, n // TILE, input_step, 0)
+    for j, out in enumerate((dx_own, dx_sib, dx_px, dx_pd)):
+        out_copies.append(go(dxb.at[block(j), :], out, j))
+    if first:
+        out_copies.append(w_save)
+    for copy in out_copies:
+        copy.wait()
+
+
+def layer(k, first, last, parts, C, n, total, scal, tok, sib, px, pd, cot, scot, carry_l, carry_t, bias, w, acc, hid):
+    D = 4 * C
+    N = 8 * LANES
+    shape = jax.ShapeDtypeStruct
+    ins = [scal, tok, sib, px, pd, cot, scot, carry_l, carry_t, bias]
+    specs = [SMEM] + [ANY] * 8 + [VMEM]
+    alias = {}
+    piece = shape((C, n), bf16)
+    outs = [shape((C, total), bf16)] + [piece] * 5 + [shape((SEGS, N), f32)]
+    out_specs = [ANY] * 6 + [VMEM]
+    if first:
+        ins += list(w)
+        specs += [ANY] * len(w)
+    else:
+        ins += [w, acc, hid]
+        specs += [ANY] * 3
+        alias = {12: 0}
+        if not last:
+            alias[11] = 7
+    if last:
+        outs += [shape((2 * D, N // 2), f32), shape((2 * D, N // 2), bf16)]
+        out_specs += [ANY] * 2
+    else:
+        outs += [shape((2 * D, N), f32)]
+        out_specs += [ANY]
+    if first:
+        outs += [shape((2 * D, N), bf16)]
+        out_specs += [ANY]
+    w3 = 3 * LANES
+    tall = n + SEGS * PAD
+    scratch = (
+        [
+            pltpu.VMEM((2 * D, n), bf16),
+            pltpu.VMEM((2 * D, N), bf16),
+            pltpu.VMEM((w3, n), bf16),
+            pltpu.VMEM((8, tall, LANES), f32),
+        ]
+        + [pltpu.VMEM((n, w3), f32)] * 4
+        + [pltpu.VMEM((3, tall, LANES), f32)] * 2
+        + [
+            pltpu.VMEM((2 * C, n), bf16),
+            pltpu.VMEM((n, N), bf16),
+            pltpu.VMEM((D, n), bf16),
+            pltpu.VMEM((2 * D, N), f32),
+            pltpu.VMEM((2 * D, N // 2), bf16),
+            pltpu.VMEM((4, SEGS, w3), f32),
+            pltpu.VMEM((D, LANES), f32),
+            pltpu.VMEM((SEGS, n), f32),
+            pltpu.VMEM((n, LANES), f32),
+            pltpu.SemaphoreType.DMA((12 + 2 * parts,)),
+        ]
+    )
+    return pl.pallas_call(
+        functools.partial(layer_kernel, k, first, last, parts, C, n),
+        out_shape=outs,
+        in_specs=specs,
+        out_specs=out_specs,
+        scratch_shapes=scratch,
+        input_output_aliases=alias,
+        compiler_params=pltpu.CompilerParams(vmem_limit_bytes=58 << 20),
+        cost_estimate=pl.CostEstimate(
+            flops=12 * D * N * n, bytes_accessed=24 << 20, transcendentals=9 * n * LANES
+        ),
+        name="layer",
+    )(*ins)
+
+
+def finish_kernel(n, me_ref, own, px, sib, pd, *refs):
+    out, a, b, sem = refs[-4:]
+    here = pl.ds(pl.multiple_of(me_ref[1] * n, n), n)
+    there = pl.ds(pl.multiple_of(me_ref[3] * n, n), n)
+    a[...] = (own[...].astype(f32) + px[...].astype(f32)).astype(bf16)
+    first = pltpu.make_async_copy(a, out.at[:, here], sem.at[0])
+    first.start()
+    b[...] = (sib[...].astype(f32) + pd[...].astype(f32)).astype(bf16)
+    second = pltpu.make_async_copy(b, out.at[:, there], sem.at[1])
+    second.start()
+    first.wait()
+    second.wait()
+
+
+def finish(C, n, total, scal, own, px, sib, pd, grad):
+    ins = [scal, own, px, sib, pd]
+    specs = [SMEM] + [VMEM] * 4
+    alias = {}
+    if grad is not None:
+        ins.append(grad)
+        specs.append(ANY)
+        alias = {5: 0}
+    return pl.pallas_call(
+        functools.partial(finish_kernel, n),
+        out_shape=jax.ShapeDtypeStruct((C, total), bf16),
+        in_specs=specs,
+        out_specs=ANY,
+        scratch_shapes=[pltpu.VMEM((C, n), bf16)] * 2 + [pltpu.SemaphoreType.DMA((2,))],
+        input_output_aliases=alias,
+        cost_estimate=pl.CostEstimate(flops=4 * C * n, bytes_accessed=12 * C * n, transcendentals=0),
+        name="finish",
+    )(*ins)
+
+
+def place_kernel(n, rows_ref, *refs):
+    out, sem = refs[-2:]
+    pieces = refs[:-3]
+    copies = []
+    for k, piece in enumerate(pieces):
+        there = pl.ds(pl.multiple_of(rows_ref[k] * n, n), n)
+        copies.append(pltpu.make_async_copy(piece, out.at[:, there], sem.at[k]))
+        copies[-1].start()
+    for copy in copies:
+        copy.wait()
+
+
+def place(n, rows, pieces, hid):
+    return pl.pallas_call(
+        functools.partial(place_kernel, n),
+        out_shape=jax.ShapeDtypeStruct(hid.shape, hid.dtype),
+        in_specs=[SMEM] + [ANY] * (len(pieces) + 1),
+        out_specs=ANY,
+        scratch_shapes=[pltpu.SemaphoreType.DMA((len(pieces),))],
+        input_output_aliases={1 + len(pieces): 0},
+        cost_estimate=pl.CostEstimate(flops=0, bytes_accessed=4 * hid.size, transcendentals=0),
+        name="place",
+    )(rows, *pieces, hid)
+
+
+def pack(w):
+    tail = w.shape[1] - LANES
+    rest = w.shape[2:]
+    return jnp.concatenate(
+        [
+            w[:, :LANES].reshape((3 * LANES,) + rest),
+            w[:, LANES:].reshape((3 * tail,) + rest),
+            jnp.zeros((LANES - 3 * tail,) + rest, w.dtype),
+        ],
+        0,
+    )
+
+
+def unpack(w, C):
+    tail = C - LANES
+    rest = w.shape[1:]
+    return jnp.concatenate(
+        [
+            w[: 3 * LANES].reshape((3, LANES) + rest),
+            w[3 * LANES : 3 * LANES + 3 * tail].reshape((3, tail) + rest),
+        ],
+        1,
+    )
+
+
+def local(chan, parts, tokens, weights, bias, segment_ids, cotangent):
+    C, total = tokens.shape
+    n = LEN
+    rows = total // n
+    micros = rows // 2
+    me = lax.axis_index("chan")
+    place_dp = lax.axis_index("dp")
+    core = me & 1
+
+    def chan_move(v, j):
+        return lax.ppermute(v, "chan", [(i, i ^ j) for i in range(chan)])
+
+    def dp_move(v, j):
+        return lax.ppermute(v, "dp", [(i, i ^ j) for i in range(parts)])
+
+    px, pd = [], []
+    for k in range(micros):
+        mine = lax.dynamic_slice(tokens, (0, (2 * k + core) * n), (C, n))
+        other = lax.dynamic_slice(tokens, (0, (2 * k + 1 - core) * n), (C, n))
+        px.append(chan_move(mine, 2))
+        pd.append(chan_move(other, 3))
+    shard = pack(weights).T
+    g = {0: shard}
+    g[4] = dp_move(shard, 4)
+    g[1] = dp_move(shard, 1)
+    g[2] = dp_move(shard, 2)
+    g[5] = dp_move(g[4], 1)
+    g[6] = dp_move(g[4], 2)
+    g[3] = dp_move(g[1], 2)
+    g[7] = dp_move(g[6], 1)
+    w = [g[j] for j in range(parts)] + [chan_move(g[j], 1) for j in range(parts)]
+    b_own = pack(bias)[None, :]
+    b_all = jnp.concatenate([b_own, chan_move(b_own, 1)], 1)
+    sib = chan_move(tokens, 1)
+    scot = chan_move(cotangent, 1)
+
+    ids = segment_ids.reshape(rows, n)
+    same = jnp.concatenate([jnp.zeros((rows, 1), jnp.bool_), ids[:, 1:] == ids[:, :-1]], 1)
+    carry = jnp.where(same, 1.0, 0.0).astype(f32).reshape(micros, 2, n)
+    carry = jnp.where(core == 0, carry[:, 0], carry[:, 1])
+    carry_l = jnp.broadcast_to(carry[:, None, :], (micros, SEGS, n))
+    carry_t = carry.reshape(micros, SEGS, n // SEGS).swapaxes(1, 2).reshape(micros, n, 1)
+    carry_t = jnp.broadcast_to(carry_t, (micros, n, LANES))
+
+    acc = hid = grad = None
+    bias_sum = 0.0
+    hid_parts, pending = [], []
+    for k in range(micros):
+        scal = jnp.stack([me, 2 * k + core, place_dp, 2 * k + 1 - core]).astype(jnp.int32)
+        first, last = k == 0, k == micros - 1
+        out = layer(
+            k, first, last, parts, C, n, total, scal, tokens, sib, px[k], pd[k], cotangent, scot,
+            carry_l, carry_t, b_all, w, acc, hid,
+        )
+        hid, hid_sib, own, d_sib, d_px, d_pd, bsum, acc = out[:8]
+        if first:
+            w = out[8]
+        pending.append((scal, own, chan_move(d_px, 2), chan_move(d_sib, 1), chan_move(d_pd, 3)))
+        hid_parts.append(chan_move(hid_sib, 1))
+        bias_sum = bias_sum + bsum
+        if last:
+            acc_sib = out[8]
+    for scal, own, r_px, r_sib, r_pd in pending:
+        grad = finish(C, n, total, scal, own, r_px, r_sib, r_pd, grad)
+    others = jnp.stack([2 * k + 1 - core for k in range(micros)]).astype(jnp.int32)
+    hid = place(n, others, hid_parts, hid)
+
+    half = 4 * LANES
+    partial = (acc + chan_move(acc_sib, 1).astype(f32)).reshape(parts, C, half)
+
+    def rows_of(j):
+        return lax.dynamic_index_in_dim(partial, place_dp ^ j, 0, keepdims=False)
+
+    def send(v, j):
+        return dp_move(v.astype(bf16), j).astype(f32)
+
+    r7 = send(rows_of(7), 1)
+    r3 = send(rows_of(3), 2)
+    r5 = send(rows_of(5), 1)
+    r2 = send(rows_of(2), 2)
+    r6 = send(rows_of(6) + r7, 2)
+    r1 = send(rows_of(1) + r3, 1)
+    r4 = send(rows_of(4) + r5 + r6, 4)
+    shard_grad = rows_of(0) + r2 + r1 + r4
+    weight_grad = unpack(shard_grad.T, C)
+
+    bias_sum = jnp.sum(bias_sum, 0)
+    b = bias_sum[:half] + chan_move(bias_sum[half:], 1)
+    for j in (1, 2, 4):
+        b = b + dp_move(b, j)
+    bias_grad = unpack(b, C)
+    return (hid, grad, weight_grad, bias_grad)
 
 
 def combine(earlier, later):
     return (earlier[0] * later[0], later[0] * earlier[1] + later[1])
 
 
-def local(tokens, weights, bias, segment_ids, cotangent):
+def local_any(tokens, weights, bias, segment_ids, cotangent):
     width_part, total_rows = tokens.shape
     batch_rows = total_rows // MICRO
     grad_shard = jnp.zeros(weights.shape, jnp.float32)
@@ -48,9 +614,7 @@
         cell = lax.associative_scan(combine, (decay, source), axis=1)[1]
         hidden_parts.append((output_gate * cell).astype(jnp.bfloat16))
         decay_next = jnp.concatenate([decay[:, 1:], jnp.zeros((width_part, 1), jnp.float32)], 1)
-        dcell = lax.associative_scan(
-            combine, (decay_next, cot * output_gate), reverse=True, axis=1
-        )[1]
+        dcell = lax.associative_scan(combine, (decay_next, cot * output_gate), reverse=True, axis=1)[1]
         cell_before = (
             jnp.concatenate([jnp.zeros((width_part, 1), jnp.float32), cell[:, :-1]], 1)
             * carry_on[None, :]
@@ -75,9 +639,7 @@
         input_parts.append(
             lax.psum_scatter(term, "chan", scatter_dimension=0, tiled=True).astype(jnp.bfloat16)
         )
-        grad_shard = grad_shard + lax.psum_scatter(
-            weight_term, "dp", scatter_dimension=2, tiled=True
-        )
+        grad_shard = grad_shard + lax.psum_scatter(weight_term, "dp", scatter_dimension=2, tiled=True)
     bias_grad = lax.psum(bias_total, "dp")
     hidden = jnp.concatenate(hidden_parts, 1)
     input_grad = jnp.concatenate(input_parts, 1)
@@ -85,6 +647,19 @@
 
 
 def solution(mesh):
+    chan, parts = mesh.shape["chan"], mesh.shape["dp"]
     in_specs = (P("chan", "dp"), P(None, "chan", "dp"), P(None, "chan"), P("dp"), P("chan", "dp"))
     out_specs = (P("chan", "dp"), P("chan", "dp"), P(None, "chan", "dp"), P(None, "chan"))
-    return jax.shard_map(local, mesh=mesh, in_specs=in_specs, out_specs=out_specs, check_vma=False)
+
+    def run(tokens, weights, bias, segment_ids, cotangent):
+        C = tokens.shape[0] // chan
+        row_part = weights.shape[2] // parts
+        pairs = tokens.shape[1] // parts % (2 * LEN) == 0
+        tail = C - LANES
+        fits = chan == 4 and parts == 8 and row_part == C and pairs and 0 < 3 * tail < LANES and tail % 32 == 0
+        body = functools.partial(local, chan, parts) if fits else local_any
+        return jax.shard_map(body, mesh=mesh, in_specs=in_specs, out_specs=out_specs, check_vma=False)(
+            tokens, weights, bias, segment_ids, cotangent
+        )
+
+    return run

time: 4490 us -> 278 us (0.06)
  local copies, waits for them, and re-layouts: 3790 us -> 12.1 us
  other arithmetic: 295 us -> 13.3 us
  waiting for transfers between devices: 289 us -> 71.5 us
  Pallas kernels: 0 us -> 142 us
    slice x527 -> x11, local copies, waits for them, and re-layouts: 2810 us -> 2.8 us  [the longest x2 1.48 us: pack(): w[:, LANES:].reshape((3 * tail,) + rest)]
    pad x160 -> x0, local copies, waits for them, and re-layouts: 779 us -> none  [the longest x80 402 us: local(): cell = lax.associative_scan(combine, (decay, source), axis=1)[1]]
    unnamed x15 -> x0, waiting for transfers between devices: 193 us -> none
    pallas_call x0 -> x9, Pallas kernels: none -> 142 us  [the longest x4 91.9 us: layer(): pl.pallas_call(functools.partial(layer_kernel, k, first, last, parts, C,...]
    mul x80 -> x0, other arithmetic: 134 us -> none  [the longest x72 112 us: combine(): return (earlier[0] * later[0], later[0] * earlier[1] + later[1])]
    unnamed x602 -> x55, local copies, waits for them, and re-layouts: 129 us -> 2.45 us
    add x181 -> x5, other arithmetic: 107 us -> 2.52 us  [the longest x1 2.51 us: local(): partial = (acc + chan_move(acc_sib, 1).astype(f32)).reshape(parts, C, half)]
    all_gather x5 -> x0, waiting for transfers between devices: 96.5 us -> none  [the longest x1 50.5 us: local(): lax.all_gather(weights, 'dp', axis=2, tiled=True)]
  transfers between devices with their start and end apart: 10 -> 54, of which waited for: 7 -> 16; matrix products, arithmetic and copies ran while one was open for 41% -> 8% of each run, Pallas kernels for 0% -> 43%
where the time goes in v1:
time: 278 us; the launch traced here: 276 us
  Pallas kernels  142 us (51%)
  waiting for transfers between devices  71.5 us (26%)
  starting transfers between devices  35.3 us (13%)
  other arithmetic  13.3 us (5%)
  local copies, waits for them, and re-layouts  12.1 us (4%)
    pallas_call x4, Pallas kernels, layer(): pl.pallas_call(functools.partial(layer_kernel, k, first, last, parts, C,...  91.9 us
    ppermute x37, waiting for transfers between devices, chan_move(): return lax.ppermute(v, 'chan', [(i, i ^ j) for i in range(chan)])  44.5 us
    pallas_call x1, Pallas kernels, place(): pl.pallas_call(functools.partial(place_kernel, n), out_shape=jax.ShapeDty...  41.5 us
    ppermute x17, waiting for transfers between devices, dp_move(): return lax.ppermute(v, 'dp', [(i, i ^ j) for i in range(parts)])  27 us
    ppermute x37, starting transfers between devices, chan_move(): return lax.ppermute(v, 'chan', [(i, i ^ j) for i in range(chan)])  19.3 us
    ppermute x17, starting transfers between devices, dp_move(): return lax.ppermute(v, 'dp', [(i, i ^ j) for i in range(parts)])  16 us
    pallas_call x4, Pallas kernels, finish(): pl.pallas_call(functools.partial(finish_kernel, n), out_shape=jax.ShapeDt...  8.83 us
  transfers between devices with their start and end apart: 54, of which 16 were waited for; matrix products, arithmetic and copies ran while one was open for 8% of the time, Pallas kernels for 43%

profile of v1, /device:TPU:0, one launch (start us, length us, event | category | flops | bytes accessed | tf_op | source)
XLA Modules:
  0.0 275.7 jit_solution(13576471627565311627)
XLA Ops:
  3.4 3.0 %collective-permute-start.5 = (bf16[160,512]{1,0:T(8,128)(2,1)S(1)}, bf16[160,512]{1,0:T(8,128)(2,1)S(1)}, u32[]{:S(2)}, u32[]{:S(2)}) collective-permute-start(bf16[160,512]{1,0:T(8,128)(2,1)S(1)} %maximum_bitcast_fusion.refs_10_), channel_id=1, source_target_pairs={{0,4},{4,0},{8,12},{12,8},{16,20},{20,16},{24,28},{28,24},{1,5},{5... | collective-permute-start | bytes 491528 | tf_op jit(solution)/shard_map/ppermute | solution.py:495
  13.2 2.6 collective-permute-start.8
  15.9 8.0 %collective-permute-done.8.refs_14_ = bf16[160,512]{1,0:T(8,128)(2,1)} collective-permute-done((bf16[160,512]{1,0:T(8,128)(2,1)S(1)}, bf16[160,512]{1,0:T(8,128)(2,1)}, u32[]{:S(2)}, u32[]{:S(2)}) %collective-permute-start.8) | collective-permute-done | bytes 163872 | tf_op jit(solution)/shard_map/ppermute | solution.py:495
  25.3 8.4 %collective-permute-done.2.refs_4_ = bf16[160,1024]{1,0:T(8,128)(2,1)S(1)} collective-permute-done((bf16[160,1024]{1,0:T(8,128)(2,1)S(1)}, bf16[160,1024]{1,0:T(8,128)(2,1)S(1)}, u32[]{:S(2)}, u32[]{:S(2)}) %collective-permute-start.2) | collective-permute-done | bytes 327712 | tf_op jit(solution)/shard_map/ppermute | solution.py:492
  34.9 5.3 %collective-permute-done.10.refs_16_ = bf16[160,512]{1,0:T(8,128)(2,1)} collective-permute-done((bf16[160,512]{1,0:T(8,128)(2,1)}, bf16[160,512]{1,0:T(8,128)(2,1)}, u32[]{:S(2)}, u32[]{:S(2)}) %collective-permute-start.10) | collective-permute-done | bytes 163872 | tf_op jit(solution)/shard_map/ppermute | solution.py:495
  42.1 5.0 %collective-permute-done.11.refs_17_ = bf16[160,512]{1,0:T(8,128)(2,1)} collective-permute-done((bf16[160,512]{1,0:T(8,128)(2,1)}, bf16[160,512]{1,0:T(8,128)(2,1)}, u32[]{:S(2)}, u32[]{:S(2)}) %collective-permute-start.11) | collective-permute-done | bytes 163872 | tf_op jit(solution)/shard_map/ppermute | solution.py:495
  55.8 22.9 %layer.4 = (bf16[160,8192]{1,0:T(8,128)(2,1)}, bf16[160,1024]{1,0:T(8,128)(2,1)}, bf16[160,1024]{1,0:T(8,128)(2,1)}, bf16[160,1024]{1,0:T(8,128)(2,1)}, bf16[160...) custom-call(s32[4]{0:T(128)} %pad_add_fusion.refs_0_.me_ref, ...), custom_call_target="tpu_custom_call" | custom-call | flops 8053063680 | bytes 25165824 | tf_op jit(solution)/shard_map/layer/pallas_call | solution.py:383
  80.5 22.9 %layer.5 = (bf16[160,8192]{1,0:T(8,128)(2,1)}, bf16[160,1024]{1,0:T(8,128)(2,1)}, bf16[160,1024]{1,0:T(8,128)(2,1)}, bf16[160,1024]{1,0:T(8,128)(2,1)}, bf16[160...) custom-call(s32[4]{0:T(128)} %pad_add_fusion.1.refs_0_.me_ref, ...), custom_call_target="tpu_custom_call", output_to_operand_aliasing={{0}: (12, {}), {7}: (11, {})} | custom-call | flops 8053063680 | bytes 25165824 | tf_op jit(solution)/shard_map/layer/pallas_call | solution.py:383
  104.2 23.0 %layer.6 = (bf16[160,8192]{1,0:T(8,128)(2,1)}, bf16[160,1024]{1,0:T(8,128)(2,1)}, bf16[160,1024]{1,0:T(8,128)(2,1)}, bf16[160,1024]{1,0:T(8,128)(2,1)}, bf16[160...) custom-call(s32[4]{0:T(128)} %pad_add_fusion.2.refs_0_.me_ref, ...), custom_call_target="tpu_custom_call", output_to_operand_aliasing={{0}: (12, {}), {7}: (11, {})} | custom-call | flops 8053063680 | bytes 25165824 | tf_op jit(solution)/shard_map/layer/pallas_call | solution.py:383
  128.0 23.2 %layer.7 = (bf16[160,8192]{1,0:T(8,128)(2,1)}, bf16[160,1024]{1,0:T(8,128)(2,1)}, bf16[160,1024]{1,0:T(8,128)(2,1)}, bf16[160,1024]{1,0:T(8,128)(2,1)}, bf16[160...) custom-call(s32[4]{0:T(128)} %add_add_fusion.1.refs_0_.me_ref, ...), custom_call_target="tpu_custom_call", output_to_operand_aliasing={{0}: (12, {})} | custom-call | flops 8053063680 | bytes 25165824 | tf_op jit(solution)/shard_map/layer/pallas_call | solution.py:383
  155.0 3.3 %collective-permute-done.51 = f32[512]{0:T(512)S(1)} collective-permute-done((f32[512]{0:T(512)S(1)}, f32[512]{0:T(512)S(1)}, u32[]{:S(2)}, u32[]{:S(2)}) %collective-permute-start.51) | collective-permute-done | bytes 2080 | tf_op jit(solution)/shard_map/ppermute | solution.py:495
  159.1 2.8 %collective-permute-done.52 = f32[512]{0:T(512)S(1)} collective-permute-done((f32[512]{0:T(512)S(1)}, f32[512]{0:T(512)S(1)}, u32[]{:S(2)}, u32[]{:S(2)}) %collective-permute-start.52) | collective-permute-done | bytes 2080 | tf_op jit(solution)/shard_map/ppermute | solution.py:495
  163.2 2.5 convert_add_fusion
  177.3 3.5 %collective-permute-done.30.px = bf16[160,1024]{1,0:T(8,128)(2,1)S(1)} collective-permute-done((bf16[160,1024]{1,0:T(8,128)(2,1)}, bf16[160,1024]{1,0:T(8,128)(2,1)S(1)}, u32[]{:S(2)}, u32[]{:S(2)}) %collective-permute-start.30) | collective-permute-done | bytes 327712 | tf_op jit(solution)/shard_map/ppermute | solution.py:492
  181.1 6.8 %collective-permute-done.33.px = bf16[160,1024]{1,0:T(8,128)(2,1)} collective-permute-done((bf16[160,1024]{1,0:T(8,128)(2,1)}, bf16[160,1024]{1,0:T(8,128)(2,1)}, u32[]{:S(2)}, u32[]{:S(2)}) %collective-permute-start.33) | collective-permute-done | bytes 327712 | tf_op jit(solution)/shard_map/ppermute | solution.py:492
  188.2 4.8 %collective-permute-done.35.pd = bf16[160,1024]{1,0:T(8,128)(2,1)} collective-permute-done((bf16[160,1024]{1,0:T(8,128)(2,1)}, bf16[160,1024]{1,0:T(8,128)(2,1)}, u32[]{:S(2)}, u32[]{:S(2)}) %collective-permute-start.35) | collective-permute-done | bytes 327712 | tf_op jit(solution)/shard_map/ppermute | solution.py:492
  194.9 7.0 %collective-permute-done.36.px = bf16[160,1024]{1,0:T(8,128)(2,1)} collective-permute-done((bf16[160,1024]{1,0:T(8,128)(2,1)}, bf16[160,1024]{1,0:T(8,128)(2,1)}, u32[]{:S(2)}, u32[]{:S(2)}) %collective-permute-start.36) | collective-permute-done | bytes 327712 | tf_op jit(solution)/shard_map/ppermute | solution.py:492
  208.9 7.0 %collective-permute-done.39.px = bf16[160,1024]{1,0:T(8,128)(2,1)S(1)} collective-permute-done((bf16[160,1024]{1,0:T(8,128)(2,1)}, bf16[160,1024]{1,0:T(8,128)(2,1)S(1)}, u32[]{:S(2)}, u32[]{:S(2)}) %collective-permute-start.39) | collective-permute-done | bytes 327712 | tf_op jit(solution)/shard_map/ppermute | solution.py:492
  216.6 4.5 %collective-permute-done.41.pd = bf16[160,1024]{1,0:T(8,128)(2,1)} collective-permute-done((bf16[160,1024]{1,0:T(8,128)(2,1)}, bf16[160,1024]{1,0:T(8,128)(2,1)}, u32[]{:S(2)}, u32[]{:S(2)}) %collective-permute-start.41) | collective-permute-done | bytes 327712 | tf_op jit(solution)/shard_map/ppermute | solution.py:492
  223.0 41.5 %place.1 = bf16[160,8192]{1,0:T(8,128)(2,1)} custom-call(s32[4]{0:T(128)} %add_add_fusion.rows_ref, bf16[160,1024]{1,0:T(8,128)(2,1)} %collective-permute-done.20.refs_0_, bf16[160,1024]{1,0:T(8,128)(2,1)} %collective-permute-done.23.refs_1_, bf16[160,1024]{1,0:T(8,128)(2,1)} %collective-permute-done.26.refs_2_, ...), custom_call_target="tpu_custom_call", output_to_operand_aliasing={{}: (5, {})} | custom-call | bytes 5242880 | tf_op jit(solution)/shard_map/place/pallas_call | solution.py:445
  264.5 2.2 finish.4.refs_0_
  266.7 2.2 finish.5.refs_0_
  268.9 2.2 finish.6.refs_0_
  271.2 2.2 finish.7
  (196 shorter events, 57.6 us)
Async XLA Ops:
  0.6 50.7 %collective-permute-start = (bf16[160,8192]{1,0:T(8,128)(2,1)}, bf16[160,8192]{1,0:T(8,128)(2,1)}, u32[]{:S(2)}, u32[]{:S(2)}) collective-permute-start(bf16[160,8192]{1,0:T(8,128)(2,1)} %refs_1_.7), channel_id=1, source_target_pairs={{0,1},{1,0},{2,3},{3,2},{4,5},{5,4},{6,7},{7,6},{8,9},{9,8},{10,11... | collective-permute-start | bytes 7864328 | tf_op jit(solution)/shard_map/ppermute | solution.py:492
  1.1 51.6 %collective-permute-start.3 = (bf16[160,8192]{1,0:T(8,128)(2,1)}, bf16[160,8192]{1,0:T(8,128)(2,1)}, u32[]{:S(2)}, u32[]{:S(2)}) collective-permute-start(bf16[160,8192]{1,0:T(8,128)(2,1)} %refs_5_.7), channel_id=1, source_target_pairs={{0,1},{1,0},{2,3},{3,2},{4,5},{5,4},{6,7},{7,6},{8,9},{9,8},{10,11... | collective-permute-start | bytes 7864328 | tf_op jit(solution)/shard_map/ppermute | solution.py:492
  49.2 29.6 %collective-permute-start.21 = (bf16[160,1024]{1,0:T(8,128)(2,1)S(1)}, bf16[160,1024]{1,0:T(8,128)(2,1)S(1)}, u32[]{:S(2)}, u32[]{:S(2)}) collective-permute-start(bf16[160,1024]{1,0:T(8,128)(2,1)S(1)} %get-tuple-element.83), channel_id=1, source_target_pairs={{0,2},{1,3},{2,0},{3,1},{4,6},{5,7},{6,4},{7,5},{8,10},{9,11},{10,... | collective-permute-start | bytes 983048 | tf_op jit(solution)/shard_map/ppermute | solution.py:492
  49.8 30.0 %collective-permute-start.22 = (bf16[160,1024]{1,0:T(8,128)(2,1)S(1)}, bf16[160,1024]{1,0:T(8,128)(2,1)S(1)}, u32[]{:S(2)}, u32[]{:S(2)}) collective-permute-start(bf16[160,1024]{1,0:T(8,128)(2,1)S(1)} %get-tuple-element.82), channel_id=1, source_target_pairs={{0,3},{1,2},{2,1},{3,0},{4,7},{5,6},{6,5},{7,4},{8,11},{9,10},{10,... | collective-permute-start | bytes 983048 | tf_op jit(solution)/shard_map/ppermute | solution.py:492
  50.6 52.7 %collective-permute-start.24 = (bf16[160,1024]{1,0:T(8,128)(2,1)S(1)}, bf16[160,1024]{1,0:T(8,128)(2,1)S(1)}, u32[]{:S(2)}, u32[]{:S(2)}) collective-permute-start(bf16[160,1024]{1,0:T(8,128)(2,1)S(1)} %get-tuple-element.81), channel_id=1, source_target_pairs={{0,2},{1,3},{2,0},{3,1},{4,6},{5,7},{6,4},{7,5},{8,10},{9,11},{10,... | collective-permute-start | bytes 983048 | tf_op jit(solution)/shard_map/ppermute | solution.py:492
  51.3 52.1 %collective-permute-start.25 = (bf16[160,1024]{1,0:T(8,128)(2,1)S(1)}, bf16[160,1024]{1,0:T(8,128)(2,1)S(1)}, u32[]{:S(2)}, u32[]{:S(2)}) collective-permute-start(bf16[160,1024]{1,0:T(8,128)(2,1)S(1)} %get-tuple-element.80), channel_id=1, source_target_pairs={{0,3},{1,2},{2,1},{3,0},{4,7},{5,6},{6,5},{7,4},{8,11},{9,10},{10,... | collective-permute-start | bytes 983048 | tf_op jit(solution)/shard_map/ppermute | solution.py:492
  52.7 74.5 %collective-permute-start.27 = (bf16[160,1024]{1,0:T(8,128)(2,1)S(1)}, bf16[160,1024]{1,0:T(8,128)(2,1)S(1)}, u32[]{:S(2)}, u32[]{:S(2)}) collective-permute-start(bf16[160,1024]{1,0:T(8,128)(2,1)S(1)} %get-tuple-element.79), channel_id=1, source_target_pairs={{0,2},{1,3},{2,0},{3,1},{4,6},{5,7},{6,4},{7,5},{8,10},{9,11},{10,... | collective-permute-start | bytes 983048 | tf_op jit(solution)/shard_map/ppermute | solution.py:492
  78.8 48.4 %collective-permute-start.28 = (bf16[160,1024]{1,0:T(8,128)(2,1)S(1)}, bf16[160,1024]{1,0:T(8,128)(2,1)S(1)}, u32[]{:S(2)}, u32[]{:S(2)}) collective-permute-start(bf16[160,1024]{1,0:T(8,128)(2,1)S(1)} %get-tuple-element.78), channel_id=1, source_target_pairs={{0,3},{1,2},{2,1},{3,0},{4,7},{5,6},{6,5},{7,4},{8,11},{9,10},{10,... | collective-permute-start | bytes 983048 | tf_op jit(solution)/shard_map/ppermute | solution.py:492
  170.5 17.4 %collective-permute-start.33 = (bf16[160,1024]{1,0:T(8,128)(2,1)}, bf16[160,1024]{1,0:T(8,128)(2,1)}, u32[]{:S(2)}, u32[]{:S(2)}) collective-permute-start(bf16[160,1024]{1,0:T(8,128)(2,1)} %get-tuple-element.55), channel_id=1, source_target_pairs={{0,2},{1,3},{2,0},{3,1},{4,6},{5,7},{6,4},{7,5},{8,10},{9,11},{10,... | collective-permute-start | bytes 983048 | tf_op jit(solution)/shard_map/ppermute | solution.py:492
  172.0 16.2 %collective-permute-start.34 = (bf16[160,1024]{1,0:T(8,128)(2,1)}, bf16[160,1024]{1,0:T(8,128)(2,1)}, u32[]{:S(2)}, u32[]{:S(2)}) collective-permute-start(bf16[160,1024]{1,0:T(8,128)(2,1)} %get-tuple-element.56), channel_id=1, source_target_pairs={{0,1},{1,0},{2,3},{3,2},{4,5},{5,4},{6,7},{7,6},{8,9},{9,8},{10,11... | collective-permute-start | bytes 983048 | tf_op jit(solution)/shard_map/ppermute | solution.py:492
  173.2 19.9 %collective-permute-start.35 = (bf16[160,1024]{1,0:T(8,128)(2,1)}, bf16[160,1024]{1,0:T(8,128)(2,1)}, u32[]{:S(2)}, u32[]{:S(2)}) collective-permute-start(bf16[160,1024]{1,0:T(8,128)(2,1)} %get-tuple-element.57), channel_id=1, source_target_pairs={{0,3},{1,2},{2,1},{3,0},{4,7},{5,6},{6,5},{7,4},{8,11},{9,10},{10,... | collective-permute-start | bytes 983048 | tf_op jit(solution)/shard_map/ppermute | solution.py:492
  174.6 27.4 %collective-permute-start.36 = (bf16[160,1024]{1,0:T(8,128)(2,1)}, bf16[160,1024]{1,0:T(8,128)(2,1)}, u32[]{:S(2)}, u32[]{:S(2)}) collective-permute-start(bf16[160,1024]{1,0:T(8,128)(2,1)} %get-tuple-element.59), channel_id=1, source_target_pairs={{0,2},{1,3},{2,0},{3,1},{4,6},{5,7},{6,4},{7,5},{8,10},{9,11},{10,... | collective-permute-start | bytes 983048 | tf_op jit(solution)/shard_map/ppermute | solution.py:492
  180.8 21.7 %collective-permute-start.46 = (bf16[160,512]{1,0:T(8,128)(2,1)}, bf16[160,512]{1,0:T(8,128)(2,1)}, u32[]{:S(2)}, u32[]{:S(2)}) collective-permute-start(bf16[160,512]{1,0:T(8,128)(2,1)} %get-tuple-element.74), channel_id=1, source_target_pairs={{0,4},{4,0},{8,12},{12,8},{16,20},{20,16},{24,28},{28,24},{1,5},{5... | collective-permute-start | bytes 491528 | tf_op jit(solution)/shard_map/ppermute | solution.py:495
  187.9 14.6 %collective-permute-start.48 = (bf16[160,512]{1,0:T(8,128)(2,1)}, bf16[160,512]{1,0:T(8,128)(2,1)}, u32[]{:S(2)}, u32[]{:S(2)}) collective-permute-start(bf16[160,512]{1,0:T(8,128)(2,1)} %get-tuple-element.77), channel_id=1, source_target_pairs={{0,8},{4,12},{8,0},{12,4},{16,24},{20,28},{24,16},{28,20},{1,9},{5... | collective-permute-start | bytes 491528 | tf_op jit(solution)/shard_map/ppermute | solution.py:495
  188.2 18.2 %collective-permute-start.37 = (bf16[160,1024]{1,0:T(8,128)(2,1)}, bf16[160,1024]{1,0:T(8,128)(2,1)S(1)}, u32[]{:S(2)}, u32[]{:S(2)}) collective-permute-start(bf16[160,1024]{1,0:T(8,128)(2,1)} %get-tuple-element.60), channel_id=1, source_target_pairs={{0,1},{1,0},{2,3},{3,2},{4,5},{5,4},{6,7},{7,6},{8,9},{9,8},{10,11... | collective-permute-start | bytes 983048 | tf_op jit(solution)/shard_map/ppermute | solution.py:492
  193.0 14.0 %collective-permute-start.38 = (bf16[160,1024]{1,0:T(8,128)(2,1)}, bf16[160,1024]{1,0:T(8,128)(2,1)S(1)}, u32[]{:S(2)}, u32[]{:S(2)}) collective-permute-start(bf16[160,1024]{1,0:T(8,128)(2,1)} %get-tuple-element.61), channel_id=1, source_target_pairs={{0,3},{1,2},{2,1},{3,0},{4,7},{5,6},{6,5},{7,4},{8,11},{9,10},{10,... | collective-permute-start | bytes 983048 | tf_op jit(solution)/shard_map/ppermute | solution.py:492
  202.0 13.9 %collective-permute-start.39 = (bf16[160,1024]{1,0:T(8,128)(2,1)}, bf16[160,1024]{1,0:T(8,128)(2,1)S(1)}, u32[]{:S(2)}, u32[]{:S(2)}) collective-permute-start(bf16[160,1024]{1,0:T(8,128)(2,1)} %get-tuple-element.63), channel_id=1, source_target_pairs={{0,2},{1,3},{2,0},{3,1},{4,6},{5,7},{6,4},{7,5},{8,10},{9,11},{10,... | collective-permute-start | bytes 983048 | tf_op jit(solution)/shard_map/ppermute | solution.py:492
  202.6 13.7 %collective-permute-start.40 = (bf16[160,1024]{1,0:T(8,128)(2,1)}, bf16[160,1024]{1,0:T(8,128)(2,1)S(1)}, u32[]{:S(2)}, u32[]{:S(2)}) collective-permute-start(bf16[160,1024]{1,0:T(8,128)(2,1)} %get-tuple-element.64), channel_id=1, source_target_pairs={{0,1},{1,0},{2,3},{3,2},{4,5},{5,4},{6,7},{7,6},{8,9},{9,8},{10,11... | collective-permute-start | bytes 983048 | tf_op jit(solution)/shard_map/ppermute | solution.py:492
  202.6 18.6 %collective-permute-start.41 = (bf16[160,1024]{1,0:T(8,128)(2,1)}, bf16[160,1024]{1,0:T(8,128)(2,1)}, u32[]{:S(2)}, u32[]{:S(2)}) collective-permute-start(bf16[160,1024]{1,0:T(8,128)(2,1)} %get-tuple-element.65), channel_id=1, source_target_pairs={{0,3},{1,2},{2,1},{3,0},{4,7},{5,6},{6,5},{7,4},{8,11},{9,10},{10,... | collective-permute-start | bytes 983048 | tf_op jit(solution)/shard_map/ppermute | solution.py:492
  206.5 64.7 %collective-permute-start.31 = (bf16[160,1024]{1,0:T(8,128)(2,1)}, bf16[160,1024]{1,0:T(8,128)(2,1)}, u32[]{:S(2)}, u32[]{:S(2)}) collective-permute-start(bf16[160,1024]{1,0:T(8,128)(2,1)} %get-tuple-element.52), channel_id=1, source_target_pairs={{0,1},{1,0},{2,3},{3,2},{4,5},{5,4},{6,7},{7,6},{8,9},{9,8},{10,11... | collective-permute-start | bytes 983048 | tf_op jit(solution)/shard_map/ppermute | solution.py:492
  207.1 64.1 %collective-permute-start.32 = (bf16[160,1024]{1,0:T(8,128)(2,1)}, bf16[160,1024]{1,0:T(8,128)(2,1)}, u32[]{:S(2)}, u32[]{:S(2)}) collective-permute-start(bf16[160,1024]{1,0:T(8,128)(2,1)} %get-tuple-element.53), channel_id=1, source_target_pairs={{0,3},{1,2},{2,1},{3,0},{4,7},{5,6},{6,5},{7,4},{8,11},{9,10},{10,... | collective-permute-start | bytes 983048 | tf_op jit(solution)/shard_map/ppermute | solution.py:492
  215.9 57.5 %collective-permute-start.43 = (bf16[160,512]{1,0:T(8,128)(2,1)S(1)}, bf16[160,512]{1,0:T(8,128)(2,1)}, u32[]{:S(2)}, u32[]{:S(2)}) collective-permute-start(bf16[160,512]{1,0:T(8,128)(2,1)S(1)} %get-tuple-element.72), channel_id=1, source_target_pairs={{0,8},{4,12},{8,0},{12,4},{16,24},{20,28},{24,16},{28,20},{1,9},{5... | collective-permute-start | bytes 491528 | tf_op jit(solution)/shard_map/ppermute | solution.py:495
  216.2 57.2 %collective-permute-start.45 = (bf16[160,512]{1,0:T(8,128)(2,1)}, bf16[160,512]{1,0:T(8,128)(2,1)}, u32[]{:S(2)}, u32[]{:S(2)}) collective-permute-start(bf16[160,512]{1,0:T(8,128)(2,1)} %get-tuple-element.76), channel_id=1, source_target_pairs={{0,4},{4,0},{8,12},{12,8},{16,20},{20,16},{24,28},{28,24},{1,5},{5... | collective-permute-start | bytes 491528 | tf_op jit(solution)/shard_map/ppermute | solution.py:495
  221.1 52.3 %collective-permute-start.49 = (bf16[160,512]{1,0:T(8,128)(2,1)}, bf16[160,512]{1,0:T(8,128)(2,1)}, u32[]{:S(2)}, u32[]{:S(2)}) collective-permute-start(bf16[160,512]{1,0:T(8,128)(2,1)} %fusion.2), channel_id=1, source_target_pairs={{0,16},{4,20},{8,24},{12,28},{16,0},{20,4},{24,8},{28,12},{1,17},{... | collective-permute-start | bytes 491528 | tf_op jit(solution)/shard_map/ppermute | solution.py:495
  (57 other events, 614.6 us)

commit v2 on v0

--- a/solution.py
+++ b/solution.py
@@ -1,17 +1,755 @@
+import functools
+
 import jax
 import jax.numpy as jnp
 from jax import lax
+from jax.experimental import pallas as pl
+from jax.experimental.pallas import tpu as pltpu
 from jax.sharding import PartitionSpec as P
 
 LEN = 1024
 MICRO = 4
+LANES = 128
+SEGS = 8
+PAD = 8
+TILE = 256
+UNROLL = 16
+FTILE = 1024
+CALLS = 2
+EARLY = (0, 1, 2, 4)
+LATE = (3, 5, 6, 7)
+f32 = jnp.float32
+bf16 = jnp.bfloat16
+ANY = pl.BlockSpec(memory_space=pl.ANY)
+VMEM = pl.BlockSpec(memory_space=pltpu.VMEM)
+SMEM = pl.BlockSpec(memory_space=pltpu.SMEM)
+
+
+def dot(a, b, ca, cb):
+    return lax.dot_general(a, b, (((ca,), (cb,)), ((), ())), preferred_element_type=f32)
+
+
+def sigmoid(v):
+    return 0.5 * jnp.tanh(0.5 * v) + 0.5
+
+
+def layer_kernel(k, calls, rows, parts, C, n, *refs):
+    first, last = k == 0, k == calls - 1
+    refs = list(refs)
+    tok, sib, cot, scot, ids, bias, bias_sib, x_near, x_far = refs[:9]
+    refs = refs[9:]
+    if first:
+        w_in, refs = refs[: parts + 1 + len(LATE)], refs[parts + 1 + len(LATE) :]
+    else:
+        w_in, acc_in, refs = refs[0], refs[1], refs[3:]
+    hid, to_sib, dx_px, dx_pd, dx_own = refs[:5]
+    refs = refs[5:]
+    if last:
+        acc_own, acc_sib, refs = refs[0], refs[1], refs[2:]
+    else:
+        acc_out, refs = refs[0], refs[1:]
+    if first:
+        w_out, refs = refs[0], refs[1:]
+    (xb, wb, cb, pre, zs, fs, os_, cbs, ct, hs, hb, dp, dxb, accb, ab, small, nxt, sums, cl, ca_t, id_b, bb, sem, rsem) = refs
+    D = 4 * C
+    tl = C - LANES
+    steps = n // SEGS
+    sp = steps + PAD
+    half = 4 * LANES
+    me, place = lax.axis_index("chan"), lax.axis_index("dp")
+    core = me & 1
+
+    def go(src, dst, i):
+        copy = pltpu.make_async_copy(src, dst, sem.at[i])
+        copy.start()
+        return copy
+
+    def here(r):
+        return pl.ds(pl.multiple_of((2 * (k * rows + r) + core) * n, n), n)
+
+    def span(r):
+        return pl.ds(pl.multiple_of(r * n, n), n)
+
+    def block(j):
+        return pl.ds(pl.multiple_of((me ^ j) * C, 32), C)
+
+    def seg(h):
+        return pl.ds(pl.multiple_of(h * sp, 8), steps)
+
+    def id_rows(r):
+        return pl.ds(pl.multiple_of((2 * (k * rows + r) + core) * SEGS, SEGS), SEGS)
+
+    def x_copies(r):
+        from_row = span(r)
+        pairs = (
+            (tok.at[:, here(r)], xb.at[block(0), span(r)]),
+            (sib.at[:, here(r)], xb.at[block(1), span(r)]),
+            (x_near.at[:, from_row], xb.at[block(2), span(r)]),
+            (x_far.at[:, from_row], xb.at[block(3), span(r)]),
+            (ids.at[id_rows(r)], id_b.at[r]),
+        )
+        return [pltpu.make_async_copy(a, b, rsem.at[r, i]) for i, (a, b) in enumerate(pairs)]
+
+    def c_copies(r):
+        pairs = (
+            (cot.at[0:LANES, here(r)], cb.at[0:LANES, span(r)]),
+            (scot.at[0:LANES, here(r)], cb.at[LANES : 2 * LANES, span(r)]),
+            (cot.at[LANES:C, here(r)], cb.at[2 * LANES : 2 * LANES + tl, span(r)]),
+            (scot.at[LANES:C, here(r)], cb.at[2 * LANES + tl : 2 * LANES + 2 * tl, span(r)]),
+        )
+        return [pltpu.make_async_copy(a, b, rsem.at[r, 5 + i]) for i, (a, b) in enumerate(pairs)]
+
+    def hidden_copies(r):
+        pairs = (
+            (hb.at[0:LANES, span(r)], hid.at[0:LANES, here(r)]),
+            (hb.at[LANES : 2 * LANES, span(r)], to_sib.at[C : C + LANES, span(r)]),
+            (hb.at[2 * LANES : 2 * LANES + tl, span(r)], hid.at[LANES:C, here(r)]),
+            (hb.at[2 * LANES + tl : 2 * LANES + 2 * tl, span(r)], to_sib.at[C + LANES : 2 * C, span(r)]),
+        )
+        return [pltpu.make_async_copy(a, b, rsem.at[r, 10 + i]) for i, (a, b) in enumerate(pairs)]
+
+    def grad_copies(r):
+        outs = (dx_own, to_sib.at[0:C], dx_px, dx_pd)
+        return [
+            pltpu.make_async_copy(dxb.at[block(j), span(r)], out.at[:, span(r)], rsem.at[r, 14 + j])
+            for j, out in enumerate(outs)
+        ]
+
+    for copy in x_copies(0):
+        copy.start()
+    if first:
+        w_copies = []
+        for j in range(parts):
+            at = pl.ds(pl.multiple_of((place ^ j) * C, 32), C)
+            w_copies.append(go(w_in[j], wb.at[at, 0:half], 8 + j))
+            if j in EARLY:
+                other = w_in[parts].at[EARLY.index(j) * C : (EARLY.index(j) + 1) * C]
+            else:
+                other = w_in[parts + 1 + LATE.index(j)]
+            w_copies.append(go(other, wb.at[at, half : 2 * half], 8 + parts + j))
+    else:
+        w_copies = [go(w_in, wb, 0)]
+    b_copies = [go(bias, bb.at[:, 0:half], 1), go(bias_sib, bb.at[:, half : 2 * half], 3)]
+    for copy in c_copies(0):
+        copy.start()
+    sums[...] = jnp.zeros_like(sums)
+    lane = lax.broadcasted_iota(jnp.int32, (SEGS, LANES), 1)
+    edge = lax.broadcasted_iota(jnp.int32, (D, LANES), 1) == LANES - 1
+    cols = [slice(q * LANES, (q + 1) * LANES) for q in range(3)]
+    one = jnp.ones((SEGS, LANES), f32)
+    zero = jnp.zeros((SEGS, LANES), f32)
+
+    def strided(ref, t, q):
+        return ref[q, pl.ds(t, SEGS, stride=sp), :]
+
+    def now(t):
+        return pl.ds(pl.multiple_of(t * SEGS, SEGS), SEGS)
+
+    def row(r, _):
+        for copy in x_copies(r):
+            copy.wait()
+        seg_ids = id_b[r]
+        before = pltpu.roll(seg_ids, 1, 1)
+        before = jnp.where(lane == 0, pltpu.roll(before, 1, 0), before)
+        sub = lax.broadcasted_iota(jnp.int32, (SEGS, steps), 0)
+        carry = jnp.where((seg_ids == before) & ((lane > 0) | (sub > 0)), 1.0, 0.0).astype(f32)
+        for s in range(SEGS):
+            cl[:, s * steps : (s + 1) * steps] = jnp.broadcast_to(carry[s : s + 1, :], (SEGS, steps))
+        for t in range(steps):
+            ca_t[t * SEGS : (t + 1) * SEGS, :] = jnp.broadcast_to(carry[:, t : t + 1], (SEGS, LANES))
+        rb = 32
+
+        def prev_step(i, _):
+            o = pl.multiple_of(i * rb, rb)
+            v = xb[pl.ds(o, rb), span(r)].astype(f32)
+            xb[pl.ds(D + o, rb), span(r)] = (pltpu.roll(v, 1, 1) * cl[0:1, :]).astype(bf16)
+            return 0
+
+        lax.fori_loop(0, D // rb, prev_step, 0)
+
+        @pl.when(r == 0)
+        def _():
+            for copy in w_copies:
+                copy.wait()
+            for copy in b_copies:
+                copy.wait()
+            if first:
+                go(wb, w_out, 0)
+            else:
+                go(acc_in, accb, 2)
+
+        for copy in c_copies(r):
+            copy.wait()
+
+        @pl.when(r + 1 < rows)
+        def _():
+            for copy in x_copies(r + 1) + c_copies(r + 1):
+                copy.start()
+
+        b = [jnp.broadcast_to(bb[0:1, q * LANES : (q + 1) * LANES], (SEGS, LANES)) for q in range(8)]
+
+        def forward_step(i, _):
+            o = pl.multiple_of(r * n + i * FTILE, FTILE)
+            v = dot(xb[:, pl.ds(o, FTILE)], wb[...], 0, 0)
+            for h in range(FTILE // steps):
+                at = seg(i * (FTILE // steps) + h)
+                for q in range(8):
+                    pre[q, at, :] = v[h * steps : (h + 1) * steps, q * LANES : (q + 1) * LANES]
+                c = cb[:, pl.ds(pl.multiple_of(o + h * steps, LANES), steps)].astype(f32).T
+                for q in range(3):
+                    ct[q, at, :] = c[:, q * LANES : (q + 1) * LANES]
+            return 0
+
+        lax.fori_loop(0, n // FTILE, forward_step, 0)
+
+        def gates_step(t, state):
+            gain, total = state
+            v = [strided(pre, t, q) + b[q] for q in range(8)]
+            u, w = v[3], v[7]
+            tz = jnp.where(lane < tl, u, pltpu.roll(w, tl, 1))
+            tf = jnp.where(lane < tl, pltpu.roll(u, LANES - tl, 1), w)
+            to = jnp.where(lane < tl, pltpu.roll(u, LANES - 2 * tl, 1), pltpu.roll(w, LANES - tl, 1))
+            z = [jnp.tanh(g) for g in (v[0], v[4], tz)]
+            f = [sigmoid(g) for g in (v[1], v[5], tf)]
+            o = [sigmoid(g) for g in (v[2], v[6], to)]
+            at = now(t)
+            ca = ca_t[at, :]
+            gains, totals = [], []
+            for q in range(3):
+                zs[at, cols[q]] = z[q]
+                fs[at, cols[q]] = f[q]
+                os_[at, cols[q]] = o[q]
+                gains.append(gain[q] * (f[q] * ca))
+                totals.append(z[q] + f[q] * (ca * total[q] - z[q]))
+            return tuple(gains), tuple(totals)
+
+        gain, total = lax.fori_loop(0, steps, gates_step, ((one,) * 3, (zero,) * 3), unroll=UNROLL)
+        for q in range(3):
+            small[0, :, cols[q]] = gain[q]
+            small[1, :, cols[q]] = total[q]
+        run = jnp.zeros((1, 3 * LANES), f32)
+        for s in range(SEGS):
+            small[2, s : s + 1, :] = run
+            run = small[0, s : s + 1, :] * run + small[1, s : s + 1, :]
+        cell = tuple(small[2, :, cols[q]] for q in range(3))
+
+        def cell_step(t, state):
+            cell, back, gain = state
+            at = now(t)
+            ca = ca_t[at, :]
+            cells, backs, gains = [], [], []
+            for q in range(3):
+                z, f, o = zs[at, cols[q]], fs[at, cols[q]], os_[at, cols[q]]
+                prev = ca * cell[q]
+                cbs[at, cols[q]] = prev
+                new = z + f * (prev - z)
+                hs[q, pl.ds(t, SEGS, stride=sp), :] = o * new
+                g = jnp.where(t == 0, one, gain[q] * (f * ca))
+                cells.append(new)
+                gains.append(g)
+                backs.append(back[q] + g * (strided(ct, t, q) * o))
+            return tuple(cells), tuple(backs), tuple(gains)
+
+        cell, back, gain = lax.fori_loop(0, steps, cell_step, (cell, (zero,) * 3, (one,) * 3), unroll=UNROLL)
+        for q in range(3):
+            small[0, :, cols[q]] = back[q]
+            small[1, :, cols[q]] = gain[q]
+            small[3, :, cols[q]] = fs[0:SEGS, cols[q]] * ca_t[0:SEGS, :]
+        run = jnp.zeros((1, 3 * LANES), f32)
+        for s in range(SEGS - 1, -1, -1):
+            small[2, s : s + 1, :] = run
+            run = small[3, s : s + 1, :] * (small[0, s : s + 1, :] + small[1, s : s + 1, :] * run)
+        later = tuple(small[2, :, cols[q]] for q in range(3))
+
+        def grad_step(i, later):
+            t = steps - 1 - i
+            at = now(t)
+            ca = ca_t[at, :]
+            gz, gf, go_, laters = [], [], [], []
+            for q in range(3):
+                z, f, o, prev = zs[at, cols[q]], fs[at, cols[q]], os_[at, cols[q]], cbs[at, cols[q]]
+                c = strided(ct, t, q)
+                dc = c * o + later[q]
+                laters.append((f * ca) * dc)
+                d = prev - z
+                u = dc * (1.0 - f)
+                gz.append(u * (1.0 - z * z))
+                gf.append(u * (f * d))
+                go_.append(c * (z + f * d) * (o * (1.0 - o)))
+            z, f, o = gz[2], gf[2], go_[2]
+            u = jnp.where(
+                lane < tl,
+                z,
+                jnp.where(
+                    lane < 2 * tl,
+                    pltpu.roll(f, tl, 1),
+                    jnp.where(lane < 3 * tl, pltpu.roll(o, 2 * tl, 1), 0.0),
+                ),
+            )
+            w = jnp.where(
+                lane < tl,
+                pltpu.roll(z, LANES - tl, 1),
+                jnp.where(lane < 2 * tl, f, jnp.where(lane < 3 * tl, pltpu.roll(o, tl, 1), 0.0)),
+            )
+            for q, v in enumerate((gz[0], gf[0], go_[0], u, gz[1], gf[1], go_[1], w)):
+                pre[q, pl.ds(t, SEGS, stride=sp), :] = v
+            return tuple(laters)
+
+        lax.fori_loop(0, steps, grad_step, later, unroll=UNROLL)
+
+        nxt[...] = jnp.zeros_like(nxt)
+
+        def input_step(i, _):
+            i = n // TILE - 1 - i
+            o = pl.multiple_of(i * TILE, TILE)
+            for h in range(TILE // steps):
+                into = pl.ds(pl.multiple_of(r * n + o + h * steps, LANES), steps)
+                for q in range(8):
+                    v = pre[q, seg(i * (TILE // steps) + h), :].astype(bf16)
+                    dp[into, q * LANES : (q + 1) * LANES] = v
+                    v = v.astype(f32)
+                    a = v[0:SEGS]
+                    for s in range(SEGS, steps, SEGS):
+                        a = a + v[s : s + SEGS]
+                    sums[:, q * LANES : (q + 1) * LANES] += a
+                for q in range(3):
+                    e = LANES if q < 2 else 2 * tl
+                    v = hs[q, seg(i * (TILE // steps) + h), :].T.astype(bf16)
+                    hb[q * LANES : q * LANES + e, into] = v[0:e]
+            dj = dot(wb[...], dp[pl.ds(pl.multiple_of(r * n + o, TILE), TILE), :], 1, 1)
+            after = nxt[...]
+            for h in range(TILE // LANES - 1, -1, -1):
+                at = slice(h * LANES, (h + 1) * LANES)
+                into = pl.ds(pl.multiple_of(r * n + o + h * LANES, LANES), LANES)
+                rolled = pltpu.roll(
+                    dj[D:, at] * cl[0:1, pl.ds(pl.multiple_of(o + h * LANES, LANES), LANES)], LANES - 1, 1
+                )
+                dxb[:, into] = (dj[:D, at] + jnp.where(edge, after, rolled)).astype(bf16)
+                after = rolled
+            nxt[...] = after
+            return 0
+
+        lax.fori_loop(0, n // TILE, input_step, 0)
+        for copy in hidden_copies(r) + grad_copies(r):
+            copy.start()
+        return 0
+
+    lax.fori_loop(0, rows, row, 0)
+    if not first:
+        pltpu.make_async_copy(acc_in, accb, sem.at[2]).wait()
+    for q in range(8):
+        at = slice(q * LANES, (q + 1) * LANES)
+        s = sums[:, at]
+        if not first:
+            s = s + accb[2 * D :, at]
+        if last:
+            s = jnp.sum(s, 0, keepdims=True)
+            if q >= 4:
+                ab[2 * D :, (q - 4) * LANES : (q - 3) * LANES] = in_two(s)
+        accb[2 * D :, at] = jnp.broadcast_to(s, (SEGS, LANES))
+
+    def own_copy(i):
+        at = pl.ds(pl.multiple_of(i * TILE, TILE), TILE)
+        return pltpu.make_async_copy(accb.at[:, at], (acc_own if last else acc_out).at[:, at], sem.at[4 + i])
+
+    def sib_copy(i):
+        at = pl.ds(pl.multiple_of(i * TILE, TILE), TILE)
+        return pltpu.make_async_copy(ab.at[:, at], acc_sib.at[:, at], sem.at[2 + i])
+
+    def weight_step(i, _):
+        at = pl.ds(pl.multiple_of(i * TILE, TILE), TILE)
+        v = dot(xb[...], dp[:, at], 1, 0)
+        if not first:
+            v = v + accb[0 : 2 * D, at]
+        accb[0 : 2 * D, at] = v
+        own_copy(i).start()
+        return 0
+
+    def weight_sib_step(i, _):
+        at = pl.ds(pl.multiple_of(half + i * TILE, TILE), TILE)
+        v = dot(xb[...], dp[:, at], 1, 0)
+        if not first:
+            v = v + accb[0 : 2 * D, at]
+        ab[0 : 2 * D, pl.ds(pl.multiple_of(i * TILE, TILE), TILE)] = v.astype(bf16)
+        sib_copy(i).start()
+        return 0
+
+    own_tiles = (half if last else 2 * half) // TILE
+    if last:
+        lax.fori_loop(0, half // TILE, weight_sib_step, 0)
+    lax.fori_loop(0, own_tiles, weight_step, 0)
+    for i in range(own_tiles):
+        own_copy(i).wait()
+    if last:
+        for i in range(half // TILE):
+            sib_copy(i).wait()
+    if first:
+        pltpu.make_async_copy(wb, w_out, sem.at[0]).wait()
+    for r in range(rows):
+        for copy in hidden_copies(r) + grad_copies(r):
+            copy.wait()
+
+
+def layer(k, calls, rows, parts, C, n, tok, sib, cot, scot, ids, biases, x, w, acc, hid):
+    first, last = k == 0, k == calls - 1
+    D = 4 * C
+    N = 8 * LANES
+    T = rows * n
+    shape = jax.ShapeDtypeStruct
+    ins = [tok, sib, cot, scot, ids] + list(biases) + list(x)
+    alias = {}
+    outs = [shape(tok.shape, bf16), shape((2 * C, T), bf16)] + [shape((C, T), bf16)] * 3
+    if first:
+        ins += list(w)
+    else:
+        ins += [w, acc, hid]
+        alias = {len(ins) - 1: 0}
+        if not last:
+            alias[len(ins) - 2] = 5
+    if last:
+        outs += [shape((2 * D + SEGS, N // 2), f32), shape((2 * D + 16, N // 2), bf16)]
+    else:
+        outs += [shape((2 * D + SEGS, N), f32)]
+    if first:
+        outs += [shape((2 * D, N), bf16)]
+    w3 = 3 * LANES
+    tall = n + SEGS * PAD
+    scratch = (
+        [
+            pltpu.VMEM((2 * D, T), bf16),
+            pltpu.VMEM((2 * D, N), bf16),
+            pltpu.VMEM((w3, T), bf16),
+            pltpu.VMEM((8, tall, LANES), f32),
+        ]
+        + [pltpu.VMEM((n, w3), f32)] * 4
+        + [pltpu.VMEM((3, tall, LANES), f32)] * 2
+        + [
+            pltpu.VMEM((2 * C, T), bf16),
+            pltpu.VMEM((T, N), bf16),
+            pltpu.VMEM((D, T), bf16),
+            pltpu.VMEM((2 * D + SEGS, N), f32),
+            pltpu.VMEM((2 * D + 16, N // 2), bf16),
+            pltpu.VMEM((4, SEGS, w3), f32),
+            pltpu.VMEM((D, LANES), f32),
+            pltpu.VMEM((SEGS, N), f32),
+            pltpu.VMEM((SEGS, n), f32),
+            pltpu.VMEM((n, LANES), f32),
+            pltpu.VMEM((rows, SEGS, LANES), jnp.int32),
+            pltpu.VMEM((SEGS, N), f32),
+            pltpu.SemaphoreType.DMA((8 + 2 * parts,)),
+            pltpu.SemaphoreType.DMA((rows, 18)),
+        ]
+    )
+    return pl.pallas_call(
+        functools.partial(layer_kernel, k, calls, rows, parts, C, n),
+        out_shape=outs,
+        in_specs=[ANY] * len(ins),
+        out_specs=[ANY] * len(outs),
+        scratch_shapes=scratch,
+        input_output_aliases=alias,
+        compiler_params=pltpu.CompilerParams(vmem_limit_bytes=60 << 20),
+        cost_estimate=pl.CostEstimate(flops=1, bytes_accessed=1, transcendentals=0),
+        name="layer",
+    )(*ins)
+
+
+def take_kernel(picks, n, tok, *refs):
+    outs, (bufs, sem) = refs[:-2], refs[-2:]
+    core = lax.axis_index("chan") & 1
+    copies, sends = [], []
+    for i, pick in enumerate(picks):
+        for j, (pair, mine) in enumerate(pick):
+            at = pl.ds(pl.multiple_of((2 * pair + (core if mine else 1 - core)) * n, n), n)
+            copies.append(pltpu.make_async_copy(tok.at[:, at], bufs.at[i, :, j * n : (j + 1) * n], sem.at[i, j]))
+            copies[-1].start()
+    for i, pick in enumerate(picks):
+        for copy in copies[i * len(pick) : (i + 1) * len(pick)]:
+            copy.wait()
+        sends.append(pltpu.make_async_copy(bufs.at[i], outs[i], sem.at[i, 0]))
+        sends[-1].start()
+    for send in sends:
+        send.wait()
+
+
+def take_rows(picks, C, n, tok):
+    width = len(picks[0]) * n
+    return pl.pallas_call(
+        functools.partial(take_kernel, picks, n),
+        out_shape=[jax.ShapeDtypeStruct((C, width), bf16)] * len(picks),
+        in_specs=[ANY],
+        out_specs=[ANY] * len(picks),
+        scratch_shapes=[
+            pltpu.VMEM((len(picks), C, width), bf16),
+            pltpu.SemaphoreType.DMA((len(picks), len(picks[0]))),
+        ],
+        cost_estimate=pl.CostEstimate(flops=1, bytes_accessed=1, transcendentals=0),
+        name="take",
+    )(tok)
+
+
+def pack_kernel(C, w, b, out, b_out):
+    tail = C - LANES
+    parts = [w[g, 0:LANES].astype(f32) for g in range(3)] + [w[g, LANES:C].astype(f32) for g in range(3)]
+    parts.append(jnp.zeros((LANES - 3 * tail, w.shape[2]), f32))
+    out[...] = jnp.concatenate(parts, 0).T.astype(bf16)
+    b_out[...] = jnp.zeros_like(b_out)
+    for g in range(3):
+        b_out[0:1, g * LANES : (g + 1) * LANES] = b[g : g + 1, 0:LANES]
+        b_out[0:1, 3 * LANES + g * tail : 3 * LANES + (g + 1) * tail] = b[g : g + 1, LANES:C]
+
+
+def pack(C, w, b):
+    return pl.pallas_call(
+        functools.partial(pack_kernel, C),
+        out_shape=[
+            jax.ShapeDtypeStruct((w.shape[2], 4 * LANES), bf16),
+            jax.ShapeDtypeStruct((SEGS, 4 * LANES), f32),
+        ],
+        in_specs=[VMEM] * 2,
+        out_specs=[VMEM] * 2,
+        cost_estimate=pl.CostEstimate(flops=1, bytes_accessed=1, transcendentals=0),
+        name="pack",
+    )(w, b)
+
+
+def finish_kernel(k, rows, mine, C, n, near, far, *refs):
+    total, sem = refs[-2:]
+    if mine:
+        grad = refs[-3]
+    else:
+        grad, hid = refs[-4:-2]
+    core = lax.axis_index("chan") & 1
+    which = core if mine else 1 - core
+    copies = []
+
+    def go(src, out, r):
+        at = pl.ds(pl.multiple_of((2 * (k * rows + r) + which) * n, n), n)
+        copies.append(pltpu.make_async_copy(src, out.at[:, at], sem.at[len(copies)]))
+        copies[-1].start()
+
+    for r in range(rows):
+        at = slice(r * n, (r + 1) * n)
+        if not mine:
+            go(near.at[C : 2 * C, at], hid, r)
+        total[:, at] = (near[0:C, at].astype(f32) + far[:, at].astype(f32)).astype(bf16)
+        go(total.at[:, at], grad, r)
+    for copy in copies:
+        copy.wait()
+
+
+def finish(k, rows, mine, C, n, total, near, far, grad, hid=None):
+    ins = [near, far]
+    specs = [VMEM] * 2
+    shape = jax.ShapeDtypeStruct((C, total), bf16)
+    outs = [shape]
+    alias = {}
+    for v in (grad, hid):
+        if v is not None:
+            alias[len(ins)] = 0 if v is grad else 1
+            ins.append(v)
+            specs.append(ANY)
+    if hid is not None:
+        outs.append(shape)
+    return pl.pallas_call(
+        functools.partial(finish_kernel, k, rows, mine, C, n),
+        out_shape=outs,
+        in_specs=specs,
+        out_specs=[ANY] * len(outs),
+        scratch_shapes=[pltpu.VMEM((C, rows * n), bf16), pltpu.SemaphoreType.DMA((2 * rows,))],
+        input_output_aliases=alias,
+        cost_estimate=pl.CostEstimate(flops=1, bytes_accessed=1, transcendentals=0),
+        name="finish",
+    )(*ins)
+
+
+def in_two(v):
+    high = v.astype(bf16)
+    low = v - high.astype(f32)
+    at = lax.broadcasted_iota(jnp.int32, (16, v.shape[1]), 0)
+    return jnp.where(at == 0, high.astype(f32), jnp.where(at == 1, low, 0.0)).astype(bf16)
+
+
+def from_two(v):
+    v = v[...].astype(f32)
+    return v[0:1] + v[1:2]
+
+
+def split_kernel(C, own, other, s7, s3, s5, s2, kept):
+    place = lax.axis_index("dp")
+    b = own[8 * C : 8 * C + 1, :] + from_two(other[8 * C :, :])
+    for j, out in ((7, s7), (3, s3), (5, s5), (2, s2)):
+        at = pl.ds(pl.multiple_of((place ^ j) * C, 32), C)
+        out[0:C] = (own[at, :] + other[at, :].astype(f32)).astype(bf16)
+        out[C:] = in_two(b)
+    for i, j in enumerate((0, 1, 4, 6)):
+        at = pl.ds(pl.multiple_of((place ^ j) * C, 32), C)
+        kept[i, 0:C] = own[at, :] + other[at, :].astype(f32)
+    kept[0, C : C + 8] = jnp.broadcast_to(b, (8, b.shape[1]))
+
+
+def split(C, own, other):
+    half = own.shape[1]
+    message = jax.ShapeDtypeStruct((C + 16, half), bf16)
+    return pl.pallas_call(
+        functools.partial(split_kernel, C),
+        out_shape=[message] * 4 + [jax.ShapeDtypeStruct((4, C + 16, half), f32)],
+        in_specs=[VMEM] * 2,
+        out_specs=[VMEM] * 5,
+        compiler_params=pltpu.CompilerParams(vmem_limit_bytes=40 << 20),
+        cost_estimate=pl.CostEstimate(flops=1, bytes_accessed=1, transcendentals=0),
+        name="split",
+    )(own, other)
+
+
+def second_kernel(C, kept, r7, r3, r5, s6, s1, k4):
+    b = kept[0, C : C + 1]
+    s6[0:C] = (kept[3, 0:C] + r7[0:C].astype(f32)).astype(bf16)
+    s6[C:] = in_two(b + from_two(r7[C:]))
+    s1[0:C] = (kept[1, 0:C] + r3[0:C].astype(f32)).astype(bf16)
+    s1[C:] = in_two(b + from_two(r3[C:]))
+    k4[0:C] = kept[2, 0:C] + r5[0:C].astype(f32)
+    k4[C : C + 8] = jnp.broadcast_to(b + from_two(r5[C:]), (8, b.shape[1]))
+
+
+def second(C, kept, r7, r3, r5):
+    half = kept.shape[2]
+    message = jax.ShapeDtypeStruct((C + 16, half), bf16)
+    return pl.pallas_call(
+        functools.partial(second_kernel, C),
+        out_shape=[message] * 2 + [jax.ShapeDtypeStruct((C + 16, half), f32)],
+        in_specs=[VMEM] * 4,
+        out_specs=[VMEM] * 3,
+        cost_estimate=pl.CostEstimate(flops=1, bytes_accessed=1, transcendentals=0),
+        name="second",
+    )(kept, r7, r3, r5)
+
+
+def third_kernel(C, k4, r6, s4):
+    s4[0:C] = (k4[0:C] + r6[0:C].astype(f32)).astype(bf16)
+    s4[C:] = in_two(k4[C : C + 1] + from_two(r6[C:]))
+
+
+def third(C, k4, r6):
+    return pl.pallas_call(
+        functools.partial(third_kernel, C),
+        out_shape=jax.ShapeDtypeStruct(r6.shape, bf16),
+        in_specs=[VMEM] * 2,
+        out_specs=VMEM,
+        cost_estimate=pl.CostEstimate(flops=1, bytes_accessed=1, transcendentals=0),
+        name="third",
+    )(k4, r6)
+
+
+def total_kernel(C, kept, r2, r1, r4, grad, bias):
+    v = kept[0, 0:C] + r2[0:C].astype(f32) + (r1[0:C].astype(f32) + r4[0:C].astype(f32))
+    t = v.T
+    tail = C - LANES
+    for g in range(3):
+        grad[g, 0:LANES] = t[g * LANES : (g + 1) * LANES]
+        grad[g, LANES:C] = t[3 * LANES + g * tail : 3 * LANES + (g + 1) * tail]
+    b = kept[0, C : C + 1] + from_two(r2[C:]) + (from_two(r1[C:]) + from_two(r4[C:]))
+    for g in range(3):
+        bias[g : g + 1, 0:LANES] = b[:, g * LANES : (g + 1) * LANES]
+        bias[g : g + 1, LANES:C] = b[:, 3 * LANES + g * tail : 3 * LANES + (g + 1) * tail]
+
+
+def total_sum(C, kept, r2, r1, r4):
+    return pl.pallas_call(
+        functools.partial(total_kernel, C),
+        out_shape=[jax.ShapeDtypeStruct((3, C, C), f32), jax.ShapeDtypeStruct((3, C), f32)],
+        in_specs=[VMEM] * 4,
+        out_specs=[VMEM] * 2,
+        cost_estimate=pl.CostEstimate(flops=1, bytes_accessed=1, transcendentals=0),
+        name="total",
+    )(kept, r2, r1, r4)
+
+
+def local(chan, parts, tokens, weights, bias, segment_ids, cotangent):
+    C, total = tokens.shape
+    n = LEN
+    pairs = total // n // 2
+    rows = pairs // CALLS
+    me = lax.axis_index("chan")
+    core = me & 1
+
+    def chan_move(v, j):
+        return lax.ppermute(v, "chan", [(i, i ^ j) for i in range(chan)])
+
+    def dp_move(v, j):
+        return lax.ppermute(v, "dp", [(i, i ^ j) for i in range(parts)])
+
+    def after(v, *others):
+        return lax.optimization_barrier((v,) + others)[0]
+
+    ids = segment_ids.reshape(2 * pairs * SEGS, n // SEGS)
+    def other_rows(k, tok):
+        picks = [[(k * rows + r, mine) for r in range(rows)] for mine in (True, False)]
+        return take_rows(picks, C, n, tok)
+
+    to_near, to_far = other_rows(0, tokens)
+    near, far = chan_move(to_near, 2), chan_move(to_far, 3)
+    xs = [(near, far)]
+    shard, b_own = pack(C, after(weights, to_near), bias)
+    g = {0: shard, 4: dp_move(shard, 4), 1: dp_move(shard, 1), 2: dp_move(shard, 2)}
+    sib = chan_move(tokens, 1)
+    scot = chan_move(cotangent, 1)
+    g4, g1 = lax.optimization_barrier((g[4], g[1], sib))[:2]
+    g[6] = dp_move(g4, 2)
+    g[5] = dp_move(g4, 1)
+    g[3] = dp_move(g1, 2)
+    early = chan_move(jnp.concatenate([g[j] for j in EARLY], 0), 1)
+    biases = [b_own, chan_move(after(b_own, g[4]), 1)]
+    g[7] = dp_move(after(g[6], near, scot), 1)
+    w = [g[j] for j in range(parts)] + [early] + [chan_move(g[j], 1) for j in LATE]
+    for k in range(1, CALLS):
+        to_near, to_far = other_rows(k, after(tokens, g[4]))
+        xs.append((chan_move(to_near, 2), chan_move(to_far, 3)))
+
+    acc = hid = grad = None
+    moved = []
+    for k in range(CALLS):
+        out = layer(
+            k, CALLS, rows, parts, C, n, tokens, sib, cotangent, scot, ids, biases, xs[k], w, acc, hid
+        )
+        if k == 0:
+            w = out[-1]
+        hid, to_sib, d_px, d_pd, own, acc = out[:6]
+        if k == CALLS - 1:
+            got = [v for m in moved for v in m[1:]]
+            to_sib, d_px, d_pd, acc_sib = lax.optimization_barrier((to_sib, d_px, d_pd, out[6], *got))[:4]
+            acc_sib = chan_move(acc_sib, 1)
+        else:
+            to_sib, d_px, d_pd = lax.optimization_barrier((to_sib, d_px, d_pd, *xs[k + 1]))[:3]
+        moved.append((own, chan_move(d_px, 2), chan_move(to_sib, 1), chan_move(d_pd, 3)))
+
+    def end(k, mine, *others):
+        nonlocal grad, hid
+        own, from_px, from_sib, from_pd = moved[k]
+        if mine:
+            (grad,) = finish(k, rows, True, C, n, total, after(own, *others), from_px, grad)
+        else:
+            grad, hid = finish(k, rows, False, C, n, total, after(from_sib, *others), from_pd, grad, hid)
+
+    for k in range(CALLS - 1):
+        end(k, True)
+        end(k, False)
+    s7, s3, s5, s2, kept = split(C, after(acc, grad), acc_sib)
+    r7, r3, r5 = dp_move(s7, 1), dp_move(s3, 2), dp_move(s5, 1)
+    s6, s1, k4 = second(C, kept, r7, r3, r5)
+    r6, r1, r2 = dp_move(s6, 2), dp_move(s1, 1), dp_move(s2, 2)
+    s4 = third(C, k4, r6)
+    r4 = dp_move(s4, 4)
+    end(CALLS - 1, True, s4)
+    weight_grad, bias_grad = total_sum(C, kept, r2, r1, r4)
+    end(CALLS - 1, False, weight_grad)
+    return (hid, grad, weight_grad, bias_grad)
 
 
 def combine(earlier, later):
     return (earlier[0] * later[0], later[0] * earlier[1] + later[1])
 
 
-def local(tokens, weights, bias, segment_ids, cotangent):
+def local_any(tokens, weights, bias, segment_ids, cotangent):
     width_part, total_rows = tokens.shape
     batch_rows = total_rows // MICRO
     grad_shard = jnp.zeros(weights.shape, jnp.float32)
@@ -48,9 +786,7 @@
         cell = lax.associative_scan(combine, (decay, source), axis=1)[1]
         hidden_parts.append((output_gate * cell).astype(jnp.bfloat16))
         decay_next = jnp.concatenate([decay[:, 1:], jnp.zeros((width_part, 1), jnp.float32)], 1)
-        dcell = lax.associative_scan(
-            combine, (decay_next, cot * output_gate), reverse=True, axis=1
-        )[1]
+        dcell = lax.associative_scan(combine, (decay_next, cot * output_gate), reverse=True, axis=1)[1]
         cell_before = (
             jnp.concatenate([jnp.zeros((width_part, 1), jnp.float32), cell[:, :-1]], 1)
             * carry_on[None, :]
@@ -75,9 +811,7 @@
         input_parts.append(
             lax.psum_scatter(term, "chan", scatter_dimension=0, tiled=True).astype(jnp.bfloat16)
         )
-        grad_shard = grad_shard + lax.psum_scatter(
-            weight_term, "dp", scatter_dimension=2, tiled=True
-        )
+        grad_shard = grad_shard + lax.psum_scatter(weight_term, "dp", scatter_dimension=2, tiled=True)
     bias_grad = lax.psum(bias_total, "dp")
     hidden = jnp.concatenate(hidden_parts, 1)
     input_grad = jnp.concatenate(input_parts, 1)
@@ -85,6 +819,19 @@
 
 
 def solution(mesh):
+    chan, parts = mesh.shape["chan"], mesh.shape["dp"]
     in_specs = (P("chan", "dp"), P(None, "chan", "dp"), P(None, "chan"), P("dp"), P("chan", "dp"))
     out_specs = (P("chan", "dp"), P("chan", "dp"), P(None, "chan", "dp"), P(None, "chan"))
-    return jax.shard_map(local, mesh=mesh, in_specs=in_specs, out_specs=out_specs, check_vma=False)
+
+    def run(tokens, weights, bias, segment_ids, cotangent):
+        C = tokens.shape[0] // chan
+        row_part = weights.shape[2] // parts
+        pairs = tokens.shape[1] // parts % (2 * LEN * CALLS) == 0
+        tail = C - LANES
+        fits = chan == 4 and parts == 8 and row_part == C and pairs and 0 < 3 * tail < LANES and tail % 32 == 0
+        body = functools.partial(local, chan, parts) if fits else local_any
+        return jax.shard_map(body, mesh=mesh, in_specs=in_specs, out_specs=out_specs, check_vma=False)(
+            tokens, weights, bias, segment_ids, cotangent
+        )
+
+    return run

time: 4490 us -> 181 us (0.04)
  local copies, waits for them, and re-layouts: 3790 us -> 5.01 us
  other arithmetic: 295 us -> 1.88 us
  waiting for transfers between devices: 289 us -> 42.1 us
  Pallas kernels: 0 us -> 101 us
    slice x527 -> x0, local copies, waits for them, and re-layouts: 2810 us -> none  [the longest x264 1410 us: local(): lax.associative_scan(combine, (decay_next, cot * output_gate), reverse=Tr...]
    pad x160 -> x0, local copies, waits for them, and re-layouts: 779 us -> none  [the longest x80 402 us: local(): cell = lax.associative_scan(combine, (decay, source), axis=1)[1]]
    unnamed x15 -> x0, waiting for transfers between devices: 193 us -> none
    mul x80 -> x0, other arithmetic: 134 us -> none  [the longest x72 112 us: combine(): return (earlier[0] * later[0], later[0] * earlier[1] + later[1])]
    unnamed x602 -> x50, local copies, waits for them, and re-layouts: 129 us -> 5.01 us
    add x181 -> x0, other arithmetic: 107 us -> none  [the longest x88 57.8 us: combine(): return (earlier[0] * later[0], later[0] * earlier[1] + later[1])]
    pallas_call x0 -> x13, Pallas kernels: none -> 101 us  [the longest x2 76.6 us: layer(): pl.pallas_call(functools.partial(layer_kernel, k, calls, rows, parts, C,...]
    all_gather x5 -> x0, waiting for transfers between devices: 96.5 us -> none  [the longest x1 50.5 us: local(): lax.all_gather(weights, 'dp', axis=2, tiled=True)]
  transfers between devices with their start and end apart: 10 -> 33, of which waited for: 7 -> 13; matrix products, arithmetic and copies ran while one was open for 41% -> 1% of each run, Pallas kernels for 0% -> 54%
where the time goes in v2:
time: 181 us; the launch traced here: 180 us
  Pallas kernels  101 us (56%)
  waiting for transfers between devices  42.1 us (23%)
  starting transfers between devices  29.3 us (16%)
  local copies, waits for them, and re-layouts  5.01 us (3%)
  other arithmetic  1.88 us (1%)
    pallas_call x2, Pallas kernels, layer(): pl.pallas_call(functools.partial(layer_kernel, k, calls, rows, parts, C,...  76.6 us
    ppermute x14, waiting for transfers between devices, dp_move(): return lax.ppermute(v, 'dp', [(i, i ^ j) for i in range(parts)])  34.9 us
    ppermute x14, starting transfers between devices, dp_move(): return lax.ppermute(v, 'dp', [(i, i ^ j) for i in range(parts)])  20 us
    pallas_call x4, Pallas kernels, finish(): pl.pallas_call(functools.partial(finish_kernel, k, rows, mine, C, n), out...  9.75 us
    ppermute x19, starting transfers between devices, chan_move(): return lax.ppermute(v, 'chan', [(i, i ^ j) for i in range(chan)])  9.34 us
    ppermute x19, waiting for transfers between devices, chan_move(): return lax.ppermute(v, 'chan', [(i, i ^ j) for i in range(chan)])  7.18 us
    unnamed x50, local copies, waits for them, and re-layouts  5.01 us
    pallas_call x2, Pallas kernels, take_rows(): pl.pallas_call(functools.partial(take_kernel, picks, n), out_shape=[jax.S...  4.36 us
  transfers between devices with their start and end apart: 33, of which 13 were waited for; matrix products, arithmetic and copies ran while one was open for 1% of the time, Pallas kernels for 54%

profile of v2, /device:TPU:0, one launch (start us, length us, event | category | flops | bytes accessed | tf_op | source)
XLA Modules:
  0.0 180.1 jit_solution(16082687957961546177)
XLA Ops:
  1.2 2.2 %take.2 = (bf16[160,2048]{1,0:T(8,128)(2,1)}, bf16[160,2048]{1,0:T(8,128)(2,1)}) custom-call(bf16[160,8192]{1,0:T(8,128)(2,1)} %refs_0_.3), custom_call_target="tpu_custom_call" | custom-call | flops 1 | bytes 1 | tf_op jit(solution)/shard_map/take/pallas_call | solution.py:476
  3.4 1.8 pack.1
  5.2 3.0 %collective-permute-start.9 = (bf16[160,512]{1,0:T(8,128)(2,1)}, bf16[160,512]{1,0:T(8,128)(2,1)S(1)}, u32[]{:S(2)}, u32[]{:S(2)}) collective-permute-start(bf16[160,512]{1,0:T(8,128)(2,1)} %get-tuple-element.57.refs_9_), channel_id=1, source_target_pairs={{0,8},{4,12},{8,0},{12,4},{16,24},{20,28},{24,16},{28,20},{1,9},{5... | collective-permute-start | bytes 491528 | tf_op jit(solution)/shard_map/ppermute | solution.py:679
  12.9 2.8 %collective-permute-start.2 = (bf16[160,512]{1,0:T(8,128)(2,1)}, bf16[160,512]{1,0:T(8,128)(2,1)}, u32[]{:S(2)}, u32[]{:S(2)}) collective-permute-start(bf16[160,512]{1,0:T(8,128)(2,1)} %get-tuple-element.57.refs_9_), channel_id=1, source_target_pairs={{0,16},{4,20},{8,24},{12,28},{16,0},{20,4},{24,8},{28,12},{1,17},{... | collective-permute-start | bytes 491528 | tf_op jit(solution)/shard_map/ppermute | solution.py:679
  15.7 7.6 %collective-permute-done.2.refs_13_ = bf16[160,512]{1,0:T(8,128)(2,1)} collective-permute-done((bf16[160,512]{1,0:T(8,128)(2,1)}, bf16[160,512]{1,0:T(8,128)(2,1)}, u32[]{:S(2)}, u32[]{:S(2)}) %collective-permute-start.2) | collective-permute-done | bytes 163872 | tf_op jit(solution)/shard_map/ppermute | solution.py:679
  23.3 1.9 %pad_maximum_fusion = bf16[640,512]{1,0:T(8,128)(2,1)} fusion(bf16[160,512]{1,0:T(8,128)(2,1)} %collective-permute-done.2.refs_13_, bf16[160,512]{1,0:T(8,128)(2,1)S(1)} %collective-permute-done.9.refs_11_, bf16[160,512]{1,0:T(8,128)(2,1)S(1)} %collective-permute-done.8.refs_10_, bf16[160,512]{1,0:T(8,128)(2,1)} %get-tuple-element.57.refs_9_), kind=kLoop, calls=%fused_computation | loop fusion | flops 2621440 | bytes 1310720 | tf_op jit(solution)/shard_map/concatenate | solution.py:700
  28.0 2.2 %take.3 = (bf16[160,2048]{1,0:T(8,128)(2,1)}, bf16[160,2048]{1,0:T(8,128)(2,1)}) custom-call(bf16[160,8192]{1,0:T(8,128)(2,1)} %refs_0_.3), custom_call_target="tpu_custom_call" | custom-call | flops 1 | bytes 1 | tf_op jit(solution)/shard_map/take/pallas_call | solution.py:476
  31.7 2.3 %collective-permute-done.12.refs_15_ = bf16[160,512]{1,0:T(8,128)(2,1)} collective-permute-done((bf16[160,512]{1,0:T(8,128)(2,1)}, bf16[160,512]{1,0:T(8,128)(2,1)}, u32[]{:S(2)}, u32[]{:S(2)}) %collective-permute-start.12) | collective-permute-done | bytes 163872 | tf_op jit(solution)/shard_map/ppermute | solution.py:679
  34.5 4.7 %collective-permute-done.7.refs_8_ = bf16[160,2048]{1,0:T(8,128)(2,1)} collective-permute-done((bf16[160,2048]{1,0:T(8,128)(2,1)}, bf16[160,2048]{1,0:T(8,128)(2,1)}, u32[]{:S(2)}, u32[]{:S(2)}) %collective-permute-start.7) | collective-permute-done | bytes 655392 | tf_op jit(solution)/shard_map/ppermute | solution.py:676
  41.8 4.7 %collective-permute-done.11.refs_14_ = bf16[160,512]{1,0:T(8,128)(2,1)S(1)} collective-permute-done((bf16[160,512]{1,0:T(8,128)(2,1)}, bf16[160,512]{1,0:T(8,128)(2,1)S(1)}, u32[]{:S(2)}, u32[]{:S(2)}) %collective-permute-start.11) | collective-permute-done | bytes 163872 | tf_op jit(solution)/shard_map/ppermute | solution.py:679
  47.0 2.8 %collective-permute-done.13.refs_16_ = bf16[160,512]{1,0:T(8,128)(2,1)S(1)} collective-permute-done((bf16[160,512]{1,0:T(8,128)(2,1)}, bf16[160,512]{1,0:T(8,128)(2,1)S(1)}, u32[]{:S(2)}, u32[]{:S(2)}) %collective-permute-start.13) | collective-permute-done | bytes 163872 | tf_op jit(solution)/shard_map/ppermute | solution.py:679
  52.0 38.2 %layer.2 = (bf16[160,8192]{1,0:T(8,128)(2,1)}, bf16[320,2048]{1,0:T(8,128)(2,1)}, bf16[160,2048]{1,0:T(8,128)(2,1)}, bf16[160,2048]{1,0:T(8,128)(2,1)}, bf16[160...) custom-call(bf16[160,8192]{1,0:T(8,128)(2,1)} %refs_0_.3, bf16[160,8192]{1,0:T(8,128)(2,1)} %copy-done.2, ...), custom_call_target="tpu_custom_call" | custom-call | flops 1 | bytes 1 | tf_op jit(solution)/shard_map/layer/pallas_call | solution.py:443
  92.1 38.4 %layer.3 = (bf16[160,8192]{1,0:T(8,128)(2,1)}, bf16[320,2048]{1,0:T(8,128)(2,1)}, bf16[160,2048]{1,0:T(8,128)(2,1)}, bf16[160,2048]{1,0:T(8,128)(2,1)}, bf16[160...) custom-call(bf16[160,8192]{1,0:T(8,128)(2,1)} %refs_0_.3, ...), custom_call_target="tpu_custom_call", output_to_operand_aliasing={{0}: (11, {})} | custom-call | flops 1 | bytes 1 | tf_op jit(solution)/shard_map/layer/pallas_call | solution.py:443
  132.7 2.2 %finish.4.refs_0_ = bf16[160,8192]{1,0:T(8,128)(2,1)} custom-call(bf16[160,2048]{1,0:T(8,128)(2,1)} %get-tuple-element.81.near, bf16[160,2048]{1,0:T(8,128)(2,1)} %copy-done.9), custom_call_target="tpu_custom_call" | custom-call | flops 1 | bytes 1 | tf_op jit(solution)/shard_map/finish/pallas_call | solution.py:553
  134.9 2.7 %finish.5 = (bf16[160,8192]{1,0:T(8,128)(2,1)}, bf16[160,8192]{1,0:T(8,128)(2,1)}) custom-call(bf16[320,2048]{1,0:T(8,128)(2,1)} %collective-permute-done.20.near, bf16[160,2048]{1,0:T(8,128)(2,1)} %copy-done.8, bf16[160,8192]{1,0:T(8,128)(2,1)} %finish.4.refs_0_, ...), custom_call_target="tpu_custom_call", output_to_operand_aliasing={{0}: (2, {}), {1}: (3, {})} | custom-call | flops 1 | bytes 1 | tf_op jit(solution)/shard_map/finish/pallas_call | solution.py:553
  142.7 3.8 %collective-permute-done.25.r7 = bf16[176,512]{1,0:T(8,128)(2,1)S(1)} collective-permute-done((bf16[176,512]{1,0:T(8,128)(2,1)S(1)}, bf16[176,512]{1,0:T(8,128)(2,1)S(1)}, u32[]{:S(2)}, u32[]{:S(2)}) %collective-permute-start.25) | collective-permute-done | bytes 180256 | tf_op jit(solution)/shard_map/ppermute | solution.py:679
  149.7 2.4 %collective-permute-done.27.r5 = bf16[176,512]{1,0:T(8,128)(2,1)S(1)} collective-permute-done((bf16[176,512]{1,0:T(8,128)(2,1)S(1)}, bf16[176,512]{1,0:T(8,128)(2,1)S(1)}, u32[]{:S(2)}, u32[]{:S(2)}) %collective-permute-start.27) | collective-permute-done | bytes 180256 | tf_op jit(solution)/shard_map/ppermute | solution.py:679
  152.7 2.4 %second.1 = (bf16[176,512]{1,0:T(8,128)(2,1)}, bf16[176,512]{1,0:T(8,128)(2,1)}, f32[176,512]{1,0:T(8,128)}) custom-call(f32[4,176,512]{2,1,0:T(8,128)} %copy-done, bf16[176,512]{1,0:T(8,128)(2,1)} %copy-done.13, bf16[176,512]{1,0:T(8,128)(2,1)} %copy-done.15, bf16[176,512]{1,0:T(8,128)(2,1)} %copy-done.16), custom_call_target="tpu_custom_call" | custom-call | flops 1 | bytes 1 | tf_op jit(solution)/shard_map/second/pallas_call | solution.py:617
  157.1 4.5 %collective-permute-done.29.r6 = bf16[176,512]{1,0:T(8,128)(2,1)S(1)} collective-permute-done((bf16[176,512]{1,0:T(8,128)(2,1)}, bf16[176,512]{1,0:T(8,128)(2,1)S(1)}, u32[]{:S(2)}, u32[]{:S(2)}) %collective-permute-start.29) | collective-permute-done | bytes 180256 | tf_op jit(solution)/shard_map/ppermute | solution.py:679
  165.0 2.6 %collective-permute-start.30 = (bf16[176,512]{1,0:T(8,128)(2,1)}, bf16[176,512]{1,0:T(8,128)(2,1)S(1)}, u32[]{:S(2)}, u32[]{:S(2)}) collective-permute-start(bf16[176,512]{1,0:T(8,128)(2,1)} %third.1), channel_id=1, source_target_pairs={{0,16},{4,20},{8,24},{12,28},{16,0},{20,4},{24,8},{28,12},{1,17},{... | collective-permute-start | bytes 540680 | tf_op jit(solution)/shard_map/ppermute | solution.py:679
  167.5 2.2 %finish.6.refs_0_ = bf16[160,8192]{1,0:T(8,128)(2,1)} custom-call(bf16[160,2048]{1,0:T(8,128)(2,1)} %get-tuple-element.98.near, bf16[160,2048]{1,0:T(8,128)(2,1)} %copy-done.7, bf16[160,8192]{1,0:T(8,128)(2,1)} %get-tuple-element.83.refs_0_), custom_call_target="tpu_custom_call", output_to_operand_aliasing={{}: (2, {})} | custom-call | flops 1 | bytes 1 | tf_op jit(solution)/shard_map/finish/pallas_call | solution.py:553
  169.8 3.6 %collective-permute-done.30.r4 = bf16[176,512]{1,0:T(8,128)(2,1)S(1)} collective-permute-done((bf16[176,512]{1,0:T(8,128)(2,1)}, bf16[176,512]{1,0:T(8,128)(2,1)S(1)}, u32[]{:S(2)}, u32[]{:S(2)}) %collective-permute-start.30) | collective-permute-done | bytes 180256 | tf_op jit(solution)/shard_map/ppermute | solution.py:679
  174.0 2.5 %total.1 = (f32[3,160,160]{2,1,0:T(8,128)}, f32[3,160]{1,0:T(4,128)}) custom-call(f32[4,176,512]{2,1,0:T(8,128)} %copy-done, bf16[176,512]{1,0:T(8,128)(2,1)} %copy-done.11, bf16[176,512]{1,0:T(8,128)(2,1)} %copy-done.12, bf16[176,512]{1,0:T(8,128)(2,1)} %copy-done.14), custom_call_target="tpu_custom_call" | custom-call | flops 1 | bytes 1 | tf_op jit(solution)/shard_map/total/pallas_call | solution.py:657
  177.4 2.6 %finish.7 = (bf16[160,8192]{1,0:T(8,128)(2,1)}, bf16[160,8192]{1,0:T(8,128)(2,1)}) custom-call(bf16[320,2048]{1,0:T(8,128)(2,1)} %collective-permute-done.22.near, bf16[160,2048]{1,0:T(8,128)(2,1)} %copy-done.6, bf16[160,8192]{1,0:T(8,128)(2,1)} %finish.6.refs_0_, ...), custom_call_target="tpu_custom_call", output_to_operand_aliasing={{0}: (2, {}), {1}: (3, {})} | custom-call | flops 1 | bytes 1 | tf_op jit(solution)/shard_map/finish/pallas_call | solution.py:553
  (106 shorter events, 35.0 us)
Async XLA Ops:
  0.6 24.5 %collective-permute-start = (bf16[160,8192]{1,0:T(8,128)(2,1)}, bf16[160,8192]{1,0:T(8,128)(2,1)S(1)}, u32[]{:S(2)}, u32[]{:S(2)}) collective-permute-start(bf16[160,8192]{1,0:T(8,128)(2,1)} %refs_0_.3), channel_id=1, source_target_pairs={{0,1},{1,0},{2,3},{3,2},{4,5},{5,4},{6,7},{7,6},{8,9},{9,8},{10,11... | collective-permute-start | bytes 7864328 | tf_op jit(solution)/shard_map/ppermute | solution.py:676
  1.1 30.6 %collective-permute-start.1 = (bf16[160,8192]{1,0:T(8,128)(2,1)}, bf16[160,8192]{1,0:T(8,128)(2,1)}, u32[]{:S(2)}, u32[]{:S(2)}) collective-permute-start(bf16[160,8192]{1,0:T(8,128)(2,1)} %refs_2_.3), channel_id=1, source_target_pairs={{0,1},{1,0},{2,3},{3,2},{4,5},{5,4},{6,7},{7,6},{8,9},{9,8},{10,11... | collective-permute-start | bytes 7864328 | tf_op jit(solution)/shard_map/ppermute | solution.py:676
  5.2 7.7 %collective-permute-start.9 = (bf16[160,512]{1,0:T(8,128)(2,1)}, bf16[160,512]{1,0:T(8,128)(2,1)S(1)}, u32[]{:S(2)}, u32[]{:S(2)}) collective-permute-start(bf16[160,512]{1,0:T(8,128)(2,1)} %get-tuple-element.57.refs_9_), channel_id=1, source_target_pairs={{0,8},{4,12},{8,0},{12,4},{16,24},{20,28},{24,16},{28,20},{1,9},{5... | collective-permute-start | bytes 491528 | tf_op jit(solution)/shard_map/ppermute | solution.py:679
  8.2 21.9 %collective-permute-start.6 = (bf16[160,2048]{1,0:T(8,128)(2,1)}, bf16[160,2048]{1,0:T(8,128)(2,1)S(1)}, u32[]{:S(2)}, u32[]{:S(2)}) collective-permute-start(bf16[160,2048]{1,0:T(8,128)(2,1)} %get-tuple-element.54), channel_id=1, source_target_pairs={{0,2},{1,3},{2,0},{3,1},{4,6},{5,7},{6,4},{7,5},{8,10},{9,11},{10,... | collective-permute-start | bytes 1966088 | tf_op jit(solution)/shard_map/ppermute | solution.py:676
  12.9 10.4 %collective-permute-start.2 = (bf16[160,512]{1,0:T(8,128)(2,1)}, bf16[160,512]{1,0:T(8,128)(2,1)}, u32[]{:S(2)}, u32[]{:S(2)}) collective-permute-start(bf16[160,512]{1,0:T(8,128)(2,1)} %get-tuple-element.57.refs_9_), channel_id=1, source_target_pairs={{0,16},{4,20},{8,24},{12,28},{16,0},{20,4},{24,8},{28,12},{1,17},{... | collective-permute-start | bytes 491528 | tf_op jit(solution)/shard_map/ppermute | solution.py:679
  15.6 23.6 %collective-permute-start.7 = (bf16[160,2048]{1,0:T(8,128)(2,1)}, bf16[160,2048]{1,0:T(8,128)(2,1)}, u32[]{:S(2)}, u32[]{:S(2)}) collective-permute-start(bf16[160,2048]{1,0:T(8,128)(2,1)} %get-tuple-element.62), channel_id=1, source_target_pairs={{0,3},{1,2},{2,1},{3,0},{4,7},{5,6},{6,5},{7,4},{8,11},{9,10},{10,... | collective-permute-start | bytes 1966088 | tf_op jit(solution)/shard_map/ppermute | solution.py:676
  25.1 16.1 %collective-permute-start.14 = (bf16[640,512]{1,0:T(8,128)(2,1)}, bf16[640,512]{1,0:T(8,128)(2,1)}, u32[]{:S(2)}, u32[]{:S(2)}) collective-permute-start(bf16[640,512]{1,0:T(8,128)(2,1)} %pad_maximum_fusion), channel_id=1, source_target_pairs={{0,1},{1,0},{2,3},{3,2},{4,5},{5,4},{6,7},{7,6},{8,9},{9,8},{10,11... | collective-permute-start | bytes 1966088 | tf_op jit(solution)/shard_map/ppermute | solution.py:676
  30.2 60.0 %collective-permute-start.4 = (bf16[160,2048]{1,0:T(8,128)(2,1)}, bf16[160,2048]{1,0:T(8,128)(2,1)}, u32[]{:S(2)}, u32[]{:S(2)}) collective-permute-start(bf16[160,2048]{1,0:T(8,128)(2,1)} %get-tuple-element.60), channel_id=1, source_target_pairs={{0,2},{1,3},{2,0},{3,1},{4,6},{5,7},{6,4},{7,5},{8,10},{9,11},{10,... | collective-permute-start | bytes 1966088 | tf_op jit(solution)/shard_map/ppermute | solution.py:676
  31.7 58.5 %collective-permute-start.5 = (bf16[160,2048]{1,0:T(8,128)(2,1)}, bf16[160,2048]{1,0:T(8,128)(2,1)}, u32[]{:S(2)}, u32[]{:S(2)}) collective-permute-start(bf16[160,2048]{1,0:T(8,128)(2,1)} %get-tuple-element.61), channel_id=1, source_target_pairs={{0,3},{1,2},{2,1},{3,0},{4,7},{5,6},{6,5},{7,4},{8,11},{9,10},{10,... | collective-permute-start | bytes 1966088 | tf_op jit(solution)/shard_map/ppermute | solution.py:676
  34.0 6.7 %collective-permute-start.10 = (bf16[160,512]{1,0:T(8,128)(2,1)}, bf16[160,512]{1,0:T(8,128)(2,1)S(1)}, u32[]{:S(2)}, u32[]{:S(2)}) collective-permute-start(bf16[160,512]{1,0:T(8,128)(2,1)} %copy-done.5), channel_id=1, source_target_pairs={{0,8},{4,12},{8,0},{12,4},{16,24},{20,28},{24,16},{28,20},{1,9},{5... | collective-permute-start | bytes 491528 | tf_op jit(solution)/shard_map/ppermute | solution.py:679
  39.2 7.3 %collective-permute-start.11 = (bf16[160,512]{1,0:T(8,128)(2,1)}, bf16[160,512]{1,0:T(8,128)(2,1)S(1)}, u32[]{:S(2)}, u32[]{:S(2)}) collective-permute-start(bf16[160,512]{1,0:T(8,128)(2,1)} %collective-permute-done.2.refs_13_), channel_id=1, source_target_pairs={{0,4},{4,0},{8,12},{12,8},{16,20},{20,16},{24,28},{28,24},{1,5},{5... | collective-permute-start | bytes 491528 | tf_op jit(solution)/shard_map/ppermute | solution.py:679
  41.3 8.6 %collective-permute-start.13 = (bf16[160,512]{1,0:T(8,128)(2,1)}, bf16[160,512]{1,0:T(8,128)(2,1)S(1)}, u32[]{:S(2)}, u32[]{:S(2)}) collective-permute-start(bf16[160,512]{1,0:T(8,128)(2,1)} %collective-permute-done.12.refs_15_), channel_id=1, source_target_pairs={{0,4},{4,0},{8,12},{12,8},{16,20},{20,16},{24,28},{28,24},{1,5},{5... | collective-permute-start | bytes 491528 | tf_op jit(solution)/shard_map/ppermute | solution.py:679
  90.2 40.4 %collective-permute-start.20 = (bf16[320,2048]{1,0:T(8,128)(2,1)}, bf16[320,2048]{1,0:T(8,128)(2,1)}, u32[]{:S(2)}, u32[]{:S(2)}) collective-permute-start(bf16[320,2048]{1,0:T(8,128)(2,1)} %get-tuple-element.77), channel_id=1, source_target_pairs={{0,1},{1,0},{2,3},{3,2},{4,5},{5,4},{6,7},{7,6},{8,9},{9,8},{10,11... | collective-permute-start | bytes 3932168 | tf_op jit(solution)/shard_map/ppermute | solution.py:676
  90.4 40.2 %collective-permute-start.19 = (bf16[160,2048]{1,0:T(8,128)(2,1)}, bf16[160,2048]{1,0:T(8,128)(2,1)S(1)}, u32[]{:S(2)}, u32[]{:S(2)}) collective-permute-start(bf16[160,2048]{1,0:T(8,128)(2,1)} %get-tuple-element.76), channel_id=1, source_target_pairs={{0,2},{1,3},{2,0},{3,1},{4,6},{5,7},{6,4},{7,5},{8,10},{9,11},{10,... | collective-permute-start | bytes 1966088 | tf_op jit(solution)/shard_map/ppermute | solution.py:676
  91.2 39.4 %collective-permute-start.21 = (bf16[160,2048]{1,0:T(8,128)(2,1)}, bf16[160,2048]{1,0:T(8,128)(2,1)S(1)}, u32[]{:S(2)}, u32[]{:S(2)}) collective-permute-start(bf16[160,2048]{1,0:T(8,128)(2,1)} %get-tuple-element.78), channel_id=1, source_target_pairs={{0,3},{1,2},{2,1},{3,0},{4,7},{5,6},{6,5},{7,4},{8,11},{9,10},{10,... | collective-permute-start | bytes 1966088 | tf_op jit(solution)/shard_map/ppermute | solution.py:676
  130.6 7.0 %collective-permute-start.23 = (bf16[1296,512]{1,0:T(8,128)(2,1)}, bf16[1296,512]{1,0:T(8,128)(2,1)}, u32[]{:S(2)}, u32[]{:S(2)}) collective-permute-start(bf16[1296,512]{1,0:T(8,128)(2,1)} %get-tuple-element.85), channel_id=1, source_target_pairs={{0,1},{1,0},{2,3},{3,2},{4,5},{5,4},{6,7},{7,6},{8,9},{9,8},{10,11... | collective-permute-start | bytes 3981320 | tf_op jit(solution)/shard_map/ppermute | solution.py:676
  131.5 45.0 %collective-permute-start.22 = (bf16[320,2048]{1,0:T(8,128)(2,1)}, bf16[320,2048]{1,0:T(8,128)(2,1)}, u32[]{:S(2)}, u32[]{:S(2)}) collective-permute-start(bf16[320,2048]{1,0:T(8,128)(2,1)} %get-tuple-element.79), channel_id=1, source_target_pairs={{0,1},{1,0},{2,3},{3,2},{4,5},{5,4},{6,7},{7,6},{8,9},{9,8},{10,11... | collective-permute-start | bytes 3932168 | tf_op jit(solution)/shard_map/ppermute | solution.py:676
  131.9 33.0 %collective-permute-start.32 = (bf16[160,2048]{1,0:T(8,128)(2,1)}, bf16[160,2048]{1,0:T(8,128)(2,1)S(1)}, u32[]{:S(2)}, u32[]{:S(2)}) collective-permute-start(bf16[160,2048]{1,0:T(8,128)(2,1)} %get-tuple-element.99), channel_id=1, source_target_pairs={{0,2},{1,3},{2,0},{3,1},{4,6},{5,7},{6,4},{7,5},{8,10},{9,11},{10,... | collective-permute-start | bytes 1966088 | tf_op jit(solution)/shard_map/ppermute | solution.py:676
  141.9 34.6 %collective-permute-start.31 = (bf16[160,2048]{1,0:T(8,128)(2,1)}, bf16[160,2048]{1,0:T(8,128)(2,1)S(1)}, u32[]{:S(2)}, u32[]{:S(2)}) collective-permute-start(bf16[160,2048]{1,0:T(8,128)(2,1)} %get-tuple-element.96), channel_id=1, source_target_pairs={{0,3},{1,2},{2,1},{3,0},{4,7},{5,6},{6,5},{7,4},{8,11},{9,10},{10,... | collective-permute-start | bytes 1966088 | tf_op jit(solution)/shard_map/ppermute | solution.py:676
  142.3 7.4 %collective-permute-start.26 = (bf16[176,512]{1,0:T(8,128)(2,1)S(1)}, bf16[176,512]{1,0:T(8,128)(2,1)S(1)}, u32[]{:S(2)}, u32[]{:S(2)}) collective-permute-start(bf16[176,512]{1,0:T(8,128)(2,1)S(1)} %get-tuple-element.89), channel_id=1, source_target_pairs={{0,8},{4,12},{8,0},{12,4},{16,24},{20,28},{24,16},{28,20},{1,9},{5... | collective-permute-start | bytes 540680 | tf_op jit(solution)/shard_map/ppermute | solution.py:679
  155.1 6.6 %collective-permute-start.29 = (bf16[176,512]{1,0:T(8,128)(2,1)}, bf16[176,512]{1,0:T(8,128)(2,1)S(1)}, u32[]{:S(2)}, u32[]{:S(2)}) collective-permute-start(bf16[176,512]{1,0:T(8,128)(2,1)} %get-tuple-element.93), channel_id=1, source_target_pairs={{0,8},{4,12},{8,0},{12,4},{16,24},{20,28},{24,16},{28,20},{1,9},{5... | collective-permute-start | bytes 540680 | tf_op jit(solution)/shard_map/ppermute | solution.py:679
  155.4 14.4 %collective-permute-start.24 = (bf16[176,512]{1,0:T(8,128)(2,1)S(1)}, bf16[176,512]{1,0:T(8,128)(2,1)S(1)}, u32[]{:S(2)}, u32[]{:S(2)}) collective-permute-start(bf16[176,512]{1,0:T(8,128)(2,1)S(1)} %get-tuple-element.87), channel_id=1, source_target_pairs={{0,8},{4,12},{8,0},{12,4},{16,24},{20,28},{24,16},{28,20},{1,9},{5... | collective-permute-start | bytes 540680 | tf_op jit(solution)/shard_map/ppermute | solution.py:679
  161.7 8.1 %collective-permute-start.28 = (bf16[176,512]{1,0:T(8,128)(2,1)}, bf16[176,512]{1,0:T(8,128)(2,1)S(1)}, u32[]{:S(2)}, u32[]{:S(2)}) collective-permute-start(bf16[176,512]{1,0:T(8,128)(2,1)} %get-tuple-element.91), channel_id=1, source_target_pairs={{0,4},{4,0},{8,12},{12,8},{16,20},{20,16},{24,28},{28,24},{1,5},{5... | collective-permute-start | bytes 540680 | tf_op jit(solution)/shard_map/ppermute | solution.py:679
  165.0 8.4 %collective-permute-start.30 = (bf16[176,512]{1,0:T(8,128)(2,1)}, bf16[176,512]{1,0:T(8,128)(2,1)S(1)}, u32[]{:S(2)}, u32[]{:S(2)}) collective-permute-start(bf16[176,512]{1,0:T(8,128)(2,1)} %third.1), channel_id=1, source_target_pairs={{0,16},{4,20},{8,24},{12,28},{16,0},{20,4},{24,8},{28,12},{1,17},{... | collective-permute-start | bytes 540680 | tf_op jit(solution)/shard_map/ppermute | solution.py:679
  (34 other events, 215.8 us)

commit v3 on v2

--- a/solution.py
+++ b/solution.py
@@ -15,13 +15,14 @@
 TILE = 256
 UNROLL = 16
 FTILE = 1024
+TILES = LEN // TILE
 CALLS = 2
-EARLY = (0, 1, 2, 4)
-LATE = (3, 5, 6, 7)
+GROUPS = ((0, 1, 4), (2, 5, 6), (3, 7))
 f32 = jnp.float32
 bf16 = jnp.bfloat16
 ANY = pl.BlockSpec(memory_space=pl.ANY)
 VMEM = pl.BlockSpec(memory_space=pltpu.VMEM)
+HBM = pl.BlockSpec(memory_space=pltpu.HBM)
 SMEM = pl.BlockSpec(memory_space=pltpu.SMEM)
 
 
@@ -39,7 +40,7 @@
     tok, sib, cot, scot, ids, bias, bias_sib, x_near, x_far = refs[:9]
     refs = refs[9:]
     if first:
-        w_in, refs = refs[: parts + 1 + len(LATE)], refs[parts + 1 + len(LATE) :]
+        w_in, refs = refs[: parts + len(GROUPS)], refs[parts + len(GROUPS) :]
     else:
         w_in, acc_in, refs = refs[0], refs[1], refs[3:]
     hid, to_sib, dx_px, dx_pd, dx_own = refs[:5]
@@ -50,7 +51,7 @@
         acc_out, refs = refs[0], refs[1:]
     if first:
         w_out, refs = refs[0], refs[1:]
-    (xb, wb, cb, pre, zs, fs, os_, cbs, ct, hs, hb, dp, dxb, accb, ab, small, nxt, sums, cl, ca_t, id_b, bb, sem, rsem) = refs
+    (xb, wb, cb, pre, gp, zs, fs, os_, cbs, ct, hs, hb, dp, dxb, accb, ab, small, nxt, sums, cl, ca_t, id_b, bb, sem, rsem) = refs
     D = 4 * C
     tl = C - LANES
     steps = n // SEGS
@@ -122,16 +123,16 @@
         for j in range(parts):
             at = pl.ds(pl.multiple_of((place ^ j) * C, 32), C)
             w_copies.append(go(w_in[j], wb.at[at, 0:half], 8 + j))
-            if j in EARLY:
-                other = w_in[parts].at[EARLY.index(j) * C : (EARLY.index(j) + 1) * C]
-            else:
-                other = w_in[parts + 1 + LATE.index(j)]
+            which = [j in group for group in GROUPS].index(True)
+            spot = GROUPS[which].index(j)
+            other = w_in[parts + which].at[spot * C : (spot + 1) * C]
             w_copies.append(go(other, wb.at[at, half : 2 * half], 8 + parts + j))
     else:
         w_copies = [go(w_in, wb, 0)]
     b_copies = [go(bias, bb.at[:, 0:half], 1), go(bias_sib, bb.at[:, half : 2 * half], 3)]
-    for copy in c_copies(0):
-        copy.start()
+    for r in range(rows):
+        for copy in (x_copies(r) if r else []) + c_copies(r):
+            copy.start()
     sums[...] = jnp.zeros_like(sums)
     lane = lax.broadcasted_iota(jnp.int32, (SEGS, LANES), 1)
     edge = lax.broadcasted_iota(jnp.int32, (D, LANES), 1) == LANES - 1
@@ -145,7 +146,7 @@
     def now(t):
         return pl.ds(pl.multiple_of(t * SEGS, SEGS), SEGS)
 
-    def row(r, _):
+    def arrive(r):
         for copy in x_copies(r):
             copy.wait()
         seg_ids = id_b[r]
@@ -154,76 +155,163 @@
         sub = lax.broadcasted_iota(jnp.int32, (SEGS, steps), 0)
         carry = jnp.where((seg_ids == before) & ((lane > 0) | (sub > 0)), 1.0, 0.0).astype(f32)
         for s in range(SEGS):
-            cl[:, s * steps : (s + 1) * steps] = jnp.broadcast_to(carry[s : s + 1, :], (SEGS, steps))
+            cl[r, :, s * steps : (s + 1) * steps] = jnp.broadcast_to(carry[s : s + 1, :], (SEGS, steps))
         for t in range(steps):
-            ca_t[t * SEGS : (t + 1) * SEGS, :] = jnp.broadcast_to(carry[:, t : t + 1], (SEGS, LANES))
-        rb = 32
-
-        def prev_step(i, _):
-            o = pl.multiple_of(i * rb, rb)
-            v = xb[pl.ds(o, rb), span(r)].astype(f32)
-            xb[pl.ds(D + o, rb), span(r)] = (pltpu.roll(v, 1, 1) * cl[0:1, :]).astype(bf16)
-            return 0
-
-        lax.fori_loop(0, D // rb, prev_step, 0)
-
-        @pl.when(r == 0)
-        def _():
-            for copy in w_copies:
-                copy.wait()
-            for copy in b_copies:
-                copy.wait()
-            if first:
-                go(wb, w_out, 0)
-            else:
-                go(acc_in, accb, 2)
-
-        for copy in c_copies(r):
-            copy.wait()
-
-        @pl.when(r + 1 < rows)
-        def _():
-            for copy in x_copies(r + 1) + c_copies(r + 1):
+            ca_t[r, t * SEGS : (t + 1) * SEGS, :] = jnp.broadcast_to(carry[:, t : t + 1], (SEGS, LANES))
+
+    rb = 32
+
+    def previous(r, i):
+        o = pl.multiple_of(i * rb, rb)
+        v = xb[pl.ds(o, rb), span(r)].astype(f32)
+        xb[pl.ds(D + o, rb), span(r)] = (pltpu.roll(v, 1, 1) * cl[r, 0:1, :]).astype(bf16)
+
+    def forward(r, i):
+        o = pl.multiple_of(r * n + i * FTILE, FTILE)
+        v = dot(xb[:, pl.ds(o, FTILE)], wb[...], 0, 0)
+        for h in range(FTILE // steps):
+            at = seg(i * (FTILE // steps) + h)
+            for q in range(8):
+                pre[q, at, :] = v[h * steps : (h + 1) * steps, q * LANES : (q + 1) * LANES]
+            c = cb[:, pl.ds(pl.multiple_of(o + h * steps, LANES), steps)].astype(f32).T
+            for q in range(3):
+                ct[q, at, :] = c[:, q * LANES : (q + 1) * LANES]
+
+    def round_tile(r, i):
+        into = pl.ds(pl.multiple_of(r * n + i * steps, LANES), steps)
+        for q in range(8):
+            v = gp[q, seg(i), :].astype(bf16)
+            dp[into, q * LANES : (q + 1) * LANES] = v
+            v = v.astype(f32)
+            a = v[0:SEGS]
+            for s in range(SEGS, steps, SEGS):
+                a = a + v[s : s + SEGS]
+            sums[:, q * LANES : (q + 1) * LANES] += a
+        for q in range(3):
+            e = LANES if q < 2 else 2 * tl
+            hb[q * LANES : q * LANES + e, into] = hs[q, seg(i), :].T.astype(bf16)[0:e]
+
+    def input_tile(r, i):
+        i = n // TILE - 1 - i
+        o = pl.multiple_of(i * TILE, TILE)
+        dj = dot(wb[...], dp[pl.ds(pl.multiple_of(r * n + o, TILE), TILE), :], 1, 1)
+        after = nxt[...]
+        for h in range(TILE // LANES - 1, -1, -1):
+            at = slice(h * LANES, (h + 1) * LANES)
+            into = pl.ds(pl.multiple_of(r * n + o + h * LANES, LANES), LANES)
+            rolled = pltpu.roll(
+                dj[D:, at] * cl[r, 0:1, pl.ds(pl.multiple_of(o + h * LANES, LANES), LANES)], LANES - 1, 1
+            )
+            dxb[:, into] = (dj[:D, at] + jnp.where(edge, after, rolled)).astype(bf16)
+            after = rolled
+        nxt[...] = after
+
+    def weight_tile(r, i, add):
+        at = pl.ds(pl.multiple_of(i * TILE, TILE), TILE)
+        v = dot(xb[:, span(r)], dp[span(r), at], 1, 0)
+        return (v + accb[0 : 2 * D, at] if add else v), at
+
+    def weight_step(r, i):
+        v, at = weight_tile(r, i, not (first and r == 0))
+        accb[0 : 2 * D, at] = v
+
+    def gates_step(r, b, t, state):
+        gain, total = state
+        v = [strided(pre, t, q) + b[q] for q in range(8)]
+        u, w = v[3], v[7]
+        tz = jnp.where(lane < tl, u, pltpu.roll(w, tl, 1))
+        tf = jnp.where(lane < tl, pltpu.roll(u, LANES - tl, 1), w)
+        to = jnp.where(lane < tl, pltpu.roll(u, LANES - 2 * tl, 1), pltpu.roll(w, LANES - tl, 1))
+        z = [jnp.tanh(g) for g in (v[0], v[4], tz)]
+        f = [sigmoid(g) for g in (v[1], v[5], tf)]
+        o = [sigmoid(g) for g in (v[2], v[6], to)]
+        at = now(t)
+        ca = ca_t[r, at, :]
+        gains, totals = [], []
+        for q in range(3):
+            zs[at, cols[q]] = z[q]
+            fs[at, cols[q]] = f[q]
+            os_[at, cols[q]] = o[q]
+            gains.append(gain[q] * (f[q] * ca))
+            totals.append(z[q] + f[q] * (ca * total[q] - z[q]))
+        return tuple(gains), tuple(totals)
+
+    def cell_step(r, t, state):
+        cell, back, gain = state
+        at = now(t)
+        ca = ca_t[r, at, :]
+        cells, backs, gains = [], [], []
+        for q in range(3):
+            z, f, o = zs[at, cols[q]], fs[at, cols[q]], os_[at, cols[q]]
+            prev = ca * cell[q]
+            cbs[at, cols[q]] = prev
+            new = z + f * (prev - z)
+            hs[q, pl.ds(t, SEGS, stride=sp), :] = o * new
+            g = jnp.where(t == 0, one, gain[q] * (f * ca))
+            cells.append(new)
+            gains.append(g)
+            backs.append(back[q] + g * (strided(ct, t, q) * o))
+        return tuple(cells), tuple(backs), tuple(gains)
+
+    def grad_step(r, i, later):
+        t = steps - 1 - i
+        at = now(t)
+        ca = ca_t[r, at, :]
+        gz, gf, go_, laters = [], [], [], []
+        for q in range(3):
+            z, f, o, prev = zs[at, cols[q]], fs[at, cols[q]], os_[at, cols[q]], cbs[at, cols[q]]
+            c = strided(ct, t, q)
+            dc = c * o + later[q]
+            laters.append((f * ca) * dc)
+            d = prev - z
+            u = dc * (1.0 - f)
+            gz.append(u * (1.0 - z * z))
+            gf.append(u * (f * d))
+            go_.append(c * (z + f * d) * (o * (1.0 - o)))
+        z, f, o = gz[2], gf[2], go_[2]
+        u = jnp.where(
+            lane < tl,
+            z,
+            jnp.where(
+                lane < 2 * tl,
+                pltpu.roll(f, tl, 1),
+                jnp.where(lane < 3 * tl, pltpu.roll(o, 2 * tl, 1), 0.0),
+            ),
+        )
+        w = jnp.where(
+            lane < tl,
+            pltpu.roll(z, LANES - tl, 1),
+            jnp.where(lane < 2 * tl, f, jnp.where(lane < 3 * tl, pltpu.roll(o, tl, 1), 0.0)),
+        )
+        for q, v in enumerate((gz[0], gf[0], go_[0], u, gz[1], gf[1], go_[1], w)):
+            gp[q, pl.ds(t, SEGS, stride=sp), :] = v
+        return tuple(laters)
+
+    def scan(step, state, beside=None):
+        if beside is None:
+            return lax.fori_loop(0, steps, step, state, unroll=UNROLL)
+        count = steps // TILES
+
+        def body(i, state):
+            beside(i)
+            for u in range(count):
+                state = step(i * count + u, state)
+            return state
+
+        return lax.fori_loop(0, TILES, body, state)
+
+    def row(r):
+        b = [jnp.broadcast_to(bb[0:1, q * LANES : (q + 1) * LANES], (SEGS, LANES)) for q in range(8)]
+        inputs = weights = None
+        if r > 0:
+            nxt[...] = jnp.zeros_like(nxt)
+            inputs, weights = functools.partial(input_tile, r - 1), functools.partial(weight_step, r - 1)
+        gain, total = scan(functools.partial(gates_step, r, b), ((one,) * 3, (zero,) * 3), inputs)
+        if r > 0:
+            for copy in grad_copies(r - 1):
                 copy.start()
-
-        b = [jnp.broadcast_to(bb[0:1, q * LANES : (q + 1) * LANES], (SEGS, LANES)) for q in range(8)]
-
-        def forward_step(i, _):
-            o = pl.multiple_of(r * n + i * FTILE, FTILE)
-            v = dot(xb[:, pl.ds(o, FTILE)], wb[...], 0, 0)
-            for h in range(FTILE // steps):
-                at = seg(i * (FTILE // steps) + h)
-                for q in range(8):
-                    pre[q, at, :] = v[h * steps : (h + 1) * steps, q * LANES : (q + 1) * LANES]
-                c = cb[:, pl.ds(pl.multiple_of(o + h * steps, LANES), steps)].astype(f32).T
-                for q in range(3):
-                    ct[q, at, :] = c[:, q * LANES : (q + 1) * LANES]
-            return 0
-
-        lax.fori_loop(0, n // FTILE, forward_step, 0)
-
-        def gates_step(t, state):
-            gain, total = state
-            v = [strided(pre, t, q) + b[q] for q in range(8)]
-            u, w = v[3], v[7]
-            tz = jnp.where(lane < tl, u, pltpu.roll(w, tl, 1))
-            tf = jnp.where(lane < tl, pltpu.roll(u, LANES - tl, 1), w)
-            to = jnp.where(lane < tl, pltpu.roll(u, LANES - 2 * tl, 1), pltpu.roll(w, LANES - tl, 1))
-            z = [jnp.tanh(g) for g in (v[0], v[4], tz)]
-            f = [sigmoid(g) for g in (v[1], v[5], tf)]
-            o = [sigmoid(g) for g in (v[2], v[6], to)]
-            at = now(t)
-            ca = ca_t[at, :]
-            gains, totals = [], []
-            for q in range(3):
-                zs[at, cols[q]] = z[q]
-                fs[at, cols[q]] = f[q]
-                os_[at, cols[q]] = o[q]
-                gains.append(gain[q] * (f[q] * ca))
-                totals.append(z[q] + f[q] * (ca * total[q] - z[q]))
-            return tuple(gains), tuple(totals)
-
-        gain, total = lax.fori_loop(0, steps, gates_step, ((one,) * 3, (zero,) * 3), unroll=UNROLL)
+            if r == 1 and not first:
+                pltpu.make_async_copy(acc_in, accb, sem.at[2]).wait()
         for q in range(3):
             small[0, :, cols[q]] = gain[q]
             small[1, :, cols[q]] = total[q]
@@ -232,111 +320,61 @@
             small[2, s : s + 1, :] = run
             run = small[0, s : s + 1, :] * run + small[1, s : s + 1, :]
         cell = tuple(small[2, :, cols[q]] for q in range(3))
-
-        def cell_step(t, state):
-            cell, back, gain = state
-            at = now(t)
-            ca = ca_t[at, :]
-            cells, backs, gains = [], [], []
-            for q in range(3):
-                z, f, o = zs[at, cols[q]], fs[at, cols[q]], os_[at, cols[q]]
-                prev = ca * cell[q]
-                cbs[at, cols[q]] = prev
-                new = z + f * (prev - z)
-                hs[q, pl.ds(t, SEGS, stride=sp), :] = o * new
-                g = jnp.where(t == 0, one, gain[q] * (f * ca))
-                cells.append(new)
-                gains.append(g)
-                backs.append(back[q] + g * (strided(ct, t, q) * o))
-            return tuple(cells), tuple(backs), tuple(gains)
-
-        cell, back, gain = lax.fori_loop(0, steps, cell_step, (cell, (zero,) * 3, (one,) * 3), unroll=UNROLL)
+        cell, back, gain = scan(functools.partial(cell_step, r), (cell, (zero,) * 3, (one,) * 3))
         for q in range(3):
             small[0, :, cols[q]] = back[q]
             small[1, :, cols[q]] = gain[q]
-            small[3, :, cols[q]] = fs[0:SEGS, cols[q]] * ca_t[0:SEGS, :]
+            small[3, :, cols[q]] = fs[0:SEGS, cols[q]] * ca_t[r, 0:SEGS, :]
         run = jnp.zeros((1, 3 * LANES), f32)
         for s in range(SEGS - 1, -1, -1):
             small[2, s : s + 1, :] = run
             run = small[3, s : s + 1, :] * (small[0, s : s + 1, :] + small[1, s : s + 1, :] * run)
         later = tuple(small[2, :, cols[q]] for q in range(3))
-
-        def grad_step(i, later):
-            t = steps - 1 - i
-            at = now(t)
-            ca = ca_t[at, :]
-            gz, gf, go_, laters = [], [], [], []
-            for q in range(3):
-                z, f, o, prev = zs[at, cols[q]], fs[at, cols[q]], os_[at, cols[q]], cbs[at, cols[q]]
-                c = strided(ct, t, q)
-                dc = c * o + later[q]
-                laters.append((f * ca) * dc)
-                d = prev - z
-                u = dc * (1.0 - f)
-                gz.append(u * (1.0 - z * z))
-                gf.append(u * (f * d))
-                go_.append(c * (z + f * d) * (o * (1.0 - o)))
-            z, f, o = gz[2], gf[2], go_[2]
-            u = jnp.where(
-                lane < tl,
-                z,
-                jnp.where(
-                    lane < 2 * tl,
-                    pltpu.roll(f, tl, 1),
-                    jnp.where(lane < 3 * tl, pltpu.roll(o, 2 * tl, 1), 0.0),
-                ),
-            )
-            w = jnp.where(
-                lane < tl,
-                pltpu.roll(z, LANES - tl, 1),
-                jnp.where(lane < 2 * tl, f, jnp.where(lane < 3 * tl, pltpu.roll(o, tl, 1), 0.0)),
-            )
-            for q, v in enumerate((gz[0], gf[0], go_[0], u, gz[1], gf[1], go_[1], w)):
-                pre[q, pl.ds(t, SEGS, stride=sp), :] = v
-            return tuple(laters)
-
-        lax.fori_loop(0, steps, grad_step, later, unroll=UNROLL)
-
-        nxt[...] = jnp.zeros_like(nxt)
-
-        def input_step(i, _):
-            i = n // TILE - 1 - i
-            o = pl.multiple_of(i * TILE, TILE)
-            for h in range(TILE // steps):
-                into = pl.ds(pl.multiple_of(r * n + o + h * steps, LANES), steps)
-                for q in range(8):
-                    v = pre[q, seg(i * (TILE // steps) + h), :].astype(bf16)
-                    dp[into, q * LANES : (q + 1) * LANES] = v
-                    v = v.astype(f32)
-                    a = v[0:SEGS]
-                    for s in range(SEGS, steps, SEGS):
-                        a = a + v[s : s + SEGS]
-                    sums[:, q * LANES : (q + 1) * LANES] += a
-                for q in range(3):
-                    e = LANES if q < 2 else 2 * tl
-                    v = hs[q, seg(i * (TILE // steps) + h), :].T.astype(bf16)
-                    hb[q * LANES : q * LANES + e, into] = v[0:e]
-            dj = dot(wb[...], dp[pl.ds(pl.multiple_of(r * n + o, TILE), TILE), :], 1, 1)
-            after = nxt[...]
-            for h in range(TILE // LANES - 1, -1, -1):
-                at = slice(h * LANES, (h + 1) * LANES)
-                into = pl.ds(pl.multiple_of(r * n + o + h * LANES, LANES), LANES)
-                rolled = pltpu.roll(
-                    dj[D:, at] * cl[0:1, pl.ds(pl.multiple_of(o + h * LANES, LANES), LANES)], LANES - 1, 1
-                )
-                dxb[:, into] = (dj[:D, at] + jnp.where(edge, after, rolled)).astype(bf16)
-                after = rolled
-            nxt[...] = after
+        scan(functools.partial(grad_step, r), later, weights)
+
+    arrive(0)
+    lax.fori_loop(0, D // rb, lambda i, _: (previous(0, i), 0)[1], 0)
+    for r in range(1, rows):
+        arrive(r)
+    for copy in w_copies + b_copies:
+        copy.wait()
+    if first:
+        go(wb, w_out, 0)
+    else:
+        go(acc_in, accb, 2)
+    for r in range(rows):
+        for copy in c_copies(r):
+            copy.wait()
+
+        def forward_step(i, _):
+            forward(r, i)
+            if r + 1 < rows:
+                for j in range(D // rb * FTILE // n):
+                    previous(r + 1, i * (D // rb * FTILE // n) + j)
+            if r > 0:
+                for j in range(FTILE // steps):
+                    round_tile(r - 1, i * (FTILE // steps) + j)
             return 0
 
-        lax.fori_loop(0, n // TILE, input_step, 0)
-        for copy in hidden_copies(r) + grad_copies(r):
-            copy.start()
+        lax.fori_loop(0, n // FTILE, forward_step, 0)
+        if r > 0:
+            for copy in hidden_copies(r - 1):
+                copy.start()
+        row(r)
+    end = rows - 1
+    nxt[...] = jnp.zeros_like(nxt)
+    if end == 0 and not first:
+        pltpu.make_async_copy(acc_in, accb, sem.at[2]).wait()
+
+    def input_step(i, _):
+        for j in range(TILE // steps):
+            round_tile(end, (TILES - 1 - i) * (TILE // steps) + j)
+        input_tile(end, i)
         return 0
 
-    lax.fori_loop(0, rows, row, 0)
-    if not first:
-        pltpu.make_async_copy(acc_in, accb, sem.at[2]).wait()
+    lax.fori_loop(0, TILES, input_step, 0)
+    for copy in hidden_copies(end) + grad_copies(end):
+        copy.start()
     for q in range(8):
         at = slice(q * LANES, (q + 1) * LANES)
         s = sums[:, at]
@@ -356,28 +394,22 @@
         at = pl.ds(pl.multiple_of(i * TILE, TILE), TILE)
         return pltpu.make_async_copy(ab.at[:, at], acc_sib.at[:, at], sem.at[2 + i])
 
-    def weight_step(i, _):
-        at = pl.ds(pl.multiple_of(i * TILE, TILE), TILE)
-        v = dot(xb[...], dp[:, at], 1, 0)
-        if not first:
-            v = v + accb[0 : 2 * D, at]
+    def own_step(i, _):
+        v, at = weight_tile(end, i, not (first and rows == 1))
         accb[0 : 2 * D, at] = v
         own_copy(i).start()
         return 0
 
-    def weight_sib_step(i, _):
-        at = pl.ds(pl.multiple_of(half + i * TILE, TILE), TILE)
-        v = dot(xb[...], dp[:, at], 1, 0)
-        if not first:
-            v = v + accb[0 : 2 * D, at]
+    def sib_step(i, _):
+        v, _ = weight_tile(end, half // TILE + i, not (first and rows == 1))
         ab[0 : 2 * D, pl.ds(pl.multiple_of(i * TILE, TILE), TILE)] = v.astype(bf16)
         sib_copy(i).start()
         return 0
 
     own_tiles = (half if last else 2 * half) // TILE
     if last:
-        lax.fori_loop(0, half // TILE, weight_sib_step, 0)
-    lax.fori_loop(0, own_tiles, weight_step, 0)
+        lax.fori_loop(0, half // TILE, sib_step, 0)
+    lax.fori_loop(0, own_tiles, own_step, 0)
     for i in range(own_tiles):
         own_copy(i).wait()
     if last:
@@ -420,6 +452,7 @@
             pltpu.VMEM((2 * D, N), bf16),
             pltpu.VMEM((w3, T), bf16),
             pltpu.VMEM((8, tall, LANES), f32),
+            pltpu.VMEM((8, tall, LANES), f32),
         ]
         + [pltpu.VMEM((n, w3), f32)] * 4
         + [pltpu.VMEM((3, tall, LANES), f32)] * 2
@@ -432,8 +465,8 @@
             pltpu.VMEM((4, SEGS, w3), f32),
             pltpu.VMEM((D, LANES), f32),
             pltpu.VMEM((SEGS, N), f32),
-            pltpu.VMEM((SEGS, n), f32),
-            pltpu.VMEM((n, LANES), f32),
+            pltpu.VMEM((rows, SEGS, n), f32),
+            pltpu.VMEM((rows, n, LANES), f32),
             pltpu.VMEM((rows, SEGS, LANES), jnp.int32),
             pltpu.VMEM((SEGS, N), f32),
             pltpu.SemaphoreType.DMA((8 + 2 * parts,)),
@@ -574,17 +607,25 @@
     return v[0:1] + v[1:2]
 
 
-def split_kernel(C, own, other, s7, s3, s5, s2, kept):
+def split_kernel(C, own, other, s7, s3, s5, s2, k0, k1, k4, k6, bufs, kept, sem):
     place = lax.axis_index("dp")
     b = own[8 * C : 8 * C + 1, :] + from_two(other[8 * C :, :])
-    for j, out in ((7, s7), (3, s3), (5, s5), (2, s2)):
+    two = in_two(b)
+    copies = []
+    for i, (j, out) in enumerate(((7, s7), (3, s3), (5, s5), (2, s2))):
         at = pl.ds(pl.multiple_of((place ^ j) * C, 32), C)
-        out[0:C] = (own[at, :] + other[at, :].astype(f32)).astype(bf16)
-        out[C:] = in_two(b)
-    for i, j in enumerate((0, 1, 4, 6)):
+        bufs[i, 0:C] = (own[at, :] + other[at, :].astype(f32)).astype(bf16)
+        bufs[i, C:] = two
+        copies.append(pltpu.make_async_copy(bufs.at[i], out, sem.at[i]))
+        copies[-1].start()
+    for i, (j, out) in enumerate(((6, k6), (1, k1), (4, k4), (0, k0))):
         at = pl.ds(pl.multiple_of((place ^ j) * C, 32), C)
         kept[i, 0:C] = own[at, :] + other[at, :].astype(f32)
-    kept[0, C : C + 8] = jnp.broadcast_to(b, (8, b.shape[1]))
+        kept[i, C : C + 8] = jnp.broadcast_to(b, (8, b.shape[1]))
+        copies.append(pltpu.make_async_copy(kept.at[i, 0 : C + 8], out, sem.at[4 + i]))
+        copies[-1].start()
+    for copy in copies:
+        copy.wait()
 
 
 def split(C, own, other):
@@ -592,76 +633,93 @@
     message = jax.ShapeDtypeStruct((C + 16, half), bf16)
     return pl.pallas_call(
         functools.partial(split_kernel, C),
-        out_shape=[message] * 4 + [jax.ShapeDtypeStruct((4, C + 16, half), f32)],
+        out_shape=[message] * 4 + [jax.ShapeDtypeStruct((C + 8, half), f32)] * 4,
         in_specs=[VMEM] * 2,
-        out_specs=[VMEM] * 5,
-        compiler_params=pltpu.CompilerParams(vmem_limit_bytes=40 << 20),
+        out_specs=[HBM] * 8,
+        scratch_shapes=[
+            pltpu.VMEM((4, C + 16, half), bf16),
+            pltpu.VMEM((4, C + 8, half), f32),
+            pltpu.SemaphoreType.DMA((8,)),
+        ],
+        compiler_params=pltpu.CompilerParams(vmem_limit_bytes=62 << 20),
         cost_estimate=pl.CostEstimate(flops=1, bytes_accessed=1, transcendentals=0),
         name="split",
     )(own, other)
 
 
-def second_kernel(C, kept, r7, r3, r5, s6, s1, k4):
-    b = kept[0, C : C + 1]
-    s6[0:C] = (kept[3, 0:C] + r7[0:C].astype(f32)).astype(bf16)
-    s6[C:] = in_two(b + from_two(r7[C:]))
-    s1[0:C] = (kept[1, 0:C] + r3[0:C].astype(f32)).astype(bf16)
-    s1[C:] = in_two(b + from_two(r3[C:]))
-    k4[0:C] = kept[2, 0:C] + r5[0:C].astype(f32)
-    k4[C : C + 8] = jnp.broadcast_to(b + from_two(r5[C:]), (8, b.shape[1]))
-
-
-def second(C, kept, r7, r3, r5):
-    half = kept.shape[2]
-    message = jax.ShapeDtypeStruct((C + 16, half), bf16)
+def second_kernel(C, k6, k1, r7, r3, s6, s1, bufs, sem):
+    b = k6[C : C + 1]
+    copies = []
+    for i, (k, r, out) in enumerate(((k6, r7, s6), (k1, r3, s1))):
+        bufs[i, 0:C] = (k[0:C] + r[0:C].astype(f32)).astype(bf16)
+        bufs[i, C:] = in_two(b + from_two(r[C:]))
+        copies.append(pltpu.make_async_copy(bufs.at[i], out, sem.at[i]))
+        copies[-1].start()
+    for copy in copies:
+        copy.wait()
+
+
+def second(C, k6, k1, r7, r3):
+    message = jax.ShapeDtypeStruct(r7.shape, bf16)
     return pl.pallas_call(
         functools.partial(second_kernel, C),
-        out_shape=[message] * 2 + [jax.ShapeDtypeStruct((C + 16, half), f32)],
+        out_shape=[message] * 2,
         in_specs=[VMEM] * 4,
-        out_specs=[VMEM] * 3,
+        out_specs=[HBM] * 2,
+        scratch_shapes=[pltpu.VMEM((2,) + r7.shape, bf16), pltpu.SemaphoreType.DMA((2,))],
         cost_estimate=pl.CostEstimate(flops=1, bytes_accessed=1, transcendentals=0),
         name="second",
-    )(kept, r7, r3, r5)
-
-
-def third_kernel(C, k4, r6, s4):
-    s4[0:C] = (k4[0:C] + r6[0:C].astype(f32)).astype(bf16)
-    s4[C:] = in_two(k4[C : C + 1] + from_two(r6[C:]))
-
-
-def third(C, k4, r6):
+    )(k6, k1, r7, r3)
+
+
+def third_kernel(C, k4, r5, r6, s4, buf, sem):
+    buf[0:C] = (k4[0:C] + r5[0:C].astype(f32) + r6[0:C].astype(f32)).astype(bf16)
+    buf[C:] = in_two(k4[C : C + 1] + from_two(r5[C:]) + from_two(r6[C:]))
+    copy = pltpu.make_async_copy(buf, s4, sem)
+    copy.start()
+    copy.wait()
+
+
+def third(C, k4, r5, r6):
     return pl.pallas_call(
         functools.partial(third_kernel, C),
         out_shape=jax.ShapeDtypeStruct(r6.shape, bf16),
-        in_specs=[VMEM] * 2,
-        out_specs=VMEM,
+        in_specs=[VMEM] * 3,
+        out_specs=HBM,
+        scratch_shapes=[pltpu.VMEM(r6.shape, bf16), pltpu.SemaphoreType.DMA],
         cost_estimate=pl.CostEstimate(flops=1, bytes_accessed=1, transcendentals=0),
         name="third",
-    )(k4, r6)
-
-
-def total_kernel(C, kept, r2, r1, r4, grad, bias):
-    v = kept[0, 0:C] + r2[0:C].astype(f32) + (r1[0:C].astype(f32) + r4[0:C].astype(f32))
+    )(k4, r5, r6)
+
+
+def total_kernel(C, k0, r2, r1, r4, grad, bias, buf, b_buf, sem):
+    v = k0[0:C] + r2[0:C].astype(f32) + (r1[0:C].astype(f32) + r4[0:C].astype(f32))
     t = v.T
     tail = C - LANES
+    b = k0[C : C + 1] + from_two(r2[C:]) + (from_two(r1[C:]) + from_two(r4[C:]))
     for g in range(3):
-        grad[g, 0:LANES] = t[g * LANES : (g + 1) * LANES]
-        grad[g, LANES:C] = t[3 * LANES + g * tail : 3 * LANES + (g + 1) * tail]
-    b = kept[0, C : C + 1] + from_two(r2[C:]) + (from_two(r1[C:]) + from_two(r4[C:]))
-    for g in range(3):
-        bias[g : g + 1, 0:LANES] = b[:, g * LANES : (g + 1) * LANES]
-        bias[g : g + 1, LANES:C] = b[:, 3 * LANES + g * tail : 3 * LANES + (g + 1) * tail]
-
-
-def total_sum(C, kept, r2, r1, r4):
+        buf[g, 0:LANES] = t[g * LANES : (g + 1) * LANES]
+        buf[g, LANES:C] = t[3 * LANES + g * tail : 3 * LANES + (g + 1) * tail]
+        b_buf[g : g + 1, 0:LANES] = b[:, g * LANES : (g + 1) * LANES]
+        b_buf[g : g + 1, LANES:C] = b[:, 3 * LANES + g * tail : 3 * LANES + (g + 1) * tail]
+    copies = [pltpu.make_async_copy(buf, grad, sem.at[0]), pltpu.make_async_copy(b_buf, bias, sem.at[1])]
+    for copy in copies:
+        copy.start()
+    for copy in copies:
+        copy.wait()
+
+
+def total_sum(C, k0, r2, r1, r4):
+    shapes = ((3, C, C), (3, C))
     return pl.pallas_call(
         functools.partial(total_kernel, C),
-        out_shape=[jax.ShapeDtypeStruct((3, C, C), f32), jax.ShapeDtypeStruct((3, C), f32)],
+        out_shape=[jax.ShapeDtypeStruct(shape, f32) for shape in shapes],
         in_specs=[VMEM] * 4,
-        out_specs=[VMEM] * 2,
+        out_specs=[HBM] * 2,
+        scratch_shapes=[pltpu.VMEM(shape, f32) for shape in shapes] + [pltpu.SemaphoreType.DMA((2,))],
         cost_estimate=pl.CostEstimate(flops=1, bytes_accessed=1, transcendentals=0),
         name="total",
-    )(kept, r2, r1, r4)
+    )(k0, r2, r1, r4)
 
 
 def local(chan, parts, tokens, weights, bias, segment_ids, cotangent):
@@ -690,19 +748,27 @@
     near, far = chan_move(to_near, 2), chan_move(to_far, 3)
     xs = [(near, far)]
     shard, b_own = pack(C, after(weights, to_near), bias)
-    g = {0: shard, 4: dp_move(shard, 4), 1: dp_move(shard, 1), 2: dp_move(shard, 2)}
     sib = chan_move(tokens, 1)
     scot = chan_move(cotangent, 1)
-    g4, g1 = lax.optimization_barrier((g[4], g[1], sib))[:2]
+    g = {0: shard, 4: dp_move(shard, 4), 1: dp_move(shard, 1)}
+    def to_sibling(group):
+        return chan_move(jnp.concatenate([g[j] for j in group], 0), 1)
+
+    g4, own = lax.optimization_barrier((g[4], shard, sib))[:2]
     g[6] = dp_move(g4, 2)
     g[5] = dp_move(g4, 1)
+    w_sib = [to_sibling(GROUPS[0])]
+    biases = [b_own, chan_move(after(b_own, g[4]), 1)]
+    g[2] = dp_move(own, 2)
+    g6, g1 = lax.optimization_barrier((g[6], g[1], near, scot))[:2]
+    g[7] = dp_move(g6, 1)
     g[3] = dp_move(g1, 2)
-    early = chan_move(jnp.concatenate([g[j] for j in EARLY], 0), 1)
-    biases = [b_own, chan_move(after(b_own, g[4]), 1)]
-    g[7] = dp_move(after(g[6], near, scot), 1)
-    w = [g[j] for j in range(parts)] + [early] + [chan_move(g[j], 1) for j in LATE]
+    w_sib.append(to_sibling(GROUPS[1]))
+    g[3] = after(g[3], far)
+    w_sib.append(to_sibling(GROUPS[2]))
+    w = [g[j] for j in range(parts)] + w_sib
     for k in range(1, CALLS):
-        to_near, to_far = other_rows(k, after(tokens, g[4]))
+        to_near, to_far = other_rows(k, after(tokens, g[6]))
         xs.append((chan_move(to_near, 2), chan_move(to_far, 3)))
 
     acc = hid = grad = None
@@ -730,18 +796,20 @@
         else:
             grad, hid = finish(k, rows, False, C, n, total, after(from_sib, *others), from_pd, grad, hid)
 
+    s7, s3, s5, s2, k0, k1, k4, k6 = split(C, acc, after(acc_sib, moved[-1][2]))
+    r7, r3 = dp_move(s7, 1), dp_move(s3, 2)
     for k in range(CALLS - 1):
-        end(k, True)
-        end(k, False)
-    s7, s3, s5, s2, kept = split(C, after(acc, grad), acc_sib)
-    r7, r3, r5 = dp_move(s7, 1), dp_move(s3, 2), dp_move(s5, 1)
-    s6, s1, k4 = second(C, kept, r7, r3, r5)
-    r6, r1, r2 = dp_move(s6, 2), dp_move(s1, 1), dp_move(s2, 2)
-    s4 = third(C, k4, r6)
+        end(k, True, s7)
+    s6, s1 = second(C, k6, k1, r7, after(r3, grad))
+    r5, r2 = dp_move(after(s5, r7), 1), dp_move(after(s2, r3), 2)
+    r6, r1 = dp_move(s6, 2), dp_move(s1, 1)
+    for k in range(CALLS - 1):
+        end(k, False, s6)
+    s4 = third(C, k4, r5, after(r6, grad, r1, r2))
     r4 = dp_move(s4, 4)
     end(CALLS - 1, True, s4)
-    weight_grad, bias_grad = total_sum(C, kept, r2, r1, r4)
-    end(CALLS - 1, False, weight_grad)
+    end(CALLS - 1, False, s4)
+    weight_grad, bias_grad = total_sum(C, k0, r2, r1, after(r4, grad))
     return (hid, grad, weight_grad, bias_grad)
 
 

time: 181 us -> 168 us (0.928)
  waiting for transfers between devices: 42.1 us -> 30.4 us
  Pallas kernels: 101 us -> 96.2 us
    ppermute x14, waiting for transfers between devices: 34.9 us -> 23 us  [dp_move(): return lax.ppermute(v, 'dp', [(i, i ^ j) for i in range(parts)])]
    pallas_call x2, Pallas kernels: 76.6 us -> 70.9 us  [layer(): pl.pallas_call(functools.partial(layer_kernel, k, calls, rows, parts, C,...]
    pallas_call x1, Pallas kernels: 1.55 us -> 3.54 us  [split(): pl.pallas_call(functools.partial(split_kernel, C), out_shape=[message] *...]
    unnamed x50 -> x44, local copies, waits for them, and re-layouts: 5.01 us -> 6.59 us
    ppermute x19 -> x17, starting transfers between devices: 9.34 us -> 9.62 us  [chan_move(): return lax.ppermute(v, 'chan', [(i, i ^ j) for i in range(chan)])]
    ppermute x19 -> x17, waiting for transfers between devices: 7.18 us -> 7.32 us  [chan_move(): return lax.ppermute(v, 'chan', [(i, i ^ j) for i in range(chan)])]
  transfers between devices with their start and end apart: 33 -> 31, of which waited for: 13 -> 12; matrix products, arithmetic and copies ran while one was open for 1% -> 1% of each run, Pallas kernels for 54% -> 54%
where the time goes in v3:
time: 168 us; the launch traced here: 167 us
  Pallas kernels  96.2 us (57%)
  starting transfers between devices  30.7 us (18%)
  waiting for transfers between devices  30.4 us (18%)
  local copies, waits for them, and re-layouts  6.59 us (4%)
  other arithmetic  2.23 us (1%)
    pallas_call x2, Pallas kernels, layer(): pl.pallas_call(functools.partial(layer_kernel, k, calls, rows, parts, C,...  70.9 us
    ppermute x14, waiting for transfers between devices, dp_move(): return lax.ppermute(v, 'dp', [(i, i ^ j) for i in range(parts)])  23 us
    ppermute x14, starting transfers between devices, dp_move(): return lax.ppermute(v, 'dp', [(i, i ^ j) for i in range(parts)])  21.1 us
    ppermute x17, starting transfers between devices, chan_move(): return lax.ppermute(v, 'chan', [(i, i ^ j) for i in range(chan)])  9.62 us
    pallas_call x4, Pallas kernels, finish(): pl.pallas_call(functools.partial(finish_kernel, k, rows, mine, C, n), out...  9.6 us
    ppermute x17, waiting for transfers between devices, chan_move(): return lax.ppermute(v, 'chan', [(i, i ^ j) for i in range(chan)])  7.32 us
    unnamed x44, local copies, waits for them, and re-layouts  6.59 us
    pallas_call x2, Pallas kernels, take_rows(): pl.pallas_call(functools.partial(take_kernel, picks, n), out_shape=[jax.S...  4.34 us
  transfers between devices with their start and end apart: 31, of which 12 were waited for; matrix products, arithmetic and copies ran while one was open for 1% of the time, Pallas kernels for 54%

profile of v3, /device:TPU:0, one launch (start us, length us, event | category | flops | bytes accessed | tf_op | source)
XLA Modules:
  0.0 167.2 jit_solution(10726180935148259274)
XLA Ops:
  1.2 2.2 %take.2 = (bf16[160,2048]{1,0:T(8,128)(2,1)}, bf16[160,2048]{1,0:T(8,128)(2,1)}) custom-call(bf16[160,8192]{1,0:T(8,128)(2,1)} %refs_0_.3), custom_call_target="tpu_custom_call" | custom-call | flops 1 | bytes 1 | tf_op jit(solution)/shard_map/take/pallas_call | solution.py:509
  3.4 3.0 %collective-permute-start.7 = (bf16[160,2048]{1,0:T(8,128)(2,1)}, bf16[160,2048]{1,0:T(8,128)(2,1)S(1)}, u32[]{:S(2)}, u32[]{:S(2)}) collective-permute-start(bf16[160,2048]{1,0:T(8,128)(2,1)} %get-tuple-element.65), channel_id=1, source_target_pairs={{0,2},{1,3},{2,0},{3,1},{4,6},{5,7},{6,4},{7,5},{8,10},{9,11},{10,... | collective-permute-start | bytes 1966088 | tf_op jit(solution)/shard_map/ppermute | solution.py:734
  6.4 1.8 %pack.1 = (bf16[160,512]{1,0:T(8,128)(2,1)}, f32[8,512]{1,0:T(8,128)}) custom-call(bf16[3,160,160]{2,1,0:T(8,128)(2,1)} %w, f32[3,160]{1,0:T(4,128)} %b.1), custom_call_target="tpu_custom_call" | custom-call | flops 1 | bytes 1 | tf_op jit(solution)/shard_map/pack/pallas_call | solution.py:535
  8.2 2.6 %collective-permute-start.2 = (bf16[160,512]{1,0:T(8,128)(2,1)}, bf16[160,512]{1,0:T(8,128)(2,1)}, u32[]{:S(2)}, u32[]{:S(2)}) collective-permute-start(bf16[160,512]{1,0:T(8,128)(2,1)} %get-tuple-element.75.refs_9_), channel_id=1, source_target_pairs={{0,16},{4,20},{8,24},{12,28},{16,0},{20,4},{24,8},{28,12},{1,17},{... | collective-permute-start | bytes 491528 | tf_op jit(solution)/shard_map/ppermute | solution.py:737
  10.8 8.0 %collective-permute-done.2.refs_13_ = bf16[160,512]{1,0:T(8,128)(2,1)} collective-permute-done((bf16[160,512]{1,0:T(8,128)(2,1)}, bf16[160,512]{1,0:T(8,128)(2,1)}, u32[]{:S(2)}, u32[]{:S(2)}) %collective-permute-start.2) | collective-permute-done | bytes 163872 | tf_op jit(solution)/shard_map/ppermute | solution.py:737
  21.0 3.4 %collective-permute-done.9.refs_10_ = bf16[160,512]{1,0:T(8,128)(2,1)} collective-permute-done((bf16[160,512]{1,0:T(8,128)(2,1)}, bf16[160,512]{1,0:T(8,128)(2,1)}, u32[]{:S(2)}, u32[]{:S(2)}) %collective-permute-start.9) | collective-permute-done | bytes 163872 | tf_op jit(solution)/shard_map/ppermute | solution.py:737
  28.0 2.2 %take.3 = (bf16[160,2048]{1,0:T(8,128)(2,1)}, bf16[160,2048]{1,0:T(8,128)(2,1)}) custom-call(bf16[160,8192]{1,0:T(8,128)(2,1)} %refs_0_.3), custom_call_target="tpu_custom_call" | custom-call | flops 1 | bytes 1 | tf_op jit(solution)/shard_map/take/pallas_call | solution.py:509
  32.3 1.9 %collective-permute-start.13 = (bf16[160,512]{1,0:T(8,128)(2,1)}, bf16[160,512]{1,0:T(8,128)(2,1)S(1)}, u32[]{:S(2)}, u32[]{:S(2)}) collective-permute-start(bf16[160,512]{1,0:T(8,128)(2,1)} %collective-permute-done.4.refs_15_), channel_id=1, source_target_pairs={{0,4},{4,0},{8,12},{12,8},{16,20},{20,16},{24,28},{28,24},{1,5},{5... | collective-permute-start | bytes 491528 | tf_op jit(solution)/shard_map/ppermute | solution.py:737
  36.4 3.1 %collective-permute-done.13.refs_16_ = bf16[160,512]{1,0:T(8,128)(2,1)S(1)} collective-permute-done((bf16[160,512]{1,0:T(8,128)(2,1)}, bf16[160,512]{1,0:T(8,128)(2,1)S(1)}, u32[]{:S(2)}, u32[]{:S(2)}) %collective-permute-start.13) | collective-permute-done | bytes 163872 | tf_op jit(solution)/shard_map/ppermute | solution.py:737
  43.1 35.3 %layer.2 = (bf16[160,8192]{1,0:T(8,128)(2,1)}, bf16[320,2048]{1,0:T(8,128)(2,1)}, bf16[160,2048]{1,0:T(8,128)(2,1)}, bf16[160,2048]{1,0:T(8,128)(2,1)}, bf16[160...) custom-call(bf16[160,8192]{1,0:T(8,128)(2,1)} %refs_0_.3, bf16[160,8192]{1,0:T(8,128)(2,1)} %copy-done, ...), custom_call_target="tpu_custom_call" | custom-call | flops 1 | bytes 1 | tf_op jit(solution)/shard_map/layer/pallas_call | solution.py:476
  80.4 35.6 %layer.3 = (bf16[160,8192]{1,0:T(8,128)(2,1)}, bf16[320,2048]{1,0:T(8,128)(2,1)}, bf16[160,2048]{1,0:T(8,128)(2,1)}, bf16[160,2048]{1,0:T(8,128)(2,1)}, bf16[160...) custom-call(bf16[160,8192]{1,0:T(8,128)(2,1)} %refs_0_.3, ...), custom_call_target="tpu_custom_call", output_to_operand_aliasing={{0}: (11, {})} | custom-call | flops 1 | bytes 1 | tf_op jit(solution)/shard_map/layer/pallas_call | solution.py:476
  116.9 4.7 %collective-permute-done.20.near = bf16[320,2048]{1,0:T(8,128)(2,1)S(1)} collective-permute-done((bf16[320,2048]{1,0:T(8,128)(2,1)}, bf16[320,2048]{1,0:T(8,128)(2,1)S(1)}, u32[]{:S(2)}, u32[]{:S(2)}) %collective-permute-start.20) | collective-permute-done | bytes 1310752 | tf_op jit(solution)/shard_map/ppermute | solution.py:734
  123.7 3.5 %split.1 = (bf16[176,512]{1,0:T(8,128)(2,1)}, bf16[176,512]{1,0:T(8,128)(2,1)}, bf16[176,512]{1,0:T(8,128)(2,1)}, bf16[176,512]{1,0:T(8,128)(2,1)}, f32[168,512]...) custom-call(f32[1288,512]{1,0:T(8,128)} %get-tuple-element.93.own, ...), custom_call_target="tpu_custom_call" | custom-call | flops 1 | bytes 1 | tf_op jit(solution)/shard_map/split/pallas_call | solution.py:634
  132.0 2.4 %collective-permute-done.24.r3 = bf16[176,512]{1,0:T(8,128)(2,1)S(1)} collective-permute-done((bf16[176,512]{1,0:T(8,128)(2,1)}, bf16[176,512]{1,0:T(8,128)(2,1)S(1)}, u32[]{:S(2)}, u32[]{:S(2)}) %collective-permute-start.24) | collective-permute-done | bytes 180256 | tf_op jit(solution)/shard_map/ppermute | solution.py:737
  136.1 2.2 %finish.4.refs_0_ = bf16[160,8192]{1,0:T(8,128)(2,1)} custom-call(bf16[160,2048]{1,0:T(8,128)(2,1)} %get-tuple-element.104.near, bf16[160,2048]{1,0:T(8,128)(2,1)} %copy-done.10), custom_call_target="tpu_custom_call" | custom-call | flops 1 | bytes 1 | tf_op jit(solution)/shard_map/finish/pallas_call | solution.py:586
  139.0 2.0 %second.1 = (bf16[176,512]{1,0:T(8,128)(2,1)}, bf16[176,512]{1,0:T(8,128)(2,1)}) custom-call(f32[168,512]{1,0:T(8,128)} %get-tuple-element.100.k6, f32[168,512]{1,0:T(8,128)} %get-tuple-element.101.k1, bf16[176,512]{1,0:T(8,128)(2,1)} %copy-done.18, bf16[176,512]{1,0:T(8,128)(2,1)} %copy-done.17), custom_call_target="tpu_custom_call" | custom-call | flops 1 | bytes 1 | tf_op jit(solution)/shard_map/second/pallas_call | solution.py:664
  143.5 2.6 %finish.5 = (bf16[160,8192]{1,0:T(8,128)(2,1)}, bf16[160,8192]{1,0:T(8,128)(2,1)}) custom-call(bf16[320,2048]{1,0:T(8,128)(2,1)} %copy-done.2, bf16[160,2048]{1,0:T(8,128)(2,1)} %copy-done.7, bf16[160,8192]{1,0:T(8,128)(2,1)} %finish.4.refs_0_, bf16[160,8192]{1,0:T(8,128)(2,1)} %get-tuple-element.108.refs_1_), custom_call_target="tpu_custom_call", output_to_operand_aliasing={{0}: (2, {}), {1}: (3, {})} | custom-call | flops 1 | bytes 1 | tf_op jit(solution)/shard_map/finish/pallas_call | solution.py:586
  146.1 2.6 %collective-permute-done.26.r1 = bf16[176,512]{1,0:T(8,128)(2,1)S(1)} collective-permute-done((bf16[176,512]{1,0:T(8,128)(2,1)}, bf16[176,512]{1,0:T(8,128)(2,1)S(1)}, u32[]{:S(2)}, u32[]{:S(2)}) %collective-permute-start.26) | collective-permute-done | bytes 180256 | tf_op jit(solution)/shard_map/ppermute | solution.py:737
  148.7 2.2 %collective-permute-done.23.r5 = bf16[176,512]{1,0:T(8,128)(2,1)S(1)} collective-permute-done((bf16[176,512]{1,0:T(8,128)(2,1)S(1)}, bf16[176,512]{1,0:T(8,128)(2,1)S(1)}, u32[]{:S(2)}, u32[]{:S(2)}) %collective-permute-start.23) | collective-permute-done | bytes 180256 | tf_op jit(solution)/shard_map/ppermute | solution.py:737
  151.6 1.9 %third.1 = bf16[176,512]{1,0:T(8,128)(2,1)} custom-call(f32[168,512]{1,0:T(8,128)} %get-tuple-element.96.k4, bf16[176,512]{1,0:T(8,128)(2,1)} %copy-done.16, bf16[176,512]{1,0:T(8,128)(2,1)} %copy-done.15), custom_call_target="tpu_custom_call" | custom-call | flops 1 | bytes 1 | tf_op jit(solution)/shard_map/third/pallas_call | solution.py:684
  153.5 3.4 %collective-permute-start.30 = (bf16[176,512]{1,0:T(8,128)(2,1)}, bf16[176,512]{1,0:T(8,128)(2,1)S(1)}, u32[]{:S(2)}, u32[]{:S(2)}) collective-permute-start(bf16[176,512]{1,0:T(8,128)(2,1)} %third.1), channel_id=1, source_target_pairs={{0,16},{4,20},{8,24},{12,28},{16,0},{20,4},{24,8},{28,12},{1,17},{... | collective-permute-start | bytes 540680 | tf_op jit(solution)/shard_map/ppermute | solution.py:737
  157.8 2.2 %finish.6.refs_0_ = bf16[160,8192]{1,0:T(8,128)(2,1)} custom-call(bf16[160,2048]{1,0:T(8,128)(2,1)} %get-tuple-element.117.near, bf16[160,2048]{1,0:T(8,128)(2,1)} %copy-done.9, bf16[160,8192]{1,0:T(8,128)(2,1)} %get-tuple-element.109.refs_0_), custom_call_target="tpu_custom_call", output_to_operand_aliasing={{}: (2, {})} | custom-call | flops 1 | bytes 1 | tf_op jit(solution)/shard_map/finish/pallas_call | solution.py:586
  160.9 2.6 %finish.7 = (bf16[160,8192]{1,0:T(8,128)(2,1)}, bf16[160,8192]{1,0:T(8,128)(2,1)}) custom-call(bf16[320,2048]{1,0:T(8,128)(2,1)} %copy-done.3, bf16[160,2048]{1,0:T(8,128)(2,1)} %copy-done.8, bf16[160,8192]{1,0:T(8,128)(2,1)} %finish.6.refs_0_, bf16[160,8192]{1,0:T(8,128)(2,1)} %get-tuple-element.119.refs_1_), custom_call_target="tpu_custom_call", output_to_operand_aliasing={{0}: (2, {}), {1}: (3, {})} | custom-call | flops 1 | bytes 1 | tf_op jit(solution)/shard_map/finish/pallas_call | solution.py:586
  164.9 2.2 %total.1 = (f32[3,160,160]{2,1,0:T(8,128)}, f32[3,160]{1,0:T(4,128)}) custom-call(f32[168,512]{1,0:T(8,128)} %get-tuple-element.122.k0, bf16[176,512]{1,0:T(8,128)(2,1)} %copy-done.12, bf16[176,512]{1,0:T(8,128)(2,1)} %copy-done.13, bf16[176,512]{1,0:T(8,128)(2,1)} %copy-done.14), custom_call_target="tpu_custom_call" | custom-call | flops 1 | bytes 1 | tf_op jit(solution)/shard_map/total/pallas_call | solution.py:714
  (98 shorter events, 32.4 us)
Async XLA Ops:
  0.6 19.7 %collective-permute-start = (bf16[160,8192]{1,0:T(8,128)(2,1)}, bf16[160,8192]{1,0:T(8,128)(2,1)S(1)}, u32[]{:S(2)}, u32[]{:S(2)}) collective-permute-start(bf16[160,8192]{1,0:T(8,128)(2,1)} %refs_0_.3), channel_id=1, source_target_pairs={{0,1},{1,0},{2,3},{3,2},{4,5},{5,4},{6,7},{7,6},{8,9},{9,8},{10,11... | collective-permute-start | bytes 7864328 | tf_op jit(solution)/shard_map/ppermute | solution.py:734
  1.1 26.3 %collective-permute-start.1 = (bf16[160,8192]{1,0:T(8,128)(2,1)}, bf16[160,8192]{1,0:T(8,128)(2,1)}, u32[]{:S(2)}, u32[]{:S(2)}) collective-permute-start(bf16[160,8192]{1,0:T(8,128)(2,1)} %refs_2_.3), channel_id=1, source_target_pairs={{0,1},{1,0},{2,3},{3,2},{4,5},{5,4},{6,7},{7,6},{8,9},{9,8},{10,11... | collective-permute-start | bytes 7864328 | tf_op jit(solution)/shard_map/ppermute | solution.py:734
  3.4 22.5 %collective-permute-start.7 = (bf16[160,2048]{1,0:T(8,128)(2,1)}, bf16[160,2048]{1,0:T(8,128)(2,1)S(1)}, u32[]{:S(2)}, u32[]{:S(2)}) collective-permute-start(bf16[160,2048]{1,0:T(8,128)(2,1)} %get-tuple-element.65), channel_id=1, source_target_pairs={{0,2},{1,3},{2,0},{3,1},{4,6},{5,7},{6,4},{7,5},{8,10},{9,11},{10,... | collective-permute-start | bytes 1966088 | tf_op jit(solution)/shard_map/ppermute | solution.py:734
  8.2 10.6 %collective-permute-start.2 = (bf16[160,512]{1,0:T(8,128)(2,1)}, bf16[160,512]{1,0:T(8,128)(2,1)}, u32[]{:S(2)}, u32[]{:S(2)}) collective-permute-start(bf16[160,512]{1,0:T(8,128)(2,1)} %get-tuple-element.75.refs_9_), channel_id=1, source_target_pairs={{0,16},{4,20},{8,24},{12,28},{16,0},{20,4},{24,8},{28,12},{1,17},{... | collective-permute-start | bytes 491528 | tf_op jit(solution)/shard_map/ppermute | solution.py:737
  10.8 25.1 %collective-permute-start.8 = (bf16[160,2048]{1,0:T(8,128)(2,1)}, bf16[160,2048]{1,0:T(8,128)(2,1)}, u32[]{:S(2)}, u32[]{:S(2)}) collective-permute-start(bf16[160,2048]{1,0:T(8,128)(2,1)} %get-tuple-element.74), channel_id=1, source_target_pairs={{0,3},{1,2},{2,1},{3,0},{4,7},{5,6},{6,5},{7,4},{8,11},{9,10},{10,... | collective-permute-start | bytes 1966088 | tf_op jit(solution)/shard_map/ppermute | solution.py:734
  20.3 7.1 %collective-permute-start.4 = (bf16[160,512]{1,0:T(8,128)(2,1)}, bf16[160,512]{1,0:T(8,128)(2,1)}, u32[]{:S(2)}, u32[]{:S(2)}) collective-permute-start(bf16[160,512]{1,0:T(8,128)(2,1)} %collective-permute-done.2.refs_13_), channel_id=1, source_target_pairs={{0,8},{4,12},{8,0},{12,4},{16,24},{20,28},{24,16},{28,20},{1,9},{5... | collective-permute-start | bytes 491528 | tf_op jit(solution)/shard_map/ppermute | solution.py:737
  24.4 6.8 %collective-permute-start.10 = (bf16[160,512]{1,0:T(8,128)(2,1)}, bf16[160,512]{1,0:T(8,128)(2,1)}, u32[]{:S(2)}, u32[]{:S(2)}) collective-permute-start(bf16[160,512]{1,0:T(8,128)(2,1)} %get-tuple-element.75.refs_9_), channel_id=1, source_target_pairs={{0,8},{4,12},{8,0},{12,4},{16,24},{20,28},{24,16},{28,20},{1,9},{5... | collective-permute-start | bytes 491528 | tf_op jit(solution)/shard_map/ppermute | solution.py:737
  25.9 6.4 %collective-permute-start.12 = (bf16[160,512]{1,0:T(8,128)(2,1)}, bf16[160,512]{1,0:T(8,128)(2,1)}, u32[]{:S(2)}, u32[]{:S(2)}) collective-permute-start(bf16[160,512]{1,0:T(8,128)(2,1)} %collective-permute-done.2.refs_13_), channel_id=1, source_target_pairs={{0,4},{4,0},{8,12},{12,8},{16,20},{20,16},{24,28},{28,24},{1,5},{5... | collective-permute-start | bytes 491528 | tf_op jit(solution)/shard_map/ppermute | solution.py:737
  27.4 8.7 %collective-permute-start.11 = (bf16[160,512]{1,0:T(8,128)(2,1)}, bf16[160,512]{1,0:T(8,128)(2,1)S(1)}, u32[]{:S(2)}, u32[]{:S(2)}) collective-permute-start(bf16[160,512]{1,0:T(8,128)(2,1)} %collective-permute-done.9.refs_10_), channel_id=1, source_target_pairs={{0,8},{4,12},{8,0},{12,4},{16,24},{20,28},{24,16},{28,20},{1,9},{5... | collective-permute-start | bytes 491528 | tf_op jit(solution)/shard_map/ppermute | solution.py:737
  30.2 48.3 %collective-permute-start.5 = (bf16[160,2048]{1,0:T(8,128)(2,1)}, bf16[160,2048]{1,0:T(8,128)(2,1)}, u32[]{:S(2)}, u32[]{:S(2)}) collective-permute-start(bf16[160,2048]{1,0:T(8,128)(2,1)} %get-tuple-element.72), channel_id=1, source_target_pairs={{0,2},{1,3},{2,0},{3,1},{4,6},{5,7},{6,4},{7,5},{8,10},{9,11},{10,... | collective-permute-start | bytes 1966088 | tf_op jit(solution)/shard_map/ppermute | solution.py:734
  31.2 47.2 %collective-permute-start.6 = (bf16[160,2048]{1,0:T(8,128)(2,1)}, bf16[160,2048]{1,0:T(8,128)(2,1)}, u32[]{:S(2)}, u32[]{:S(2)}) collective-permute-start(bf16[160,2048]{1,0:T(8,128)(2,1)} %get-tuple-element.73), channel_id=1, source_target_pairs={{0,3},{1,2},{2,1},{3,0},{4,7},{5,6},{6,5},{7,4},{8,11},{9,10},{10,... | collective-permute-start | bytes 1966088 | tf_op jit(solution)/shard_map/ppermute | solution.py:734
  32.3 7.2 %collective-permute-start.13 = (bf16[160,512]{1,0:T(8,128)(2,1)}, bf16[160,512]{1,0:T(8,128)(2,1)S(1)}, u32[]{:S(2)}, u32[]{:S(2)}) collective-permute-start(bf16[160,512]{1,0:T(8,128)(2,1)} %collective-permute-done.4.refs_15_), channel_id=1, source_target_pairs={{0,4},{4,0},{8,12},{12,8},{16,20},{20,16},{24,28},{28,24},{1,5},{5... | collective-permute-start | bytes 491528 | tf_op jit(solution)/shard_map/ppermute | solution.py:737
  78.4 37.6 %collective-permute-start.18 = (bf16[320,2048]{1,0:T(8,128)(2,1)}, bf16[320,2048]{1,0:T(8,128)(2,1)S(1)}, u32[]{:S(2)}, u32[]{:S(2)}) collective-permute-start(bf16[320,2048]{1,0:T(8,128)(2,1)} %get-tuple-element.90), channel_id=1, source_target_pairs={{0,1},{1,0},{2,3},{3,2},{4,5},{5,4},{6,7},{7,6},{8,9},{9,8},{10,11... | collective-permute-start | bytes 3932168 | tf_op jit(solution)/shard_map/ppermute | solution.py:734
  78.9 37.2 %collective-permute-start.17 = (bf16[160,2048]{1,0:T(8,128)(2,1)}, bf16[160,2048]{1,0:T(8,128)(2,1)S(1)}, u32[]{:S(2)}, u32[]{:S(2)}) collective-permute-start(bf16[160,2048]{1,0:T(8,128)(2,1)} %get-tuple-element.89), channel_id=1, source_target_pairs={{0,2},{1,3},{2,0},{3,1},{4,6},{5,7},{6,4},{7,5},{8,10},{9,11},{10,... | collective-permute-start | bytes 1966088 | tf_op jit(solution)/shard_map/ppermute | solution.py:734
  79.9 36.1 %collective-permute-start.19 = (bf16[160,2048]{1,0:T(8,128)(2,1)}, bf16[160,2048]{1,0:T(8,128)(2,1)S(1)}, u32[]{:S(2)}, u32[]{:S(2)}) collective-permute-start(bf16[160,2048]{1,0:T(8,128)(2,1)} %get-tuple-element.91), channel_id=1, source_target_pairs={{0,3},{1,2},{2,1},{3,0},{4,7},{5,6},{6,5},{7,4},{8,11},{9,10},{10,... | collective-permute-start | bytes 1966088 | tf_op jit(solution)/shard_map/ppermute | solution.py:734
  127.3 7.1 %collective-permute-start.24 = (bf16[176,512]{1,0:T(8,128)(2,1)}, bf16[176,512]{1,0:T(8,128)(2,1)S(1)}, u32[]{:S(2)}, u32[]{:S(2)}) collective-permute-start(bf16[176,512]{1,0:T(8,128)(2,1)} %get-tuple-element.102), channel_id=1, source_target_pairs={{0,8},{4,12},{8,0},{12,4},{16,24},{20,28},{24,16},{28,20},{1,9},{5... | collective-permute-start | bytes 540680 | tf_op jit(solution)/shard_map/ppermute | solution.py:737
  129.0 27.9 %collective-permute-start.29 = (bf16[160,2048]{1,0:T(8,128)(2,1)}, bf16[160,2048]{1,0:T(8,128)(2,1)S(1)}, u32[]{:S(2)}, u32[]{:S(2)}) collective-permute-start(bf16[160,2048]{1,0:T(8,128)(2,1)} %get-tuple-element.118), channel_id=1, source_target_pairs={{0,2},{1,3},{2,0},{3,1},{4,6},{5,7},{6,4},{7,5},{8,10},{9,11},{10,... | collective-permute-start | bytes 1966088 | tf_op jit(solution)/shard_map/ppermute | solution.py:734
  130.0 30.1 %collective-permute-start.28 = (bf16[160,2048]{1,0:T(8,128)(2,1)}, bf16[160,2048]{1,0:T(8,128)(2,1)S(1)}, u32[]{:S(2)}, u32[]{:S(2)}) collective-permute-start(bf16[160,2048]{1,0:T(8,128)(2,1)} %get-tuple-element.115), channel_id=1, source_target_pairs={{0,3},{1,2},{2,1},{3,0},{4,7},{5,6},{6,5},{7,4},{8,11},{9,10},{10,... | collective-permute-start | bytes 1966088 | tf_op jit(solution)/shard_map/ppermute | solution.py:734
  130.5 7.8 %collective-permute-start.22 = (bf16[176,512]{1,0:T(8,128)(2,1)}, bf16[176,512]{1,0:T(8,128)(2,1)S(1)}, u32[]{:S(2)}, u32[]{:S(2)}) collective-permute-start(bf16[176,512]{1,0:T(8,128)(2,1)} %get-tuple-element.98), channel_id=1, source_target_pairs={{0,4},{4,0},{8,12},{12,8},{16,20},{20,16},{24,28},{28,24},{1,5},{5... | collective-permute-start | bytes 540680 | tf_op jit(solution)/shard_map/ppermute | solution.py:737
  134.4 8.4 %collective-permute-start.27 = (bf16[176,512]{1,0:T(8,128)(2,1)}, bf16[176,512]{1,0:T(8,128)(2,1)S(1)}, u32[]{:S(2)}, u32[]{:S(2)}) collective-permute-start(bf16[176,512]{1,0:T(8,128)(2,1)} %get-tuple-element.112), channel_id=1, source_target_pairs={{0,8},{4,12},{8,0},{12,4},{16,24},{20,28},{24,16},{28,20},{1,9},{5... | collective-permute-start | bytes 540680 | tf_op jit(solution)/shard_map/ppermute | solution.py:737
  141.0 7.8 %collective-permute-start.26 = (bf16[176,512]{1,0:T(8,128)(2,1)}, bf16[176,512]{1,0:T(8,128)(2,1)S(1)}, u32[]{:S(2)}, u32[]{:S(2)}) collective-permute-start(bf16[176,512]{1,0:T(8,128)(2,1)} %get-tuple-element.110), channel_id=1, source_target_pairs={{0,4},{4,0},{8,12},{12,8},{16,20},{20,16},{24,28},{28,24},{1,5},{5... | collective-permute-start | bytes 540680 | tf_op jit(solution)/shard_map/ppermute | solution.py:737
  142.6 6.2 %collective-permute-start.25 = (bf16[176,512]{1,0:T(8,128)(2,1)}, bf16[176,512]{1,0:T(8,128)(2,1)S(1)}, u32[]{:S(2)}, u32[]{:S(2)}) collective-permute-start(bf16[176,512]{1,0:T(8,128)(2,1)} %get-tuple-element.106), channel_id=1, source_target_pairs={{0,8},{4,12},{8,0},{12,4},{16,24},{20,28},{24,16},{28,20},{1,9},{5... | collective-permute-start | bytes 540680 | tf_op jit(solution)/shard_map/ppermute | solution.py:737
  142.9 8.1 %collective-permute-start.23 = (bf16[176,512]{1,0:T(8,128)(2,1)S(1)}, bf16[176,512]{1,0:T(8,128)(2,1)S(1)}, u32[]{:S(2)}, u32[]{:S(2)}) collective-permute-start(bf16[176,512]{1,0:T(8,128)(2,1)S(1)} %copy-done.21), channel_id=1, source_target_pairs={{0,4},{4,0},{8,12},{12,8},{16,20},{20,16},{24,28},{28,24},{1,5},{5... | collective-permute-start | bytes 540680 | tf_op jit(solution)/shard_map/ppermute | solution.py:737
  153.5 10.7 %collective-permute-start.30 = (bf16[176,512]{1,0:T(8,128)(2,1)}, bf16[176,512]{1,0:T(8,128)(2,1)S(1)}, u32[]{:S(2)}, u32[]{:S(2)}) collective-permute-start(bf16[176,512]{1,0:T(8,128)(2,1)} %third.1), channel_id=1, source_target_pairs={{0,16},{4,20},{8,24},{12,28},{16,0},{20,4},{24,8},{28,12},{1,17},{... | collective-permute-start | bytes 540680 | tf_op jit(solution)/shard_map/ppermute | solution.py:737
  (29 other events, 186.3 us)

commit v4 on v3

--- a/solution.py
+++ b/solution.py
@@ -439,7 +439,7 @@
         if not last:
             alias[len(ins) - 2] = 5
     if last:
-        outs += [shape((2 * D + SEGS, N // 2), f32), shape((2 * D + 16, N // 2), bf16)]
+        outs += [shape((2 * D + SEGS, N // 2), f32), shape((2 * D + SEGS, N // 2), bf16)]
     else:
         outs += [shape((2 * D + SEGS, N), f32)]
     if first:
@@ -461,7 +461,7 @@
             pltpu.VMEM((T, N), bf16),
             pltpu.VMEM((D, T), bf16),
             pltpu.VMEM((2 * D + SEGS, N), f32),
-            pltpu.VMEM((2 * D + 16, N // 2), bf16),
+            pltpu.VMEM((2 * D + SEGS, N // 2), bf16),
             pltpu.VMEM((4, SEGS, w3), f32),
             pltpu.VMEM((D, LANES), f32),
             pltpu.VMEM((SEGS, N), f32),
@@ -515,6 +515,7 @@
             pltpu.VMEM((len(picks), C, width), bf16),
             pltpu.SemaphoreType.DMA((len(picks), len(picks[0]))),
         ],
+        compiler_params=pltpu.CompilerParams(vmem_limit_bytes=8 << 20),
         cost_estimate=pl.CostEstimate(flops=1, bytes_accessed=1, transcendentals=0),
         name="take",
     )(tok)
@@ -540,6 +541,7 @@
         ],
         in_specs=[VMEM] * 2,
         out_specs=[VMEM] * 2,
+        compiler_params=pltpu.CompilerParams(vmem_limit_bytes=4 << 20),
         cost_estimate=pl.CostEstimate(flops=1, bytes_accessed=1, transcendentals=0),
         name="pack",
     )(w, b)
@@ -590,6 +592,7 @@
         out_specs=[ANY] * len(outs),
         scratch_shapes=[pltpu.VMEM((C, rows * n), bf16), pltpu.SemaphoreType.DMA((2 * rows,))],
         input_output_aliases=alias,
+        compiler_params=pltpu.CompilerParams(vmem_limit_bytes=8 << 20),
         cost_estimate=pl.CostEstimate(flops=1, bytes_accessed=1, transcendentals=0),
         name="finish",
     )(*ins)
@@ -598,7 +601,7 @@
 def in_two(v):
     high = v.astype(bf16)
     low = v - high.astype(f32)
-    at = lax.broadcasted_iota(jnp.int32, (16, v.shape[1]), 0)
+    at = lax.broadcasted_iota(jnp.int32, (SEGS, v.shape[1]), 0)
     return jnp.where(at == 0, high.astype(f32), jnp.where(at == 1, low, 0.0)).astype(bf16)
 
 
@@ -630,18 +633,18 @@
 
 def split(C, own, other):
     half = own.shape[1]
-    message = jax.ShapeDtypeStruct((C + 16, half), bf16)
+    message = jax.ShapeDtypeStruct((C + SEGS, half), bf16)
     return pl.pallas_call(
         functools.partial(split_kernel, C),
         out_shape=[message] * 4 + [jax.ShapeDtypeStruct((C + 8, half), f32)] * 4,
         in_specs=[VMEM] * 2,
         out_specs=[HBM] * 8,
         scratch_shapes=[
-            pltpu.VMEM((4, C + 16, half), bf16),
+            pltpu.VMEM((4, C + SEGS, half), bf16),
             pltpu.VMEM((4, C + 8, half), f32),
             pltpu.SemaphoreType.DMA((8,)),
         ],
-        compiler_params=pltpu.CompilerParams(vmem_limit_bytes=62 << 20),
+        compiler_params=pltpu.CompilerParams(vmem_limit_bytes=16 << 20),
         cost_estimate=pl.CostEstimate(flops=1, bytes_accessed=1, transcendentals=0),
         name="split",
     )(own, other)
@@ -667,6 +670,7 @@
         in_specs=[VMEM] * 4,
         out_specs=[HBM] * 2,
         scratch_shapes=[pltpu.VMEM((2,) + r7.shape, bf16), pltpu.SemaphoreType.DMA((2,))],
+        compiler_params=pltpu.CompilerParams(vmem_limit_bytes=4 << 20),
         cost_estimate=pl.CostEstimate(flops=1, bytes_accessed=1, transcendentals=0),
         name="second",
     )(k6, k1, r7, r3)
@@ -687,6 +691,7 @@
         in_specs=[VMEM] * 3,
         out_specs=HBM,
         scratch_shapes=[pltpu.VMEM(r6.shape, bf16), pltpu.SemaphoreType.DMA],
+        compiler_params=pltpu.CompilerParams(vmem_limit_bytes=4 << 20),
         cost_estimate=pl.CostEstimate(flops=1, bytes_accessed=1, transcendentals=0),
         name="third",
     )(k4, r5, r6)
@@ -717,6 +722,7 @@
         in_specs=[VMEM] * 4,
         out_specs=[HBM] * 2,
         scratch_shapes=[pltpu.VMEM(shape, f32) for shape in shapes] + [pltpu.SemaphoreType.DMA((2,))],
+        compiler_params=pltpu.CompilerParams(vmem_limit_bytes=4 << 20),
         cost_estimate=pl.CostEstimate(flops=1, bytes_accessed=1, transcendentals=0),
         name="total",
     )(k0, r2, r1, r4)
@@ -797,14 +803,13 @@
             grad, hid = finish(k, rows, False, C, n, total, after(from_sib, *others), from_pd, grad, hid)
 
     s7, s3, s5, s2, k0, k1, k4, k6 = split(C, acc, after(acc_sib, moved[-1][2]))
-    r7, r3 = dp_move(s7, 1), dp_move(s3, 2)
+    r7, r3, r5 = dp_move(s7, 1), dp_move(s3, 2), dp_move(s5, 1)
     for k in range(CALLS - 1):
         end(k, True, s7)
     s6, s1 = second(C, k6, k1, r7, after(r3, grad))
-    r5, r2 = dp_move(after(s5, r7), 1), dp_move(after(s2, r3), 2)
-    r6, r1 = dp_move(s6, 2), dp_move(s1, 1)
+    r6, r1, r2 = dp_move(s6, 2), dp_move(s1, 1), dp_move(after(s2, r3), 2)
     for k in range(CALLS - 1):
-        end(k, False, s6)
+        end(k, False, s6, r5)
     s4 = third(C, k4, r5, after(r6, grad, r1, r2))
     r4 = dp_move(s4, 4)
     end(CALLS - 1, True, s4)

time: 168 us -> 151 us (0.90)
  Pallas kernels: 96.2 us -> 79.9 us
  waiting for transfers between devices: 30.4 us -> 33.2 us
  local copies, waits for them, and re-layouts: 6.59 us -> 4.26 us
  other arithmetic: 2.23 us -> 0.09 us
    pallas_call x4, Pallas kernels: 9.6 us -> 4.07 us  [finish(): pl.pallas_call(functools.partial(finish_kernel, k, rows, mine, C, n), out...]
    pallas_call x2, Pallas kernels: 4.34 us -> 1.09 us  [take_rows(): pl.pallas_call(functools.partial(take_kernel, picks, n), out_shape=[jax.S...]
    ppermute x17, waiting for transfers between devices: 7.32 us -> 9.82 us  [chan_move(): return lax.ppermute(v, 'chan', [(i, i ^ j) for i in range(chan)])]
    unnamed x44, local copies, waits for them, and re-layouts: 6.59 us -> 4.26 us
    concatenate x3, other arithmetic: 2.23 us -> 0.09 us  [to_sibling(): return chan_move(jnp.concatenate([g[j] for j in group], 0), 1)]
    pallas_call x1, Pallas kernels: 3.54 us -> 1.79 us  [split(): pl.pallas_call(functools.partial(split_kernel, C), out_shape=[message] *...]
  transfers between devices with their start and end apart: 31 -> 31, of which waited for: 12 -> 15; matrix products, arithmetic and copies ran while one was open for 1% -> 0% of each run, Pallas kernels for 54% -> 52%
where the time goes in v4:
time: 151 us
  Pallas kernels  79.9 us (53%)
  waiting for transfers between devices  33.2 us (22%)
  starting transfers between devices  32.2 us (21%)
  local copies, waits for them, and re-layouts  4.26 us (3%)
    pallas_call x2, Pallas kernels, layer(): pl.pallas_call(functools.partial(layer_kernel, k, calls, rows, parts, C,...  70.9 us
    ppermute x14, waiting for transfers between devices, dp_move(): return lax.ppermute(v, 'dp', [(i, i ^ j) for i in range(parts)])  23.4 us
    ppermute x14, starting transfers between devices, dp_move(): return lax.ppermute(v, 'dp', [(i, i ^ j) for i in range(parts)])  21.3 us
    ppermute x17, starting transfers between devices, chan_move(): return lax.ppermute(v, 'chan', [(i, i ^ j) for i in range(chan)])  10.8 us
    ppermute x17, waiting for transfers between devices, chan_move(): return lax.ppermute(v, 'chan', [(i, i ^ j) for i in range(chan)])  9.82 us
    unnamed x44, local copies, waits for them, and re-layouts  4.26 us
    pallas_call x4, Pallas kernels, finish(): pl.pallas_call(functools.partial(finish_kernel, k, rows, mine, C, n), out...  4.07 us
  transfers between devices with their start and end apart: 31, of which 15 were waited for; matrix products, arithmetic and copies ran while one was open for 0% of the time, Pallas kernels for 52%

profile of v4, /device:TPU:0, one launch (start us, length us, event | category | flops | bytes accessed | tf_op | source)
XLA Modules:
  0.0 150.8 jit_solution(15644125523898650231)
XLA Ops:
  1.2 1.7 %copy-done = bf16[160,8192]{1,0:T(8,128)(2,1)S(1)} copy-done((bf16[160,8192]{1,0:T(8,128)(2,1)S(1)}, bf16[160,8192]{1,0:T(8,128)(2,1)}, u32[]{:S(2)}) %copy-start) | copy-done | bytes 2621464
  3.5 3.0 %collective-permute-start.7 = (bf16[160,2048]{1,0:T(8,128)(2,1)S(1)}, bf16[160,2048]{1,0:T(8,128)(2,1)S(1)}, u32[]{:S(2)}, u32[]{:S(2)}) collective-permute-start(bf16[160,2048]{1,0:T(8,128)(2,1)S(1)} %get-tuple-element.64), channel_id=1, source_target_pairs={{0,2},{1,3},{2,0},{3,1},{4,6},{5,7},{6,4},{7,5},{8,10},{9,11},{10,... | collective-permute-start | bytes 1966088 | tf_op jit(solution)/shard_map/ppermute | solution.py:740
  6.7 2.7 %collective-permute-start.2 = (bf16[160,512]{1,0:T(8,128)(2,1)S(1)}, bf16[160,512]{1,0:T(8,128)(2,1)S(1)}, u32[]{:S(2)}, u32[]{:S(2)}) collective-permute-start(bf16[160,512]{1,0:T(8,128)(2,1)S(1)} %get-tuple-element.74.refs_9_), channel_id=1, source_target_pairs={{0,16},{4,20},{8,24},{12,28},{16,0},{20,4},{24,8},{28,12},{1,17},{... | collective-permute-start | bytes 491528 | tf_op jit(solution)/shard_map/ppermute | solution.py:743
  9.4 7.7 %collective-permute-done.2.refs_13_ = bf16[160,512]{1,0:T(8,128)(2,1)S(1)} collective-permute-done((bf16[160,512]{1,0:T(8,128)(2,1)S(1)}, bf16[160,512]{1,0:T(8,128)(2,1)S(1)}, u32[]{:S(2)}, u32[]{:S(2)}) %collective-permute-start.2) | collective-permute-done | bytes 163872 | tf_op jit(solution)/shard_map/ppermute | solution.py:743
  19.3 3.1 %collective-permute-done.9.refs_10_ = bf16[160,512]{1,0:T(8,128)(2,1)S(1)} collective-permute-done((bf16[160,512]{1,0:T(8,128)(2,1)S(1)}, bf16[160,512]{1,0:T(8,128)(2,1)S(1)}, u32[]{:S(2)}, u32[]{:S(2)}) %collective-permute-start.9) | collective-permute-done | bytes 163872 | tf_op jit(solution)/shard_map/ppermute | solution.py:743
  23.9 1.5 %collective-permute-start.12 = (bf16[160,512]{1,0:T(8,128)(2,1)S(1)}, bf16[160,512]{1,0:T(8,128)(2,1)S(1)}, u32[]{:S(2)}, u32[]{:S(2)}) collective-permute-start(bf16[160,512]{1,0:T(8,128)(2,1)S(1)} %collective-permute-done.2.refs_13_), channel_id=1, source_target_pairs={{0,4},{4,0},{8,12},{12,8},{16,20},{20,16},{24,28},{28,24},{1,5},{5... | collective-permute-start | bytes 491528 | tf_op jit(solution)/shard_map/ppermute | solution.py:743
  29.2 1.6 %collective-permute-start.13 = (bf16[160,512]{1,0:T(8,128)(2,1)S(1)}, bf16[160,512]{1,0:T(8,128)(2,1)S(1)}, u32[]{:S(2)}, u32[]{:S(2)}) collective-permute-start(bf16[160,512]{1,0:T(8,128)(2,1)S(1)} %collective-permute-done.4.refs_15_), channel_id=1, source_target_pairs={{0,4},{4,0},{8,12},{12,8},{16,20},{20,16},{24,28},{28,24},{1,5},{5... | collective-permute-start | bytes 491528 | tf_op jit(solution)/shard_map/ppermute | solution.py:743
  30.9 4.8 %collective-permute-done.8.refs_8_ = bf16[160,2048]{1,0:T(8,128)(2,1)S(1)} collective-permute-done((bf16[160,2048]{1,0:T(8,128)(2,1)S(1)}, bf16[160,2048]{1,0:T(8,128)(2,1)S(1)}, u32[]{:S(2)}, u32[]{:S(2)}) %collective-permute-start.8) | collective-permute-done | bytes 655392 | tf_op jit(solution)/shard_map/ppermute | solution.py:740
  40.0 35.3 %layer.2 = (bf16[160,8192]{1,0:T(8,128)(2,1)}, bf16[320,2048]{1,0:T(8,128)(2,1)}, bf16[160,2048]{1,0:T(8,128)(2,1)}, bf16[160,2048]{1,0:T(8,128)(2,1)}, bf16[160...) custom-call(bf16[160,8192]{1,0:T(8,128)(2,1)} %refs_0_.3, bf16[160,8192]{1,0:T(8,128)(2,1)} %copy-done.8, ...), custom_call_target="tpu_custom_call" | custom-call | flops 1 | bytes 1 | tf_op jit(solution)/shard_map/layer/pallas_call | solution.py:476
  75.7 1.9 %collective-permute-start.17 = (bf16[160,2048]{1,0:T(8,128)(2,1)}, bf16[160,2048]{1,0:T(8,128)(2,1)S(1)}, u32[]{:S(2)}, u32[]{:S(2)}) collective-permute-start(bf16[160,2048]{1,0:T(8,128)(2,1)} %get-tuple-element.88), channel_id=1, source_target_pairs={{0,2},{1,3},{2,0},{3,1},{4,6},{5,7},{6,4},{7,5},{8,10},{9,11},{10,... | collective-permute-start | bytes 1966088 | tf_op jit(solution)/shard_map/ppermute | solution.py:740
  77.7 35.6 %layer.3 = (bf16[160,8192]{1,0:T(8,128)(2,1)}, bf16[320,2048]{1,0:T(8,128)(2,1)}, bf16[160,2048]{1,0:T(8,128)(2,1)}, bf16[160,2048]{1,0:T(8,128)(2,1)}, bf16[160...) custom-call(bf16[160,8192]{1,0:T(8,128)(2,1)} %refs_0_.3, ...), custom_call_target="tpu_custom_call", output_to_operand_aliasing={{0}: (11, {})} | custom-call | flops 1 | bytes 1 | tf_op jit(solution)/shard_map/layer/pallas_call | solution.py:476
  113.9 1.7 %collective-permute-start.29 = (bf16[160,2048]{1,0:T(8,128)(2,1)}, bf16[160,2048]{1,0:T(8,128)(2,1)S(1)}, u32[]{:S(2)}, u32[]{:S(2)}) collective-permute-start(bf16[160,2048]{1,0:T(8,128)(2,1)} %get-tuple-element.116), channel_id=1, source_target_pairs={{0,2},{1,3},{2,0},{3,1},{4,6},{5,7},{6,4},{7,5},{8,10},{9,11},{10,... | collective-permute-start | bytes 1966088 | tf_op jit(solution)/shard_map/ppermute | solution.py:740
  115.6 2.9 %collective-permute-done.20.near = bf16[320,2048]{1,0:T(8,128)(2,1)S(1)} collective-permute-done((bf16[320,2048]{1,0:T(8,128)(2,1)}, bf16[320,2048]{1,0:T(8,128)(2,1)S(1)}, u32[]{:S(2)}, u32[]{:S(2)}) %collective-permute-start.20) | collective-permute-done | bytes 1310752 | tf_op jit(solution)/shard_map/ppermute | solution.py:740
  118.5 1.7 %copy-done.1 = f32[1288,512]{1,0:T(8,128)S(1)} copy-done((f32[1288,512]{1,0:T(8,128)S(1)}, f32[1288,512]{1,0:T(8,128)}, u32[]{:S(2)}) %copy-start.1) | copy-done | bytes 2637848
  120.2 1.8 %split.1 = (bf16[168,512]{1,0:T(8,128)(2,1)S(1)}, bf16[168,512]{1,0:T(8,128)(2,1)S(1)}, bf16[168,512]{1,0:T(8,128)(2,1)S(1)}, bf16[168,512]{1,0:T(8,128)(2,1)S(1...) custom-call(f32[1288,512]{1,0:T(8,128)S(1)} %copy-done.1, ...), custom_call_target="tpu_custom_call" | custom-call | flops 1 | bytes 1 | tf_op jit(solution)/shard_map/split/pallas_call | solution.py:637
  122.0 1.9 %collective-permute-start.24 = (bf16[168,512]{1,0:T(8,128)(2,1)S(1)}, bf16[168,512]{1,0:T(8,128)(2,1)S(1)}, u32[]{:S(2)}, u32[]{:S(2)}) collective-permute-start(bf16[168,512]{1,0:T(8,128)(2,1)S(1)} %get-tuple-element.100), channel_id=1, source_target_pairs={{0,8},{4,12},{8,0},{12,4},{16,24},{20,28},{24,16},{28,20},{1,9},{5... | collective-permute-start | bytes 516104 | tf_op jit(solution)/shard_map/ppermute | solution.py:743
  126.9 1.9 %collective-permute-done.24.r3 = bf16[168,512]{1,0:T(8,128)(2,1)S(1)} collective-permute-done((bf16[168,512]{1,0:T(8,128)(2,1)S(1)}, bf16[168,512]{1,0:T(8,128)(2,1)S(1)}, u32[]{:S(2)}, u32[]{:S(2)}) %collective-permute-start.24) | collective-permute-done | bytes 172064 | tf_op jit(solution)/shard_map/ppermute | solution.py:743
  128.9 1.7 %collective-permute-start.27 = (bf16[168,512]{1,0:T(8,128)(2,1)S(1)}, bf16[168,512]{1,0:T(8,128)(2,1)S(1)}, u32[]{:S(2)}, u32[]{:S(2)}) collective-permute-start(bf16[168,512]{1,0:T(8,128)(2,1)S(1)} %get-tuple-element.110), channel_id=1, source_target_pairs={{0,8},{4,12},{8,0},{12,4},{16,24},{20,28},{24,16},{28,20},{1,9},{5... | collective-permute-start | bytes 516104 | tf_op jit(solution)/shard_map/ppermute | solution.py:743
  131.8 1.6 %collective-permute-start.26 = (bf16[168,512]{1,0:T(8,128)(2,1)S(1)}, bf16[168,512]{1,0:T(8,128)(2,1)S(1)}, u32[]{:S(2)}, u32[]{:S(2)}) collective-permute-start(bf16[168,512]{1,0:T(8,128)(2,1)S(1)} %get-tuple-element.108), channel_id=1, source_target_pairs={{0,4},{4,0},{8,12},{12,8},{16,20},{20,16},{24,28},{28,24},{1,5},{5... | collective-permute-start | bytes 516104 | tf_op jit(solution)/shard_map/ppermute | solution.py:743
  133.3 1.5 %collective-permute-done.22.r5 = bf16[168,512]{1,0:T(8,128)(2,1)S(1)} collective-permute-done((bf16[168,512]{1,0:T(8,128)(2,1)S(1)}, bf16[168,512]{1,0:T(8,128)(2,1)S(1)}, u32[]{:S(2)}, u32[]{:S(2)}) %collective-permute-start.22) | collective-permute-done | bytes 172064 | tf_op jit(solution)/shard_map/ppermute | solution.py:743
  136.1 1.6 %collective-permute-done.26.r1 = bf16[168,512]{1,0:T(8,128)(2,1)S(1)} collective-permute-done((bf16[168,512]{1,0:T(8,128)(2,1)S(1)}, bf16[168,512]{1,0:T(8,128)(2,1)S(1)}, u32[]{:S(2)}, u32[]{:S(2)}) %collective-permute-start.26) | collective-permute-done | bytes 172064 | tf_op jit(solution)/shard_map/ppermute | solution.py:743
  137.7 2.6 %collective-permute-done.25.r6 = bf16[168,512]{1,0:T(8,128)(2,1)S(1)} collective-permute-done((bf16[168,512]{1,0:T(8,128)(2,1)S(1)}, bf16[168,512]{1,0:T(8,128)(2,1)S(1)}, u32[]{:S(2)}, u32[]{:S(2)}) %collective-permute-start.25) | collective-permute-done | bytes 172064 | tf_op jit(solution)/shard_map/ppermute | solution.py:743
  140.6 3.8 %collective-permute-start.30 = (bf16[168,512]{1,0:T(8,128)(2,1)S(1)}, bf16[168,512]{1,0:T(8,128)(2,1)S(1)}, u32[]{:S(2)}, u32[]{:S(2)}) collective-permute-start(bf16[168,512]{1,0:T(8,128)(2,1)S(1)} %third.1), channel_id=1, source_target_pairs={{0,16},{4,20},{8,24},{12,28},{16,0},{20,4},{24,8},{28,12},{1,17},{... | collective-permute-start | bytes 516104 | tf_op jit(solution)/shard_map/ppermute | solution.py:743
  146.5 3.1 %collective-permute-done.30.r4 = bf16[168,512]{1,0:T(8,128)(2,1)S(1)} collective-permute-done((bf16[168,512]{1,0:T(8,128)(2,1)S(1)}, bf16[168,512]{1,0:T(8,128)(2,1)S(1)}, u32[]{:S(2)}, u32[]{:S(2)}) %collective-permute-start.30) | collective-permute-done | bytes 172064 | tf_op jit(solution)/shard_map/ppermute | solution.py:743
  (98 shorter events, 22.8 us)
Async XLA Ops:
  0.6 18.0 %collective-permute-start = (bf16[160,8192]{1,0:T(8,128)(2,1)}, bf16[160,8192]{1,0:T(8,128)(2,1)S(1)}, u32[]{:S(2)}, u32[]{:S(2)}) collective-permute-start(bf16[160,8192]{1,0:T(8,128)(2,1)} %refs_0_.3), channel_id=1, source_target_pairs={{0,1},{1,0},{2,3},{3,2},{4,5},{5,4},{6,7},{7,6},{8,9},{9,8},{10,11... | collective-permute-start | bytes 7864328 | tf_op jit(solution)/shard_map/ppermute | solution.py:740
  1.1 24.3 %collective-permute-start.1 = (bf16[160,8192]{1,0:T(8,128)(2,1)}, bf16[160,8192]{1,0:T(8,128)(2,1)S(1)}, u32[]{:S(2)}, u32[]{:S(2)}) collective-permute-start(bf16[160,8192]{1,0:T(8,128)(2,1)} %refs_2_.3), channel_id=1, source_target_pairs={{0,1},{1,0},{2,3},{3,2},{4,5},{5,4},{6,7},{7,6},{8,9},{9,8},{10,11... | collective-permute-start | bytes 7864328 | tf_op jit(solution)/shard_map/ppermute | solution.py:740
  3.5 20.4 %collective-permute-start.7 = (bf16[160,2048]{1,0:T(8,128)(2,1)S(1)}, bf16[160,2048]{1,0:T(8,128)(2,1)S(1)}, u32[]{:S(2)}, u32[]{:S(2)}) collective-permute-start(bf16[160,2048]{1,0:T(8,128)(2,1)S(1)} %get-tuple-element.64), channel_id=1, source_target_pairs={{0,2},{1,3},{2,0},{3,1},{4,6},{5,7},{6,4},{7,5},{8,10},{9,11},{10,... | collective-permute-start | bytes 1966088 | tf_op jit(solution)/shard_map/ppermute | solution.py:740
  6.7 10.4 %collective-permute-start.2 = (bf16[160,512]{1,0:T(8,128)(2,1)S(1)}, bf16[160,512]{1,0:T(8,128)(2,1)S(1)}, u32[]{:S(2)}, u32[]{:S(2)}) collective-permute-start(bf16[160,512]{1,0:T(8,128)(2,1)S(1)} %get-tuple-element.74.refs_9_), channel_id=1, source_target_pairs={{0,16},{4,20},{8,24},{12,28},{16,0},{20,4},{24,8},{28,12},{1,17},{... | collective-permute-start | bytes 491528 | tf_op jit(solution)/shard_map/ppermute | solution.py:743
  9.4 26.3 %collective-permute-start.8 = (bf16[160,2048]{1,0:T(8,128)(2,1)S(1)}, bf16[160,2048]{1,0:T(8,128)(2,1)S(1)}, u32[]{:S(2)}, u32[]{:S(2)}) collective-permute-start(bf16[160,2048]{1,0:T(8,128)(2,1)S(1)} %get-tuple-element.73), channel_id=1, source_target_pairs={{0,3},{1,2},{2,1},{3,0},{4,7},{5,6},{6,5},{7,4},{8,11},{9,10},{10,... | collective-permute-start | bytes 1966088 | tf_op jit(solution)/shard_map/ppermute | solution.py:740
  18.6 6.8 %collective-permute-start.4 = (bf16[160,512]{1,0:T(8,128)(2,1)S(1)}, bf16[160,512]{1,0:T(8,128)(2,1)S(1)}, u32[]{:S(2)}, u32[]{:S(2)}) collective-permute-start(bf16[160,512]{1,0:T(8,128)(2,1)S(1)} %collective-permute-done.2.refs_13_), channel_id=1, source_target_pairs={{0,8},{4,12},{8,0},{12,4},{16,24},{20,28},{24,16},{28,20},{1,9},{5... | collective-permute-start | bytes 491528 | tf_op jit(solution)/shard_map/ppermute | solution.py:743
  22.4 6.4 %collective-permute-start.10 = (bf16[160,512]{1,0:T(8,128)(2,1)S(1)}, bf16[160,512]{1,0:T(8,128)(2,1)S(1)}, u32[]{:S(2)}, u32[]{:S(2)}) collective-permute-start(bf16[160,512]{1,0:T(8,128)(2,1)S(1)} %get-tuple-element.74.refs_9_), channel_id=1, source_target_pairs={{0,8},{4,12},{8,0},{12,4},{16,24},{20,28},{24,16},{28,20},{1,9},{5... | collective-permute-start | bytes 491528 | tf_op jit(solution)/shard_map/ppermute | solution.py:743
  23.9 5.3 %collective-permute-start.12 = (bf16[160,512]{1,0:T(8,128)(2,1)S(1)}, bf16[160,512]{1,0:T(8,128)(2,1)S(1)}, u32[]{:S(2)}, u32[]{:S(2)}) collective-permute-start(bf16[160,512]{1,0:T(8,128)(2,1)S(1)} %collective-permute-done.2.refs_13_), channel_id=1, source_target_pairs={{0,4},{4,0},{8,12},{12,8},{16,20},{20,16},{24,28},{28,24},{1,5},{5... | collective-permute-start | bytes 491528 | tf_op jit(solution)/shard_map/ppermute | solution.py:743
  25.4 10.6 %collective-permute-start.11 = (bf16[160,512]{1,0:T(8,128)(2,1)S(1)}, bf16[160,512]{1,0:T(8,128)(2,1)S(1)}, u32[]{:S(2)}, u32[]{:S(2)}) collective-permute-start(bf16[160,512]{1,0:T(8,128)(2,1)S(1)} %collective-permute-done.9.refs_10_), channel_id=1, source_target_pairs={{0,8},{4,12},{8,0},{12,4},{16,24},{20,28},{24,16},{28,20},{1,9},{5... | collective-permute-start | bytes 491528 | tf_op jit(solution)/shard_map/ppermute | solution.py:743
  26.6 48.7 %collective-permute-start.5 = (bf16[160,2048]{1,0:T(8,128)(2,1)S(1)}, bf16[160,2048]{1,0:T(8,128)(2,1)}, u32[]{:S(2)}, u32[]{:S(2)}) collective-permute-start(bf16[160,2048]{1,0:T(8,128)(2,1)S(1)} %get-tuple-element.71), channel_id=1, source_target_pairs={{0,2},{1,3},{2,0},{3,1},{4,6},{5,7},{6,4},{7,5},{8,10},{9,11},{10,... | collective-permute-start | bytes 1966088 | tf_op jit(solution)/shard_map/ppermute | solution.py:740
  28.8 46.5 %collective-permute-start.6 = (bf16[160,2048]{1,0:T(8,128)(2,1)S(1)}, bf16[160,2048]{1,0:T(8,128)(2,1)}, u32[]{:S(2)}, u32[]{:S(2)}) collective-permute-start(bf16[160,2048]{1,0:T(8,128)(2,1)S(1)} %get-tuple-element.72), channel_id=1, source_target_pairs={{0,3},{1,2},{2,1},{3,0},{4,7},{5,6},{6,5},{7,4},{8,11},{9,10},{10,... | collective-permute-start | bytes 1966088 | tf_op jit(solution)/shard_map/ppermute | solution.py:740
  29.2 7.0 %collective-permute-start.13 = (bf16[160,512]{1,0:T(8,128)(2,1)S(1)}, bf16[160,512]{1,0:T(8,128)(2,1)S(1)}, u32[]{:S(2)}, u32[]{:S(2)}) collective-permute-start(bf16[160,512]{1,0:T(8,128)(2,1)S(1)} %collective-permute-done.4.refs_15_), channel_id=1, source_target_pairs={{0,4},{4,0},{8,12},{12,8},{16,20},{20,16},{24,28},{28,24},{1,5},{5... | collective-permute-start | bytes 491528 | tf_op jit(solution)/shard_map/ppermute | solution.py:743
  75.3 38.0 %collective-permute-start.18 = (bf16[320,2048]{1,0:T(8,128)(2,1)}, bf16[320,2048]{1,0:T(8,128)(2,1)S(1)}, u32[]{:S(2)}, u32[]{:S(2)}) collective-permute-start(bf16[320,2048]{1,0:T(8,128)(2,1)} %get-tuple-element.89), channel_id=1, source_target_pairs={{0,1},{1,0},{2,3},{3,2},{4,5},{5,4},{6,7},{7,6},{8,9},{9,8},{10,11... | collective-permute-start | bytes 3932168 | tf_op jit(solution)/shard_map/ppermute | solution.py:740
  75.7 37.5 %collective-permute-start.17 = (bf16[160,2048]{1,0:T(8,128)(2,1)}, bf16[160,2048]{1,0:T(8,128)(2,1)S(1)}, u32[]{:S(2)}, u32[]{:S(2)}) collective-permute-start(bf16[160,2048]{1,0:T(8,128)(2,1)} %get-tuple-element.88), channel_id=1, source_target_pairs={{0,2},{1,3},{2,0},{3,1},{4,6},{5,7},{6,4},{7,5},{8,10},{9,11},{10,... | collective-permute-start | bytes 1966088 | tf_op jit(solution)/shard_map/ppermute | solution.py:740
  77.7 35.6 %collective-permute-start.19 = (bf16[160,2048]{1,0:T(8,128)(2,1)}, bf16[160,2048]{1,0:T(8,128)(2,1)S(1)}, u32[]{:S(2)}, u32[]{:S(2)}) collective-permute-start(bf16[160,2048]{1,0:T(8,128)(2,1)} %get-tuple-element.90), channel_id=1, source_target_pairs={{0,3},{1,2},{2,1},{3,0},{4,7},{5,6},{6,5},{7,4},{8,11},{9,10},{10,... | collective-permute-start | bytes 1966088 | tf_op jit(solution)/shard_map/ppermute | solution.py:740
  113.9 30.6 %collective-permute-start.29 = (bf16[160,2048]{1,0:T(8,128)(2,1)}, bf16[160,2048]{1,0:T(8,128)(2,1)S(1)}, u32[]{:S(2)}, u32[]{:S(2)}) collective-permute-start(bf16[160,2048]{1,0:T(8,128)(2,1)} %get-tuple-element.116), channel_id=1, source_target_pairs={{0,2},{1,3},{2,0},{3,1},{4,6},{5,7},{6,4},{7,5},{8,10},{9,11},{10,... | collective-permute-start | bytes 1966088 | tf_op jit(solution)/shard_map/ppermute | solution.py:740
  115.6 29.8 %collective-permute-start.28 = (bf16[160,2048]{1,0:T(8,128)(2,1)}, bf16[160,2048]{1,0:T(8,128)(2,1)S(1)}, u32[]{:S(2)}, u32[]{:S(2)}) collective-permute-start(bf16[160,2048]{1,0:T(8,128)(2,1)} %get-tuple-element.113), channel_id=1, source_target_pairs={{0,3},{1,2},{2,1},{3,0},{4,7},{5,6},{6,5},{7,4},{8,11},{9,10},{10,... | collective-permute-start | bytes 1966088 | tf_op jit(solution)/shard_map/ppermute | solution.py:740
  122.0 6.8 %collective-permute-start.24 = (bf16[168,512]{1,0:T(8,128)(2,1)S(1)}, bf16[168,512]{1,0:T(8,128)(2,1)S(1)}, u32[]{:S(2)}, u32[]{:S(2)}) collective-permute-start(bf16[168,512]{1,0:T(8,128)(2,1)S(1)} %get-tuple-element.100), channel_id=1, source_target_pairs={{0,8},{4,12},{8,0},{12,4},{16,24},{20,28},{24,16},{28,20},{1,9},{5... | collective-permute-start | bytes 516104 | tf_op jit(solution)/shard_map/ppermute | solution.py:743
  124.0 7.2 %collective-permute-start.23 = (bf16[168,512]{1,0:T(8,128)(2,1)S(1)}, bf16[168,512]{1,0:T(8,128)(2,1)S(1)}, u32[]{:S(2)}, u32[]{:S(2)}) collective-permute-start(bf16[168,512]{1,0:T(8,128)(2,1)S(1)} %get-tuple-element.99), channel_id=1, source_target_pairs={{0,4},{4,0},{8,12},{12,8},{16,20},{20,16},{24,28},{28,24},{1,5},{5... | collective-permute-start | bytes 516104 | tf_op jit(solution)/shard_map/ppermute | solution.py:743
  125.5 9.4 %collective-permute-start.22 = (bf16[168,512]{1,0:T(8,128)(2,1)S(1)}, bf16[168,512]{1,0:T(8,128)(2,1)S(1)}, u32[]{:S(2)}, u32[]{:S(2)}) collective-permute-start(bf16[168,512]{1,0:T(8,128)(2,1)S(1)} %get-tuple-element.96), channel_id=1, source_target_pairs={{0,4},{4,0},{8,12},{12,8},{16,20},{20,16},{24,28},{28,24},{1,5},{5... | collective-permute-start | bytes 516104 | tf_op jit(solution)/shard_map/ppermute | solution.py:743
  128.9 7.3 %collective-permute-start.27 = (bf16[168,512]{1,0:T(8,128)(2,1)S(1)}, bf16[168,512]{1,0:T(8,128)(2,1)S(1)}, u32[]{:S(2)}, u32[]{:S(2)}) collective-permute-start(bf16[168,512]{1,0:T(8,128)(2,1)S(1)} %get-tuple-element.110), channel_id=1, source_target_pairs={{0,8},{4,12},{8,0},{12,4},{16,24},{20,28},{24,16},{28,20},{1,9},{5... | collective-permute-start | bytes 516104 | tf_op jit(solution)/shard_map/ppermute | solution.py:743
  131.8 5.9 %collective-permute-start.26 = (bf16[168,512]{1,0:T(8,128)(2,1)S(1)}, bf16[168,512]{1,0:T(8,128)(2,1)S(1)}, u32[]{:S(2)}, u32[]{:S(2)}) collective-permute-start(bf16[168,512]{1,0:T(8,128)(2,1)S(1)} %get-tuple-element.108), channel_id=1, source_target_pairs={{0,4},{4,0},{8,12},{12,8},{16,20},{20,16},{24,28},{28,24},{1,5},{5... | collective-permute-start | bytes 516104 | tf_op jit(solution)/shard_map/ppermute | solution.py:743
  134.9 5.4 %collective-permute-start.25 = (bf16[168,512]{1,0:T(8,128)(2,1)S(1)}, bf16[168,512]{1,0:T(8,128)(2,1)S(1)}, u32[]{:S(2)}, u32[]{:S(2)}) collective-permute-start(bf16[168,512]{1,0:T(8,128)(2,1)S(1)} %get-tuple-element.104), channel_id=1, source_target_pairs={{0,8},{4,12},{8,0},{12,4},{16,24},{20,28},{24,16},{28,20},{1,9},{5... | collective-permute-start | bytes 516104 | tf_op jit(solution)/shard_map/ppermute | solution.py:743
  140.6 9.0 %collective-permute-start.30 = (bf16[168,512]{1,0:T(8,128)(2,1)S(1)}, bf16[168,512]{1,0:T(8,128)(2,1)S(1)}, u32[]{:S(2)}, u32[]{:S(2)}) collective-permute-start(bf16[168,512]{1,0:T(8,128)(2,1)S(1)} %third.1), channel_id=1, source_target_pairs={{0,16},{4,20},{8,24},{12,28},{16,0},{20,4},{24,8},{28,12},{1,17},{... | collective-permute-start | bytes 516104 | tf_op jit(solution)/shard_map/ppermute | solution.py:743
  (29 other events, 262.7 us)

commit v5 on v4

--- a/solution.py
+++ b/solution.py
@@ -17,6 +17,7 @@
 FTILE = 1024
 TILES = LEN // TILE
 CALLS = 2
+REST = (3, 5, 2, 6, 1, 4, 0)
 GROUPS = ((0, 1, 4), (2, 5, 6), (3, 7))
 f32 = jnp.float32
 bf16 = jnp.bfloat16
@@ -46,12 +47,12 @@
     hid, to_sib, dx_px, dx_pd, dx_own = refs[:5]
     refs = refs[5:]
     if last:
-        acc_own, acc_sib, refs = refs[0], refs[1], refs[2:]
+        own_first, own_rest, sib_first, sib_rest, refs = *refs[:4], refs[4:]
     else:
         acc_out, refs = refs[0], refs[1:]
     if first:
         w_out, refs = refs[0], refs[1:]
-    (xb, wb, cb, pre, gp, zs, fs, os_, cbs, ct, hs, hb, dp, dxb, accb, ab, small, nxt, sums, cl, ca_t, id_b, bb, sem, rsem) = refs
+    (xb, wb, cb, pre, gp, zs, fs, os_, cbs, ct, hs, hb, dp, dxb, accb, ab, nxt, sums, cl, ca_t, id_b, bb, sem, rsem, osem) = refs
     D = 4 * C
     tl = C - LANES
     steps = n // SEGS
@@ -300,6 +301,18 @@
 
         return lax.fori_loop(0, TILES, body, state)
 
+    def combine_segments(gain, total, backward):
+        sub = lax.broadcasted_iota(jnp.int32, (SEGS, LANES), 0)
+        d = 1
+        while d < SEGS:
+            there = sub < SEGS - d if backward else sub >= d
+            by = SEGS - d if backward else d
+            total = total + gain * jnp.where(there, pltpu.roll(total, by, 0), 0.0)
+            gain = gain * jnp.where(there, pltpu.roll(gain, by, 0), 1.0)
+            d *= 2
+        there = sub < SEGS - 1 if backward else sub >= 1
+        return jnp.where(there, pltpu.roll(total, SEGS - 1 if backward else 1, 0), 0.0)
+
     def row(r):
         b = [jnp.broadcast_to(bb[0:1, q * LANES : (q + 1) * LANES], (SEGS, LANES)) for q in range(8)]
         inputs = weights = None
@@ -312,24 +325,10 @@
                 copy.start()
             if r == 1 and not first:
                 pltpu.make_async_copy(acc_in, accb, sem.at[2]).wait()
-        for q in range(3):
-            small[0, :, cols[q]] = gain[q]
-            small[1, :, cols[q]] = total[q]
-        run = jnp.zeros((1, 3 * LANES), f32)
-        for s in range(SEGS):
-            small[2, s : s + 1, :] = run
-            run = small[0, s : s + 1, :] * run + small[1, s : s + 1, :]
-        cell = tuple(small[2, :, cols[q]] for q in range(3))
+        cell = tuple(combine_segments(gain[q], total[q], False) for q in range(3))
         cell, back, gain = scan(functools.partial(cell_step, r), (cell, (zero,) * 3, (one,) * 3))
-        for q in range(3):
-            small[0, :, cols[q]] = back[q]
-            small[1, :, cols[q]] = gain[q]
-            small[3, :, cols[q]] = fs[0:SEGS, cols[q]] * ca_t[r, 0:SEGS, :]
-        run = jnp.zeros((1, 3 * LANES), f32)
-        for s in range(SEGS - 1, -1, -1):
-            small[2, s : s + 1, :] = run
-            run = small[3, s : s + 1, :] * (small[0, s : s + 1, :] + small[1, s : s + 1, :] * run)
-        later = tuple(small[2, :, cols[q]] for q in range(3))
+        enter = [fs[0:SEGS, cols[q]] * ca_t[r, 0:SEGS, :] for q in range(3)]
+        later = tuple(combine_segments(enter[q] * gain[q], enter[q] * back[q], True) for q in range(3))
         scan(functools.partial(grad_step, r), later, weights)
 
     arrive(0)
@@ -386,35 +385,51 @@
                 ab[2 * D :, (q - 4) * LANES : (q - 3) * LANES] = in_two(s)
         accb[2 * D :, at] = jnp.broadcast_to(s, (SEGS, LANES))
 
-    def own_copy(i):
+    def blocks_out(source, first_out, rest_out, which, i):
         at = pl.ds(pl.multiple_of(i * TILE, TILE), TILE)
-        return pltpu.make_async_copy(accb.at[:, at], (acc_own if last else acc_out).at[:, at], sem.at[4 + i])
-
-    def sib_copy(i):
+        copies = []
+        for place_in, j in enumerate((7,) + REST):
+            rows_in = pl.ds(pl.multiple_of((place ^ j) * C, 32), C)
+            out = first_out.at[0:C, at] if j == 7 else rest_out.at[(place_in - 1) * C : place_in * C, at]
+            copies.append(pltpu.make_async_copy(source.at[rows_in, at], out, osem.at[which, i, place_in]))
+        return copies
+
+    def own_copies(i):
+        if last:
+            return blocks_out(accb, own_first, own_rest, 0, i)
         at = pl.ds(pl.multiple_of(i * TILE, TILE), TILE)
-        return pltpu.make_async_copy(ab.at[:, at], acc_sib.at[:, at], sem.at[2 + i])
+        return [pltpu.make_async_copy(accb.at[:, at], acc_out.at[:, at], sem.at[4 + i])]
 
     def own_step(i, _):
         v, at = weight_tile(end, i, not (first and rows == 1))
         accb[0 : 2 * D, at] = v
-        own_copy(i).start()
+        for copy in own_copies(i):
+            copy.start()
         return 0
 
     def sib_step(i, _):
         v, _ = weight_tile(end, half // TILE + i, not (first and rows == 1))
         ab[0 : 2 * D, pl.ds(pl.multiple_of(i * TILE, TILE), TILE)] = v.astype(bf16)
-        sib_copy(i).start()
+        for copy in blocks_out(ab, sib_first, sib_rest, 1, i):
+            copy.start()
         return 0
 
     own_tiles = (half if last else 2 * half) // TILE
+    tails = []
     if last:
+        tails = [
+            go(accb.at[2 * D :, 0:half], own_first.at[C:], 4),
+            go(ab.at[2 * D :], sib_first.at[C:], 5),
+        ]
         lax.fori_loop(0, half // TILE, sib_step, 0)
     lax.fori_loop(0, own_tiles, own_step, 0)
     for i in range(own_tiles):
-        own_copy(i).wait()
+        tails += own_copies(i)
     if last:
         for i in range(half // TILE):
-            sib_copy(i).wait()
+            tails += blocks_out(ab, sib_first, sib_rest, 1, i)
+    for copy in tails:
+        copy.wait()
     if first:
         pltpu.make_async_copy(wb, w_out, sem.at[0]).wait()
     for r in range(rows):
@@ -439,7 +454,8 @@
         if not last:
             alias[len(ins) - 2] = 5
     if last:
-        outs += [shape((2 * D + SEGS, N // 2), f32), shape((2 * D + SEGS, N // 2), bf16)]
+        for kind in (f32, bf16):
+            outs += [shape((C + SEGS, N // 2), kind), shape((len(REST) * C, N // 2), kind)]
     else:
         outs += [shape((2 * D + SEGS, N), f32)]
     if first:
@@ -462,7 +478,6 @@
             pltpu.VMEM((D, T), bf16),
             pltpu.VMEM((2 * D + SEGS, N), f32),
             pltpu.VMEM((2 * D + SEGS, N // 2), bf16),
-            pltpu.VMEM((4, SEGS, w3), f32),
             pltpu.VMEM((D, LANES), f32),
             pltpu.VMEM((SEGS, N), f32),
             pltpu.VMEM((rows, SEGS, n), f32),
@@ -471,6 +486,7 @@
             pltpu.VMEM((SEGS, N), f32),
             pltpu.SemaphoreType.DMA((8 + 2 * parts,)),
             pltpu.SemaphoreType.DMA((rows, 18)),
+            pltpu.SemaphoreType.DMA((2, N // 2 // TILE, 1 + len(REST))),
         ]
     )
     return pl.pallas_call(
@@ -610,91 +626,73 @@
     return v[0:1] + v[1:2]
 
 
-def split_kernel(C, own, other, s7, s3, s5, s2, k0, k1, k4, k6, bufs, kept, sem):
-    place = lax.axis_index("dp")
-    b = own[8 * C : 8 * C + 1, :] + from_two(other[8 * C :, :])
-    two = in_two(b)
-    copies = []
-    for i, (j, out) in enumerate(((7, s7), (3, s3), (5, s5), (2, s2))):
-        at = pl.ds(pl.multiple_of((place ^ j) * C, 32), C)
-        bufs[i, 0:C] = (own[at, :] + other[at, :].astype(f32)).astype(bf16)
-        bufs[i, C:] = two
-        copies.append(pltpu.make_async_copy(bufs.at[i], out, sem.at[i]))
-        copies[-1].start()
-    for i, (j, out) in enumerate(((6, k6), (1, k1), (4, k4), (0, k0))):
-        at = pl.ds(pl.multiple_of((place ^ j) * C, 32), C)
-        kept[i, 0:C] = own[at, :] + other[at, :].astype(f32)
-        kept[i, C : C + 8] = jnp.broadcast_to(b, (8, b.shape[1]))
-        copies.append(pltpu.make_async_copy(kept.at[i, 0 : C + 8], out, sem.at[4 + i]))
-        copies[-1].start()
-    for copy in copies:
-        copy.wait()
-
-
-def split(C, own, other):
+def leaf_kernel(C, own, other, out, b_out):
+    b = own[C : C + 1] + from_two(other[C:])
+    out[0:C] = (own[0:C] + other[0:C].astype(f32)).astype(bf16)
+    out[C:] = in_two(b)
+    b_out[...] = jnp.broadcast_to(b, (SEGS, b.shape[1]))
+
+
+def leaf(C, own, other):
     half = own.shape[1]
-    message = jax.ShapeDtypeStruct((C + SEGS, half), bf16)
+    return pl.pallas_call(
+        functools.partial(leaf_kernel, C),
+        out_shape=[jax.ShapeDtypeStruct((C + SEGS, half), bf16), jax.ShapeDtypeStruct((SEGS, half), f32)],
+        in_specs=[VMEM] * 2,
+        out_specs=[VMEM] * 2,
+        compiler_params=pltpu.CompilerParams(vmem_limit_bytes=4 << 20),
+        cost_estimate=pl.CostEstimate(flops=1, bytes_accessed=1, transcendentals=0),
+        name="leaf",
+    )(own, other)
+
+
+def split_kernel(C, own, other, b, s3, s5, s2, k6, k1, k4, k0):
+    two = in_two(b[0:1])
+    for i, out in enumerate((s3, s5, s2, k6, k1, k4, k0)):
+        at = slice(i * C, (i + 1) * C)
+        v = own[at, :] + other[at, :].astype(f32)
+        if i < 3:
+            out[0:C] = v.astype(bf16)
+            out[C:] = two
+        else:
+            out[0:C] = v
+            out[C:] = b[...]
+
+
+def split(C, own, other, b):
+    half = own.shape[1]
+    shape = (C + SEGS, half)
     return pl.pallas_call(
         functools.partial(split_kernel, C),
-        out_shape=[message] * 4 + [jax.ShapeDtypeStruct((C + 8, half), f32)] * 4,
-        in_specs=[VMEM] * 2,
-        out_specs=[HBM] * 8,
-        scratch_shapes=[
-            pltpu.VMEM((4, C + SEGS, half), bf16),
-            pltpu.VMEM((4, C + 8, half), f32),
-            pltpu.SemaphoreType.DMA((8,)),
-        ],
+        out_shape=[jax.ShapeDtypeStruct(shape, bf16)] * 3 + [jax.ShapeDtypeStruct(shape, f32)] * 4,
+        in_specs=[VMEM] * 3,
+        out_specs=[VMEM] * 7,
         compiler_params=pltpu.CompilerParams(vmem_limit_bytes=16 << 20),
         cost_estimate=pl.CostEstimate(flops=1, bytes_accessed=1, transcendentals=0),
         name="split",
-    )(own, other)
-
-
-def second_kernel(C, k6, k1, r7, r3, s6, s1, bufs, sem):
-    b = k6[C : C + 1]
-    copies = []
-    for i, (k, r, out) in enumerate(((k6, r7, s6), (k1, r3, s1))):
-        bufs[i, 0:C] = (k[0:C] + r[0:C].astype(f32)).astype(bf16)
-        bufs[i, C:] = in_two(b + from_two(r[C:]))
-        copies.append(pltpu.make_async_copy(bufs.at[i], out, sem.at[i]))
-        copies[-1].start()
-    for copy in copies:
-        copy.wait()
-
-
-def second(C, k6, k1, r7, r3):
-    message = jax.ShapeDtypeStruct(r7.shape, bf16)
+    )(own, other, b)
+
+
+def pass_on_kernel(C, kept, *refs):
+    out = refs[-1]
+    v, b = kept[0:C], kept[C : C + 1]
+    for r in refs[:-1]:
+        v = v + r[0:C].astype(f32)
+        b = b + from_two(r[C:])
+    out[0:C] = v.astype(bf16)
+    out[C:] = in_two(b)
+
+
+def pass_on(C, kept, *received):
     return pl.pallas_call(
-        functools.partial(second_kernel, C),
-        out_shape=[message] * 2,
-        in_specs=[VMEM] * 4,
-        out_specs=[HBM] * 2,
-        scratch_shapes=[pltpu.VMEM((2,) + r7.shape, bf16), pltpu.SemaphoreType.DMA((2,))],
+        functools.partial(pass_on_kernel, C),
+        out_shape=jax.ShapeDtypeStruct(kept.shape, bf16),
+        in_specs=[VMEM] * (1 + len(received)),
+        out_specs=VMEM,
         compiler_params=pltpu.CompilerParams(vmem_limit_bytes=4 << 20),
         cost_estimate=pl.CostEstimate(flops=1, bytes_accessed=1, transcendentals=0),
-        name="second",
-    )(k6, k1, r7, r3)
-
-
-def third_kernel(C, k4, r5, r6, s4, buf, sem):
-    buf[0:C] = (k4[0:C] + r5[0:C].astype(f32) + r6[0:C].astype(f32)).astype(bf16)
-    buf[C:] = in_two(k4[C : C + 1] + from_two(r5[C:]) + from_two(r6[C:]))
-    copy = pltpu.make_async_copy(buf, s4, sem)
-    copy.start()
-    copy.wait()
-
-
-def third(C, k4, r5, r6):
-    return pl.pallas_call(
-        functools.partial(third_kernel, C),
-        out_shape=jax.ShapeDtypeStruct(r6.shape, bf16),
-        in_specs=[VMEM] * 3,
-        out_specs=HBM,
-        scratch_shapes=[pltpu.VMEM(r6.shape, bf16), pltpu.SemaphoreType.DMA],
-        compiler_params=pltpu.CompilerParams(vmem_limit_bytes=4 << 20),
-        cost_estimate=pl.CostEstimate(flops=1, bytes_accessed=1, transcendentals=0),
-        name="third",
-    )(k4, r5, r6)
+        name="pass_on",
+    )(kept, *received)
 
 
 def total_kernel(C, k0, r2, r1, r4, grad, bias, buf, b_buf, sem):
@@ -764,13 +762,12 @@
     g[6] = dp_move(g4, 2)
     g[5] = dp_move(g4, 1)
     w_sib = [to_sibling(GROUPS[0])]
-    biases = [b_own, chan_move(after(b_own, g[4]), 1)]
+    biases = [b_own, chan_move(after(b_own, far), 1)]
     g[2] = dp_move(own, 2)
     g6, g1 = lax.optimization_barrier((g[6], g[1], near, scot))[:2]
     g[7] = dp_move(g6, 1)
     g[3] = dp_move(g1, 2)
     w_sib.append(to_sibling(GROUPS[1]))
-    g[3] = after(g[3], far)
     w_sib.append(to_sibling(GROUPS[2]))
     w = [g[j] for j in range(parts)] + w_sib
     for k in range(1, CALLS):
@@ -780,16 +777,17 @@
     acc = hid = grad = None
     moved = []
     for k in range(CALLS):
-        out = layer(
-            k, CALLS, rows, parts, C, n, tokens, sib, cotangent, scot, ids, biases, xs[k], w, acc, hid
-        )
+        out = layer(k, CALLS, rows, parts, C, n, tokens, sib, cotangent, scot, ids, biases, xs[k], w, acc, hid)
         if k == 0:
             w = out[-1]
         hid, to_sib, d_px, d_pd, own, acc = out[:6]
         if k == CALLS - 1:
+            own_first, own_rest, sib_first, sib_rest = out[5:9]
             got = [v for m in moved for v in m[1:]]
-            to_sib, d_px, d_pd, acc_sib = lax.optimization_barrier((to_sib, d_px, d_pd, out[6], *got))[:4]
-            acc_sib = chan_move(acc_sib, 1)
+            to_sib, d_px, d_pd, sib_first, sib_rest = lax.optimization_barrier(
+                (to_sib, d_px, d_pd, sib_first, sib_rest, *got)
+            )[:5]
+            sib_first, sib_rest = chan_move(sib_first, 1), chan_move(sib_rest, 1)
         else:
             to_sib, d_px, d_pd = lax.optimization_barrier((to_sib, d_px, d_pd, *xs[k + 1]))[:3]
         moved.append((own, chan_move(d_px, 2), chan_move(to_sib, 1), chan_move(d_pd, 3)))
@@ -802,17 +800,20 @@
         else:
             grad, hid = finish(k, rows, False, C, n, total, after(from_sib, *others), from_pd, grad, hid)
 
-    s7, s3, s5, s2, k0, k1, k4, k6 = split(C, acc, after(acc_sib, moved[-1][2]))
-    r7, r3, r5 = dp_move(s7, 1), dp_move(s3, 2), dp_move(s5, 1)
+    s7, b = leaf(C, own_first, sib_first)
+    r7 = dp_move(s7, 1)
     for k in range(CALLS - 1):
         end(k, True, s7)
-    s6, s1 = second(C, k6, k1, r7, after(r3, grad))
-    r6, r1, r2 = dp_move(s6, 2), dp_move(s1, 1), dp_move(after(s2, r3), 2)
+    s3, s5, s2, k6, k1, k4, k0 = split(C, own_rest, after(sib_rest, moved[-1][2], grad), b)
+    r3, r5 = dp_move(s3, 2), dp_move(s5, 1)
+    s6 = pass_on(C, k6, r7)
+    r6 = dp_move(s6, 2)
     for k in range(CALLS - 1):
         end(k, False, s6, r5)
-    s4 = third(C, k4, r5, after(r6, grad, r1, r2))
+    r1, r2 = dp_move(pass_on(C, k1, after(r3, grad)), 1), dp_move(after(s2, r3), 2)
+    s4 = pass_on(C, k4, r5, after(r6, grad))
     r4 = dp_move(s4, 4)
-    end(CALLS - 1, True, s4)
+    end(CALLS - 1, True, s4, r1)
     end(CALLS - 1, False, s4)
     weight_grad, bias_grad = total_sum(C, k0, r2, r1, after(r4, grad))
     return (hid, grad, weight_grad, bias_grad)

time: 151 us -> 146 us (0.967)
  waiting for transfers between devices: 33.2 us -> 29.5 us
  Pallas kernels: 79.9 us -> 78 us
    ppermute x14, waiting for transfers between devices: 23.4 us -> 12.6 us  [dp_move(): return lax.ppermute(v, 'dp', [(i, i ^ j) for i in range(parts)])]
    ppermute x17 -> x18, waiting for transfers between devices: 9.82 us -> 17 us  [chan_move(): return lax.ppermute(v, 'chan', [(i, i ^ j) for i in range(chan)])]
    pallas_call x3 -> x5, Pallas kernels: 2.67 us -> 0.43 us  [the longest x1 0.19 us: split(): pl.pallas_call(functools.partial(split_kernel, C), out_shape=[jax.ShapeDt...]
    ppermute x17 -> x18, starting transfers between devices: 10.8 us -> 10.7 us  [chan_move(): return lax.ppermute(v, 'chan', [(i, i ^ j) for i in range(chan)])]
    unnamed x44 -> x48, local copies, waits for them, and re-layouts: 4.26 us -> 4.26 us
  transfers between devices with their start and end apart: 31 -> 32, of which waited for: 15 -> 11; matrix products, arithmetic and copies ran while one was open for 0% -> 0% of each run, Pallas kernels for 52% -> 53%
where the time goes in v5:
time: 146 us
  Pallas kernels  78 us (53%)
  starting transfers between devices  33.2 us (23%)
  waiting for transfers between devices  29.5 us (20%)
  local copies, waits for them, and re-layouts  4.26 us (3%)
    pallas_call x2, Pallas kernels, layer(): pl.pallas_call(functools.partial(layer_kernel, k, calls, rows, parts, C,...  71.3 us
    ppermute x14, starting transfers between devices, dp_move(): return lax.ppermute(v, 'dp', [(i, i ^ j) for i in range(parts)])  22.5 us
    ppermute x18, waiting for transfers between devices, chan_move(): return lax.ppermute(v, 'chan', [(i, i ^ j) for i in range(chan)])  17 us
    ppermute x14, waiting for transfers between devices, dp_move(): return lax.ppermute(v, 'dp', [(i, i ^ j) for i in range(parts)])  12.6 us
    ppermute x18, starting transfers between devices, chan_move(): return lax.ppermute(v, 'chan', [(i, i ^ j) for i in range(chan)])  10.7 us
    unnamed x48, local copies, waits for them, and re-layouts  4.26 us
    pallas_call x4, Pallas kernels, finish(): pl.pallas_call(functools.partial(finish_kernel, k, rows, mine, C, n), out...  4.07 us
  transfers between devices with their start and end apart: 32, of which 11 were waited for; matrix products, arithmetic and copies ran while one was open for 0% of the time, Pallas kernels for 53%

profile of v5, /device:TPU:0, one launch (start us, length us, event | category | flops | bytes accessed | tf_op | source)
XLA Modules:
  0.0 146.3 jit_solution(16754065634371747899)
XLA Ops:
  1.2 1.7 %copy-done = bf16[160,8192]{1,0:T(8,128)(2,1)S(1)} copy-done((bf16[160,8192]{1,0:T(8,128)(2,1)S(1)}, bf16[160,8192]{1,0:T(8,128)(2,1)}, u32[]{:S(2)}) %copy-start) | copy-done | bytes 2621464
  3.5 3.0 %collective-permute-start.8 = (bf16[160,2048]{1,0:T(8,128)(2,1)S(1)}, bf16[160,2048]{1,0:T(8,128)(2,1)S(1)}, u32[]{:S(2)}, u32[]{:S(2)}) collective-permute-start(bf16[160,2048]{1,0:T(8,128)(2,1)S(1)} %get-tuple-element.65), channel_id=1, source_target_pairs={{0,2},{1,3},{2,0},{3,1},{4,6},{5,7},{6,4},{7,5},{8,10},{9,11},{10,... | collective-permute-start | bytes 1966088 | tf_op jit(solution)/shard_map/ppermute | solution.py:738
  6.7 2.7 %collective-permute-start.4 = (bf16[160,512]{1,0:T(8,128)(2,1)S(1)}, bf16[160,512]{1,0:T(8,128)(2,1)S(1)}, u32[]{:S(2)}, u32[]{:S(2)}) collective-permute-start(bf16[160,512]{1,0:T(8,128)(2,1)S(1)} %get-tuple-element.75.refs_9_), channel_id=1, source_target_pairs={{0,16},{4,20},{8,24},{12,28},{16,0},{20,4},{24,8},{28,12},{1,17},{... | collective-permute-start | bytes 491528 | tf_op jit(solution)/shard_map/ppermute | solution.py:741
  9.4 1.5 %collective-permute-start.9 = (bf16[160,512]{1,0:T(8,128)(2,1)S(1)}, bf16[160,512]{1,0:T(8,128)(2,1)S(1)}, u32[]{:S(2)}, u32[]{:S(2)}) collective-permute-start(bf16[160,512]{1,0:T(8,128)(2,1)S(1)} %get-tuple-element.75.refs_9_), channel_id=1, source_target_pairs={{0,4},{4,0},{8,12},{12,8},{16,20},{20,16},{24,28},{28,24},{1,5},{5... | collective-permute-start | bytes 491528 | tf_op jit(solution)/shard_map/ppermute | solution.py:741
  10.9 6.2 %collective-permute-done.4.refs_13_ = bf16[160,512]{1,0:T(8,128)(2,1)S(1)} collective-permute-done((bf16[160,512]{1,0:T(8,128)(2,1)S(1)}, bf16[160,512]{1,0:T(8,128)(2,1)S(1)}, u32[]{:S(2)}, u32[]{:S(2)}) %collective-permute-start.4) | collective-permute-done | bytes 163872 | tf_op jit(solution)/shard_map/ppermute | solution.py:741
  18.0 1.2 collective-permute-start.10
  19.2 2.8 %collective-permute-done.8.refs_7_ = bf16[160,2048]{1,0:T(8,128)(2,1)S(1)} collective-permute-done((bf16[160,2048]{1,0:T(8,128)(2,1)S(1)}, bf16[160,2048]{1,0:T(8,128)(2,1)S(1)}, u32[]{:S(2)}, u32[]{:S(2)}) %collective-permute-start.8) | collective-permute-done | bytes 655392 | tf_op jit(solution)/shard_map/ppermute | solution.py:738
  22.0 2.1 %collective-permute-start.12 = (bf16[160,512]{1,0:T(8,128)(2,1)S(1)}, bf16[160,512]{1,0:T(8,128)(2,1)S(1)}, u32[]{:S(2)}, u32[]{:S(2)}) collective-permute-start(bf16[160,512]{1,0:T(8,128)(2,1)S(1)} %collective-permute-done.4.refs_13_), channel_id=1, source_target_pairs={{0,4},{4,0},{8,12},{12,8},{16,20},{20,16},{24,28},{28,24},{1,5},{5... | collective-permute-start | bytes 491528 | tf_op jit(solution)/shard_map/ppermute | solution.py:741
  24.2 1.5 %collective-permute-start.11 = (bf16[160,512]{1,0:T(8,128)(2,1)S(1)}, bf16[160,512]{1,0:T(8,128)(2,1)S(1)}, u32[]{:S(2)}, u32[]{:S(2)}) collective-permute-start(bf16[160,512]{1,0:T(8,128)(2,1)S(1)} %collective-permute-done.9.refs_10_), channel_id=1, source_target_pairs={{0,8},{4,12},{8,0},{12,4},{16,24},{20,28},{24,16},{28,20},{1,9},{5... | collective-permute-start | bytes 491528 | tf_op jit(solution)/shard_map/ppermute | solution.py:741
  28.7 2.2 %collective-permute-done.11.refs_12_ = bf16[160,512]{1,0:T(8,128)(2,1)S(1)} collective-permute-done((bf16[160,512]{1,0:T(8,128)(2,1)S(1)}, bf16[160,512]{1,0:T(8,128)(2,1)S(1)}, u32[]{:S(2)}, u32[]{:S(2)}) %collective-permute-start.11) | collective-permute-done | bytes 163872 | tf_op jit(solution)/shard_map/ppermute | solution.py:741
  31.7 4.0 %collective-permute-done.2.refs_8_ = bf16[160,2048]{1,0:T(8,128)(2,1)S(1)} collective-permute-done((bf16[160,2048]{1,0:T(8,128)(2,1)S(1)}, bf16[160,2048]{1,0:T(8,128)(2,1)S(1)}, u32[]{:S(2)}, u32[]{:S(2)}) %collective-permute-start.2) | collective-permute-done | bytes 655392 | tf_op jit(solution)/shard_map/ppermute | solution.py:738
  38.8 35.6 %layer.2 = (bf16[160,8192]{1,0:T(8,128)(2,1)}, bf16[320,2048]{1,0:T(8,128)(2,1)}, bf16[160,2048]{1,0:T(8,128)(2,1)}, bf16[160,2048]{1,0:T(8,128)(2,1)}, bf16[160...) custom-call(bf16[160,8192]{1,0:T(8,128)(2,1)} %refs_0_.3, bf16[160,8192]{1,0:T(8,128)(2,1)} %copy-done.9, ...), custom_call_target="tpu_custom_call" | custom-call | flops 1 | bytes 1 | tf_op jit(solution)/shard_map/layer/pallas_call | solution.py:492
  74.8 2.1 %collective-permute-start.17 = (bf16[160,2048]{1,0:T(8,128)(2,1)}, bf16[160,2048]{1,0:T(8,128)(2,1)S(1)}, u32[]{:S(2)}, u32[]{:S(2)}) collective-permute-start(bf16[160,2048]{1,0:T(8,128)(2,1)} %get-tuple-element.89), channel_id=1, source_target_pairs={{0,2},{1,3},{2,0},{3,1},{4,6},{5,7},{6,4},{7,5},{8,10},{9,11},{10,... | collective-permute-start | bytes 1966088 | tf_op jit(solution)/shard_map/ppermute | solution.py:738
  76.8 35.7 %layer.3 = (bf16[160,8192]{1,0:T(8,128)(2,1)}, bf16[320,2048]{1,0:T(8,128)(2,1)}, bf16[160,2048]{1,0:T(8,128)(2,1)}, bf16[160,2048]{1,0:T(8,128)(2,1)}, bf16[160...) custom-call(bf16[160,8192]{1,0:T(8,128)(2,1)} %refs_0_.3, ...), custom_call_target="tpu_custom_call", output_to_operand_aliasing={{0}: (11, {})} | custom-call | flops 1 | bytes 1 | tf_op jit(solution)/shard_map/layer/pallas_call | solution.py:492
  113.3 2.0 %collective-permute-start.29 = (bf16[160,2048]{1,0:T(8,128)(2,1)}, bf16[160,2048]{1,0:T(8,128)(2,1)S(1)}, u32[]{:S(2)}, u32[]{:S(2)}) collective-permute-start(bf16[160,2048]{1,0:T(8,128)(2,1)} %get-tuple-element.116), channel_id=1, source_target_pairs={{0,2},{1,3},{2,0},{3,1},{4,6},{5,7},{6,4},{7,5},{8,10},{9,11},{10,... | collective-permute-start | bytes 1966088 | tf_op jit(solution)/shard_map/ppermute | solution.py:738
  115.3 2.5 %collective-permute-done.22.other = bf16[168,512]{1,0:T(8,128)(2,1)S(1)} collective-permute-done((bf16[168,512]{1,0:T(8,128)(2,1)}, bf16[168,512]{1,0:T(8,128)(2,1)S(1)}, u32[]{:S(2)}, u32[]{:S(2)}) %collective-permute-start.22) | collective-permute-done | bytes 172064 | tf_op jit(solution)/shard_map/ppermute | solution.py:738
  118.8 1.8 %collective-permute-start.24 = (bf16[168,512]{1,0:T(8,128)(2,1)S(1)}, bf16[168,512]{1,0:T(8,128)(2,1)S(1)}, u32[]{:S(2)}, u32[]{:S(2)}) collective-permute-start(bf16[168,512]{1,0:T(8,128)(2,1)S(1)} %get-tuple-element.98), channel_id=1, source_target_pairs={{0,4},{4,0},{8,12},{12,8},{16,20},{20,16},{24,28},{28,24},{1,5},{5... | collective-permute-start | bytes 516104 | tf_op jit(solution)/shard_map/ppermute | solution.py:741
  122.1 1.8 %collective-permute-start.27 = (bf16[168,512]{1,0:T(8,128)(2,1)S(1)}, bf16[168,512]{1,0:T(8,128)(2,1)S(1)}, u32[]{:S(2)}, u32[]{:S(2)}) collective-permute-start(bf16[168,512]{1,0:T(8,128)(2,1)S(1)} %get-tuple-element.113), channel_id=1, source_target_pairs={{0,8},{4,12},{8,0},{12,4},{16,24},{20,28},{24,16},{28,20},{1,9},{5... | collective-permute-start | bytes 516104 | tf_op jit(solution)/shard_map/ppermute | solution.py:741
  124.0 2.1 %collective-permute-done.24.refs_0_ = bf16[168,512]{1,0:T(8,128)(2,1)S(1)} collective-permute-done((bf16[168,512]{1,0:T(8,128)(2,1)S(1)}, bf16[168,512]{1,0:T(8,128)(2,1)S(1)}, u32[]{:S(2)}, u32[]{:S(2)}) %collective-permute-start.24) | collective-permute-done | bytes 172064 | tf_op jit(solution)/shard_map/ppermute | solution.py:741
  126.1 1.9 %collective-permute-start.25 = (bf16[168,512]{1,0:T(8,128)(2,1)S(1)}, bf16[168,512]{1,0:T(8,128)(2,1)S(1)}, u32[]{:S(2)}, u32[]{:S(2)}) collective-permute-start(bf16[168,512]{1,0:T(8,128)(2,1)S(1)} %pass_on.3), channel_id=1, source_target_pairs={{0,8},{4,12},{8,0},{12,4},{16,24},{20,28},{24,16},{28,20},{1,9},{5... | collective-permute-start | bytes 516104 | tf_op jit(solution)/shard_map/ppermute | solution.py:741
  130.4 1.8 %collective-permute-start.28 = (bf16[168,512]{1,0:T(8,128)(2,1)S(1)}, bf16[168,512]{1,0:T(8,128)(2,1)S(1)}, u32[]{:S(2)}, u32[]{:S(2)}) collective-permute-start(bf16[168,512]{1,0:T(8,128)(2,1)S(1)} %pass_on.5), channel_id=1, source_target_pairs={{0,4},{4,0},{8,12},{12,8},{16,20},{20,16},{24,28},{28,24},{1,5},{5... | collective-permute-start | bytes 516104 | tf_op jit(solution)/shard_map/ppermute | solution.py:741
  132.3 2.7 %collective-permute-start.31 = (bf16[168,512]{1,0:T(8,128)(2,1)S(1)}, bf16[168,512]{1,0:T(8,128)(2,1)S(1)}, u32[]{:S(2)}, u32[]{:S(2)}) collective-permute-start(bf16[168,512]{1,0:T(8,128)(2,1)S(1)} %pass_on.4), channel_id=1, source_target_pairs={{0,16},{4,20},{8,24},{12,28},{16,0},{20,4},{24,8},{28,12},{1,17},{... | collective-permute-start | bytes 516104 | tf_op jit(solution)/shard_map/ppermute | solution.py:741
  134.9 1.6 %collective-permute-start.30 = (bf16[168,512]{1,0:T(8,128)(2,1)S(1)}, bf16[168,512]{1,0:T(8,128)(2,1)S(1)}, u32[]{:S(2)}, u32[]{:S(2)}) collective-permute-start(bf16[168,512]{1,0:T(8,128)(2,1)S(1)} %get-tuple-element.122), channel_id=1, source_target_pairs={{0,8},{4,12},{8,0},{12,4},{16,24},{20,28},{24,16},{28,20},{1,9},{5... | collective-permute-start | bytes 516104 | tf_op jit(solution)/shard_map/ppermute | solution.py:741
  137.5 6.5 %collective-permute-done.26.far = bf16[160,2048]{1,0:T(8,128)(2,1)S(1)} collective-permute-done((bf16[160,2048]{1,0:T(8,128)(2,1)}, bf16[160,2048]{1,0:T(8,128)(2,1)S(1)}, u32[]{:S(2)}, u32[]{:S(2)}) %collective-permute-start.26) | collective-permute-done | bytes 655392 | tf_op jit(solution)/shard_map/ppermute | solution.py:738
  (106 shorter events, 18.1 us)
Async XLA Ops:
  0.6 16.5 %collective-permute-start = (bf16[160,8192]{1,0:T(8,128)(2,1)}, bf16[160,8192]{1,0:T(8,128)(2,1)S(1)}, u32[]{:S(2)}, u32[]{:S(2)}) collective-permute-start(bf16[160,8192]{1,0:T(8,128)(2,1)} %refs_0_.3), channel_id=1, source_target_pairs={{0,1},{1,0},{2,3},{3,2},{4,5},{5,4},{6,7},{7,6},{8,9},{9,8},{10,11... | collective-permute-start | bytes 7864328 | tf_op jit(solution)/shard_map/ppermute | solution.py:738
  1.1 23.0 %collective-permute-start.1 = (bf16[160,8192]{1,0:T(8,128)(2,1)}, bf16[160,8192]{1,0:T(8,128)(2,1)S(1)}, u32[]{:S(2)}, u32[]{:S(2)}) collective-permute-start(bf16[160,8192]{1,0:T(8,128)(2,1)} %refs_2_.3), channel_id=1, source_target_pairs={{0,1},{1,0},{2,3},{3,2},{4,5},{5,4},{6,7},{7,6},{8,9},{9,8},{10,11... | collective-permute-start | bytes 7864328 | tf_op jit(solution)/shard_map/ppermute | solution.py:738
  3.5 18.5 %collective-permute-start.8 = (bf16[160,2048]{1,0:T(8,128)(2,1)S(1)}, bf16[160,2048]{1,0:T(8,128)(2,1)S(1)}, u32[]{:S(2)}, u32[]{:S(2)}) collective-permute-start(bf16[160,2048]{1,0:T(8,128)(2,1)S(1)} %get-tuple-element.65), channel_id=1, source_target_pairs={{0,2},{1,3},{2,0},{3,1},{4,6},{5,7},{6,4},{7,5},{8,10},{9,11},{10,... | collective-permute-start | bytes 1966088 | tf_op jit(solution)/shard_map/ppermute | solution.py:738
  6.7 10.4 %collective-permute-start.4 = (bf16[160,512]{1,0:T(8,128)(2,1)S(1)}, bf16[160,512]{1,0:T(8,128)(2,1)S(1)}, u32[]{:S(2)}, u32[]{:S(2)}) collective-permute-start(bf16[160,512]{1,0:T(8,128)(2,1)S(1)} %get-tuple-element.75.refs_9_), channel_id=1, source_target_pairs={{0,16},{4,20},{8,24},{12,28},{16,0},{20,4},{24,8},{28,12},{1,17},{... | collective-permute-start | bytes 491528 | tf_op jit(solution)/shard_map/ppermute | solution.py:741
  9.4 8.6 %collective-permute-start.9 = (bf16[160,512]{1,0:T(8,128)(2,1)S(1)}, bf16[160,512]{1,0:T(8,128)(2,1)S(1)}, u32[]{:S(2)}, u32[]{:S(2)}) collective-permute-start(bf16[160,512]{1,0:T(8,128)(2,1)S(1)} %get-tuple-element.75.refs_9_), channel_id=1, source_target_pairs={{0,4},{4,0},{8,12},{12,8},{16,20},{20,16},{24,28},{28,24},{1,5},{5... | collective-permute-start | bytes 491528 | tf_op jit(solution)/shard_map/ppermute | solution.py:741
  17.1 18.6 %collective-permute-start.2 = (bf16[160,2048]{1,0:T(8,128)(2,1)S(1)}, bf16[160,2048]{1,0:T(8,128)(2,1)S(1)}, u32[]{:S(2)}, u32[]{:S(2)}) collective-permute-start(bf16[160,2048]{1,0:T(8,128)(2,1)S(1)} %get-tuple-element.68), channel_id=1, source_target_pairs={{0,3},{1,2},{2,1},{3,0},{4,7},{5,6},{6,5},{7,4},{8,11},{9,10},{10,... | collective-permute-start | bytes 1966088 | tf_op jit(solution)/shard_map/ppermute | solution.py:738
  17.1 7.1 %collective-permute-start.5 = (bf16[160,512]{1,0:T(8,128)(2,1)S(1)}, bf16[160,512]{1,0:T(8,128)(2,1)S(1)}, u32[]{:S(2)}, u32[]{:S(2)}) collective-permute-start(bf16[160,512]{1,0:T(8,128)(2,1)S(1)} %collective-permute-done.4.refs_13_), channel_id=1, source_target_pairs={{0,8},{4,12},{8,0},{12,4},{16,24},{20,28},{24,16},{28,20},{1,9},{5... | collective-permute-start | bytes 491528 | tf_op jit(solution)/shard_map/ppermute | solution.py:741
  18.0 9.8 %collective-permute-start.10 = (bf16[160,512]{1,0:T(8,128)(2,1)S(1)}, bf16[160,512]{1,0:T(8,128)(2,1)S(1)}, u32[]{:S(2)}, u32[]{:S(2)}) collective-permute-start(bf16[160,512]{1,0:T(8,128)(2,1)S(1)} %get-tuple-element.75.refs_9_), channel_id=1, source_target_pairs={{0,8},{4,12},{8,0},{12,4},{16,24},{20,28},{24,16},{28,20},{1,9},{5... | collective-permute-start | bytes 491528 | tf_op jit(solution)/shard_map/ppermute | solution.py:741
  22.0 6.5 %collective-permute-start.12 = (bf16[160,512]{1,0:T(8,128)(2,1)S(1)}, bf16[160,512]{1,0:T(8,128)(2,1)S(1)}, u32[]{:S(2)}, u32[]{:S(2)}) collective-permute-start(bf16[160,512]{1,0:T(8,128)(2,1)S(1)} %collective-permute-done.4.refs_13_), channel_id=1, source_target_pairs={{0,4},{4,0},{8,12},{12,8},{16,20},{20,16},{24,28},{28,24},{1,5},{5... | collective-permute-start | bytes 491528 | tf_op jit(solution)/shard_map/ppermute | solution.py:741
  24.2 6.7 %collective-permute-start.11 = (bf16[160,512]{1,0:T(8,128)(2,1)S(1)}, bf16[160,512]{1,0:T(8,128)(2,1)S(1)}, u32[]{:S(2)}, u32[]{:S(2)}) collective-permute-start(bf16[160,512]{1,0:T(8,128)(2,1)S(1)} %collective-permute-done.9.refs_10_), channel_id=1, source_target_pairs={{0,8},{4,12},{8,0},{12,4},{16,24},{20,28},{24,16},{28,20},{1,9},{5... | collective-permute-start | bytes 491528 | tf_op jit(solution)/shard_map/ppermute | solution.py:741
  27.8 46.7 %collective-permute-start.6 = (bf16[160,2048]{1,0:T(8,128)(2,1)S(1)}, bf16[160,2048]{1,0:T(8,128)(2,1)}, u32[]{:S(2)}, u32[]{:S(2)}) collective-permute-start(bf16[160,2048]{1,0:T(8,128)(2,1)S(1)} %get-tuple-element.73), channel_id=1, source_target_pairs={{0,2},{1,3},{2,0},{3,1},{4,6},{5,7},{6,4},{7,5},{8,10},{9,11},{10,... | collective-permute-start | bytes 1966088 | tf_op jit(solution)/shard_map/ppermute | solution.py:738
  28.6 45.9 %collective-permute-start.7 = (bf16[160,2048]{1,0:T(8,128)(2,1)S(1)}, bf16[160,2048]{1,0:T(8,128)(2,1)}, u32[]{:S(2)}, u32[]{:S(2)}) collective-permute-start(bf16[160,2048]{1,0:T(8,128)(2,1)S(1)} %get-tuple-element.74), channel_id=1, source_target_pairs={{0,3},{1,2},{2,1},{3,0},{4,7},{5,6},{6,5},{7,4},{8,11},{9,10},{10,... | collective-permute-start | bytes 1966088 | tf_op jit(solution)/shard_map/ppermute | solution.py:738
  74.5 38.1 %collective-permute-start.18 = (bf16[320,2048]{1,0:T(8,128)(2,1)}, bf16[320,2048]{1,0:T(8,128)(2,1)S(1)}, u32[]{:S(2)}, u32[]{:S(2)}) collective-permute-start(bf16[320,2048]{1,0:T(8,128)(2,1)} %get-tuple-element.90), channel_id=1, source_target_pairs={{0,1},{1,0},{2,3},{3,2},{4,5},{5,4},{6,7},{7,6},{8,9},{9,8},{10,11... | collective-permute-start | bytes 3932168 | tf_op jit(solution)/shard_map/ppermute | solution.py:738
  74.8 37.8 %collective-permute-start.17 = (bf16[160,2048]{1,0:T(8,128)(2,1)}, bf16[160,2048]{1,0:T(8,128)(2,1)S(1)}, u32[]{:S(2)}, u32[]{:S(2)}) collective-permute-start(bf16[160,2048]{1,0:T(8,128)(2,1)} %get-tuple-element.89), channel_id=1, source_target_pairs={{0,2},{1,3},{2,0},{3,1},{4,6},{5,7},{6,4},{7,5},{8,10},{9,11},{10,... | collective-permute-start | bytes 1966088 | tf_op jit(solution)/shard_map/ppermute | solution.py:738
  76.8 35.7 %collective-permute-start.19 = (bf16[160,2048]{1,0:T(8,128)(2,1)}, bf16[160,2048]{1,0:T(8,128)(2,1)S(1)}, u32[]{:S(2)}, u32[]{:S(2)}) collective-permute-start(bf16[160,2048]{1,0:T(8,128)(2,1)} %get-tuple-element.91), channel_id=1, source_target_pairs={{0,3},{1,2},{2,1},{3,0},{4,7},{5,6},{6,5},{7,4},{8,11},{9,10},{10,... | collective-permute-start | bytes 1966088 | tf_op jit(solution)/shard_map/ppermute | solution.py:738
  112.6 9.0 %collective-permute-start.20 = (bf16[320,2048]{1,0:T(8,128)(2,1)}, bf16[320,2048]{1,0:T(8,128)(2,1)S(1)}, u32[]{:S(2)}, u32[]{:S(2)}) collective-permute-start(bf16[320,2048]{1,0:T(8,128)(2,1)} %get-tuple-element.92), channel_id=1, source_target_pairs={{0,1},{1,0},{2,3},{3,2},{4,5},{5,4},{6,7},{7,6},{8,9},{9,8},{10,11... | collective-permute-start | bytes 3932168 | tf_op jit(solution)/shard_map/ppermute | solution.py:738
  112.8 8.8 %collective-permute-start.21 = (bf16[1120,512]{1,0:T(8,128)(2,1)}, bf16[1120,512]{1,0:T(8,128)(2,1)S(1)}, u32[]{:S(2)}, u32[]{:S(2)}) collective-permute-start(bf16[1120,512]{1,0:T(8,128)(2,1)} %get-tuple-element.94), channel_id=1, source_target_pairs={{0,1},{1,0},{2,3},{3,2},{4,5},{5,4},{6,7},{7,6},{8,9},{9,8},{10,11... | collective-permute-start | bytes 3440648 | tf_op jit(solution)/shard_map/ppermute | solution.py:738
  113.3 23.2 %collective-permute-start.29 = (bf16[160,2048]{1,0:T(8,128)(2,1)}, bf16[160,2048]{1,0:T(8,128)(2,1)S(1)}, u32[]{:S(2)}, u32[]{:S(2)}) collective-permute-start(bf16[160,2048]{1,0:T(8,128)(2,1)} %get-tuple-element.116), channel_id=1, source_target_pairs={{0,2},{1,3},{2,0},{3,1},{4,6},{5,7},{6,4},{7,5},{8,10},{9,11},{10,... | collective-permute-start | bytes 1966088 | tf_op jit(solution)/shard_map/ppermute | solution.py:738
  115.3 28.7 %collective-permute-start.26 = (bf16[160,2048]{1,0:T(8,128)(2,1)}, bf16[160,2048]{1,0:T(8,128)(2,1)S(1)}, u32[]{:S(2)}, u32[]{:S(2)}) collective-permute-start(bf16[160,2048]{1,0:T(8,128)(2,1)} %get-tuple-element.110), channel_id=1, source_target_pairs={{0,3},{1,2},{2,1},{3,0},{4,7},{5,6},{6,5},{7,4},{8,11},{9,10},{10,... | collective-permute-start | bytes 1966088 | tf_op jit(solution)/shard_map/ppermute | solution.py:738
  118.8 7.3 %collective-permute-start.24 = (bf16[168,512]{1,0:T(8,128)(2,1)S(1)}, bf16[168,512]{1,0:T(8,128)(2,1)S(1)}, u32[]{:S(2)}, u32[]{:S(2)}) collective-permute-start(bf16[168,512]{1,0:T(8,128)(2,1)S(1)} %get-tuple-element.98), channel_id=1, source_target_pairs={{0,4},{4,0},{8,12},{12,8},{16,20},{20,16},{24,28},{28,24},{1,5},{5... | collective-permute-start | bytes 516104 | tf_op jit(solution)/shard_map/ppermute | solution.py:741
  121.8 7.4 %collective-permute-start.23 = (bf16[168,512]{1,0:T(8,128)(2,1)S(1)}, bf16[168,512]{1,0:T(8,128)(2,1)S(1)}, u32[]{:S(2)}, u32[]{:S(2)}) collective-permute-start(bf16[168,512]{1,0:T(8,128)(2,1)S(1)} %get-tuple-element.103), channel_id=1, source_target_pairs={{0,4},{4,0},{8,12},{12,8},{16,20},{20,16},{24,28},{28,24},{1,5},{5... | collective-permute-start | bytes 516104 | tf_op jit(solution)/shard_map/ppermute | solution.py:741
  122.1 8.2 %collective-permute-start.27 = (bf16[168,512]{1,0:T(8,128)(2,1)S(1)}, bf16[168,512]{1,0:T(8,128)(2,1)S(1)}, u32[]{:S(2)}, u32[]{:S(2)}) collective-permute-start(bf16[168,512]{1,0:T(8,128)(2,1)S(1)} %get-tuple-element.113), channel_id=1, source_target_pairs={{0,8},{4,12},{8,0},{12,4},{16,24},{20,28},{24,16},{28,20},{1,9},{5... | collective-permute-start | bytes 516104 | tf_op jit(solution)/shard_map/ppermute | solution.py:741
  132.3 12.8 %collective-permute-start.31 = (bf16[168,512]{1,0:T(8,128)(2,1)S(1)}, bf16[168,512]{1,0:T(8,128)(2,1)S(1)}, u32[]{:S(2)}, u32[]{:S(2)}) collective-permute-start(bf16[168,512]{1,0:T(8,128)(2,1)S(1)} %pass_on.4), channel_id=1, source_target_pairs={{0,16},{4,20},{8,24},{12,28},{16,0},{20,4},{24,8},{28,12},{1,17},{... | collective-permute-start | bytes 516104 | tf_op jit(solution)/shard_map/ppermute | solution.py:741
  134.9 10.2 %collective-permute-start.30 = (bf16[168,512]{1,0:T(8,128)(2,1)S(1)}, bf16[168,512]{1,0:T(8,128)(2,1)S(1)}, u32[]{:S(2)}, u32[]{:S(2)}) collective-permute-start(bf16[168,512]{1,0:T(8,128)(2,1)S(1)} %get-tuple-element.122), channel_id=1, source_target_pairs={{0,8},{4,12},{8,0},{12,4},{16,24},{20,28},{24,16},{28,20},{1,9},{5... | collective-permute-start | bytes 516104 | tf_op jit(solution)/shard_map/ppermute | solution.py:741
  (32 other events, 263.3 us)

commit v6 on v5

--- a/solution.py
+++ b/solution.py
@@ -12,7 +12,7 @@
 LANES = 128
 SEGS = 8
 PAD = 8
-TILE = 256
+TILE = 512
 UNROLL = 16
 FTILE = 1024
 TILES = LEN // TILE
@@ -326,10 +326,10 @@
             if r == 1 and not first:
                 pltpu.make_async_copy(acc_in, accb, sem.at[2]).wait()
         cell = tuple(combine_segments(gain[q], total[q], False) for q in range(3))
-        cell, back, gain = scan(functools.partial(cell_step, r), (cell, (zero,) * 3, (one,) * 3))
+        cell, back, gain = scan(functools.partial(cell_step, r), (cell, (zero,) * 3, (one,) * 3), weights)
         enter = [fs[0:SEGS, cols[q]] * ca_t[r, 0:SEGS, :] for q in range(3)]
         later = tuple(combine_segments(enter[q] * gain[q], enter[q] * back[q], True) for q in range(3))
-        scan(functools.partial(grad_step, r), later, weights)
+        scan(functools.partial(grad_step, r), later)
 
     arrive(0)
     lax.fori_loop(0, D // rb, lambda i, _: (previous(0, i), 0)[1], 0)

time: 146 us -> 145 us (level)
  transfers between devices with their start and end apart: 32 -> 32, of which waited for: 11 -> 11; matrix products, arithmetic and copies ran while one was open for 0% -> 0% of each run, Pallas kernels for 53% -> 52%
where the time goes in v6:
time: 145 us
  Pallas kernels  76.6 us (53%)
  starting transfers between devices  33.3 us (23%)
  waiting for transfers between devices  29.4 us (20%)
  local copies, waits for them, and re-layouts  4.26 us (3%)
    pallas_call x2, Pallas kernels, layer(): pl.pallas_call(functools.partial(layer_kernel, k, calls, rows, parts, C,...  69.8 us
    ppermute x14, starting transfers between devices, dp_move(): return lax.ppermute(v, 'dp', [(i, i ^ j) for i in range(parts)])  22.6 us
    ppermute x18, waiting for transfers between devices, chan_move(): return lax.ppermute(v, 'chan', [(i, i ^ j) for i in range(chan)])  16.9 us
    ppermute x14, waiting for transfers between devices, dp_move(): return lax.ppermute(v, 'dp', [(i, i ^ j) for i in range(parts)])  12.5 us
    ppermute x18, starting transfers between devices, chan_move(): return lax.ppermute(v, 'chan', [(i, i ^ j) for i in range(chan)])  10.7 us
    unnamed x48, local copies, waits for them, and re-layouts  4.26 us
    pallas_call x4, Pallas kernels, finish(): pl.pallas_call(functools.partial(finish_kernel, k, rows, mine, C, n), out...  4.07 us
  transfers between devices with their start and end apart: 32, of which 11 were waited for; matrix products, arithmetic and copies ran while one was open for 0% of the time, Pallas kernels for 52%

profile of v6, /device:TPU:0, one launch (start us, length us, event | category | flops | bytes accessed | tf_op | source)
XLA Modules:
  0.0 144.9 jit_solution(4171450012346690326)
XLA Ops:
  1.2 1.7 %copy-done = bf16[160,8192]{1,0:T(8,128)(2,1)S(1)} copy-done((bf16[160,8192]{1,0:T(8,128)(2,1)S(1)}, bf16[160,8192]{1,0:T(8,128)(2,1)}, u32[]{:S(2)}) %copy-start) | copy-done | bytes 2621464
  3.5 3.0 %collective-permute-start.8 = (bf16[160,2048]{1,0:T(8,128)(2,1)S(1)}, bf16[160,2048]{1,0:T(8,128)(2,1)S(1)}, u32[]{:S(2)}, u32[]{:S(2)}) collective-permute-start(bf16[160,2048]{1,0:T(8,128)(2,1)S(1)} %get-tuple-element.65), channel_id=1, source_target_pairs={{0,2},{1,3},{2,0},{3,1},{4,6},{5,7},{6,4},{7,5},{8,10},{9,11},{10,... | collective-permute-start | bytes 1966088 | tf_op jit(solution)/shard_map/ppermute | solution.py:738
  6.7 2.7 %collective-permute-start.4 = (bf16[160,512]{1,0:T(8,128)(2,1)S(1)}, bf16[160,512]{1,0:T(8,128)(2,1)S(1)}, u32[]{:S(2)}, u32[]{:S(2)}) collective-permute-start(bf16[160,512]{1,0:T(8,128)(2,1)S(1)} %get-tuple-element.75.refs_9_), channel_id=1, source_target_pairs={{0,16},{4,20},{8,24},{12,28},{16,0},{20,4},{24,8},{28,12},{1,17},{... | collective-permute-start | bytes 491528 | tf_op jit(solution)/shard_map/ppermute | solution.py:741
  9.4 1.5 %collective-permute-start.9 = (bf16[160,512]{1,0:T(8,128)(2,1)S(1)}, bf16[160,512]{1,0:T(8,128)(2,1)S(1)}, u32[]{:S(2)}, u32[]{:S(2)}) collective-permute-start(bf16[160,512]{1,0:T(8,128)(2,1)S(1)} %get-tuple-element.75.refs_9_), channel_id=1, source_target_pairs={{0,4},{4,0},{8,12},{12,8},{16,20},{20,16},{24,28},{28,24},{1,5},{5... | collective-permute-start | bytes 491528 | tf_op jit(solution)/shard_map/ppermute | solution.py:741
  10.9 6.2 %collective-permute-done.4.refs_13_ = bf16[160,512]{1,0:T(8,128)(2,1)S(1)} collective-permute-done((bf16[160,512]{1,0:T(8,128)(2,1)S(1)}, bf16[160,512]{1,0:T(8,128)(2,1)S(1)}, u32[]{:S(2)}, u32[]{:S(2)}) %collective-permute-start.4) | collective-permute-done | bytes 163872 | tf_op jit(solution)/shard_map/ppermute | solution.py:741
  18.0 1.2 collective-permute-start.10
  19.2 2.8 %collective-permute-done.8.refs_7_ = bf16[160,2048]{1,0:T(8,128)(2,1)S(1)} collective-permute-done((bf16[160,2048]{1,0:T(8,128)(2,1)S(1)}, bf16[160,2048]{1,0:T(8,128)(2,1)S(1)}, u32[]{:S(2)}, u32[]{:S(2)}) %collective-permute-start.8) | collective-permute-done | bytes 655392 | tf_op jit(solution)/shard_map/ppermute | solution.py:738
  22.0 2.1 %collective-permute-start.12 = (bf16[160,512]{1,0:T(8,128)(2,1)S(1)}, bf16[160,512]{1,0:T(8,128)(2,1)S(1)}, u32[]{:S(2)}, u32[]{:S(2)}) collective-permute-start(bf16[160,512]{1,0:T(8,128)(2,1)S(1)} %collective-permute-done.4.refs_13_), channel_id=1, source_target_pairs={{0,4},{4,0},{8,12},{12,8},{16,20},{20,16},{24,28},{28,24},{1,5},{5... | collective-permute-start | bytes 491528 | tf_op jit(solution)/shard_map/ppermute | solution.py:741
  24.2 1.5 %collective-permute-start.11 = (bf16[160,512]{1,0:T(8,128)(2,1)S(1)}, bf16[160,512]{1,0:T(8,128)(2,1)S(1)}, u32[]{:S(2)}, u32[]{:S(2)}) collective-permute-start(bf16[160,512]{1,0:T(8,128)(2,1)S(1)} %collective-permute-done.9.refs_10_), channel_id=1, source_target_pairs={{0,8},{4,12},{8,0},{12,4},{16,24},{20,28},{24,16},{28,20},{1,9},{5... | collective-permute-start | bytes 491528 | tf_op jit(solution)/shard_map/ppermute | solution.py:741
  28.7 2.2 %collective-permute-done.11.refs_12_ = bf16[160,512]{1,0:T(8,128)(2,1)S(1)} collective-permute-done((bf16[160,512]{1,0:T(8,128)(2,1)S(1)}, bf16[160,512]{1,0:T(8,128)(2,1)S(1)}, u32[]{:S(2)}, u32[]{:S(2)}) %collective-permute-start.11) | collective-permute-done | bytes 163872 | tf_op jit(solution)/shard_map/ppermute | solution.py:741
  31.7 4.0 %collective-permute-done.2.refs_8_ = bf16[160,2048]{1,0:T(8,128)(2,1)S(1)} collective-permute-done((bf16[160,2048]{1,0:T(8,128)(2,1)S(1)}, bf16[160,2048]{1,0:T(8,128)(2,1)S(1)}, u32[]{:S(2)}, u32[]{:S(2)}) %collective-permute-start.2) | collective-permute-done | bytes 655392 | tf_op jit(solution)/shard_map/ppermute | solution.py:738
  38.8 35.1 %layer.2 = (bf16[160,8192]{1,0:T(8,128)(2,1)}, bf16[320,2048]{1,0:T(8,128)(2,1)}, bf16[160,2048]{1,0:T(8,128)(2,1)}, bf16[160,2048]{1,0:T(8,128)(2,1)}, bf16[160...) custom-call(bf16[160,8192]{1,0:T(8,128)(2,1)} %refs_0_.3, bf16[160,8192]{1,0:T(8,128)(2,1)} %copy-done.9, ...), custom_call_target="tpu_custom_call" | custom-call | flops 1 | bytes 1 | tf_op jit(solution)/shard_map/layer/pallas_call | solution.py:492
  74.3 2.1 %collective-permute-start.17 = (bf16[160,2048]{1,0:T(8,128)(2,1)}, bf16[160,2048]{1,0:T(8,128)(2,1)S(1)}, u32[]{:S(2)}, u32[]{:S(2)}) collective-permute-start(bf16[160,2048]{1,0:T(8,128)(2,1)} %get-tuple-element.89), channel_id=1, source_target_pairs={{0,2},{1,3},{2,0},{3,1},{4,6},{5,7},{6,4},{7,5},{8,10},{9,11},{10,... | collective-permute-start | bytes 1966088 | tf_op jit(solution)/shard_map/ppermute | solution.py:738
  76.4 34.7 %layer.3 = (bf16[160,8192]{1,0:T(8,128)(2,1)}, bf16[320,2048]{1,0:T(8,128)(2,1)}, bf16[160,2048]{1,0:T(8,128)(2,1)}, bf16[160,2048]{1,0:T(8,128)(2,1)}, bf16[160...) custom-call(bf16[160,8192]{1,0:T(8,128)(2,1)} %refs_0_.3, ...), custom_call_target="tpu_custom_call", output_to_operand_aliasing={{0}: (11, {})} | custom-call | flops 1 | bytes 1 | tf_op jit(solution)/shard_map/layer/pallas_call | solution.py:492
  111.9 2.0 %collective-permute-start.29 = (bf16[160,2048]{1,0:T(8,128)(2,1)}, bf16[160,2048]{1,0:T(8,128)(2,1)S(1)}, u32[]{:S(2)}, u32[]{:S(2)}) collective-permute-start(bf16[160,2048]{1,0:T(8,128)(2,1)} %get-tuple-element.116), channel_id=1, source_target_pairs={{0,2},{1,3},{2,0},{3,1},{4,6},{5,7},{6,4},{7,5},{8,10},{9,11},{10,... | collective-permute-start | bytes 1966088 | tf_op jit(solution)/shard_map/ppermute | solution.py:738
  113.8 2.5 %collective-permute-done.22.other = bf16[168,512]{1,0:T(8,128)(2,1)S(1)} collective-permute-done((bf16[168,512]{1,0:T(8,128)(2,1)}, bf16[168,512]{1,0:T(8,128)(2,1)S(1)}, u32[]{:S(2)}, u32[]{:S(2)}) %collective-permute-start.22) | collective-permute-done | bytes 172064 | tf_op jit(solution)/shard_map/ppermute | solution.py:738
  117.4 1.9 %collective-permute-start.24 = (bf16[168,512]{1,0:T(8,128)(2,1)S(1)}, bf16[168,512]{1,0:T(8,128)(2,1)S(1)}, u32[]{:S(2)}, u32[]{:S(2)}) collective-permute-start(bf16[168,512]{1,0:T(8,128)(2,1)S(1)} %get-tuple-element.98), channel_id=1, source_target_pairs={{0,4},{4,0},{8,12},{12,8},{16,20},{20,16},{24,28},{28,24},{1,5},{5... | collective-permute-start | bytes 516104 | tf_op jit(solution)/shard_map/ppermute | solution.py:741
  120.7 1.9 %collective-permute-start.27 = (bf16[168,512]{1,0:T(8,128)(2,1)S(1)}, bf16[168,512]{1,0:T(8,128)(2,1)S(1)}, u32[]{:S(2)}, u32[]{:S(2)}) collective-permute-start(bf16[168,512]{1,0:T(8,128)(2,1)S(1)} %get-tuple-element.113), channel_id=1, source_target_pairs={{0,8},{4,12},{8,0},{12,4},{16,24},{20,28},{24,16},{28,20},{1,9},{5... | collective-permute-start | bytes 516104 | tf_op jit(solution)/shard_map/ppermute | solution.py:741
  122.6 2.0 %collective-permute-done.24.refs_0_ = bf16[168,512]{1,0:T(8,128)(2,1)S(1)} collective-permute-done((bf16[168,512]{1,0:T(8,128)(2,1)S(1)}, bf16[168,512]{1,0:T(8,128)(2,1)S(1)}, u32[]{:S(2)}, u32[]{:S(2)}) %collective-permute-start.24) | collective-permute-done | bytes 172064 | tf_op jit(solution)/shard_map/ppermute | solution.py:741
  124.7 1.9 %collective-permute-start.25 = (bf16[168,512]{1,0:T(8,128)(2,1)S(1)}, bf16[168,512]{1,0:T(8,128)(2,1)S(1)}, u32[]{:S(2)}, u32[]{:S(2)}) collective-permute-start(bf16[168,512]{1,0:T(8,128)(2,1)S(1)} %pass_on.3), channel_id=1, source_target_pairs={{0,8},{4,12},{8,0},{12,4},{16,24},{20,28},{24,16},{28,20},{1,9},{5... | collective-permute-start | bytes 516104 | tf_op jit(solution)/shard_map/ppermute | solution.py:741
  129.0 1.8 %collective-permute-start.28 = (bf16[168,512]{1,0:T(8,128)(2,1)S(1)}, bf16[168,512]{1,0:T(8,128)(2,1)S(1)}, u32[]{:S(2)}, u32[]{:S(2)}) collective-permute-start(bf16[168,512]{1,0:T(8,128)(2,1)S(1)} %pass_on.5), channel_id=1, source_target_pairs={{0,4},{4,0},{8,12},{12,8},{16,20},{20,16},{24,28},{28,24},{1,5},{5... | collective-permute-start | bytes 516104 | tf_op jit(solution)/shard_map/ppermute | solution.py:741
  130.9 2.7 %collective-permute-start.31 = (bf16[168,512]{1,0:T(8,128)(2,1)S(1)}, bf16[168,512]{1,0:T(8,128)(2,1)S(1)}, u32[]{:S(2)}, u32[]{:S(2)}) collective-permute-start(bf16[168,512]{1,0:T(8,128)(2,1)S(1)} %pass_on.4), channel_id=1, source_target_pairs={{0,16},{4,20},{8,24},{12,28},{16,0},{20,4},{24,8},{28,12},{1,17},{... | collective-permute-start | bytes 516104 | tf_op jit(solution)/shard_map/ppermute | solution.py:741
  133.5 1.6 %collective-permute-start.30 = (bf16[168,512]{1,0:T(8,128)(2,1)S(1)}, bf16[168,512]{1,0:T(8,128)(2,1)S(1)}, u32[]{:S(2)}, u32[]{:S(2)}) collective-permute-start(bf16[168,512]{1,0:T(8,128)(2,1)S(1)} %get-tuple-element.122), channel_id=1, source_target_pairs={{0,8},{4,12},{8,0},{12,4},{16,24},{20,28},{24,16},{28,20},{1,9},{5... | collective-permute-start | bytes 516104 | tf_op jit(solution)/shard_map/ppermute | solution.py:741
  136.1 6.5 %collective-permute-done.26.far = bf16[160,2048]{1,0:T(8,128)(2,1)S(1)} collective-permute-done((bf16[160,2048]{1,0:T(8,128)(2,1)}, bf16[160,2048]{1,0:T(8,128)(2,1)S(1)}, u32[]{:S(2)}, u32[]{:S(2)}) %collective-permute-start.26) | collective-permute-done | bytes 655392 | tf_op jit(solution)/shard_map/ppermute | solution.py:738
  (106 shorter events, 18.1 us)
Async XLA Ops:
  0.6 16.5 %collective-permute-start = (bf16[160,8192]{1,0:T(8,128)(2,1)}, bf16[160,8192]{1,0:T(8,128)(2,1)S(1)}, u32[]{:S(2)}, u32[]{:S(2)}) collective-permute-start(bf16[160,8192]{1,0:T(8,128)(2,1)} %refs_0_.3), channel_id=1, source_target_pairs={{0,1},{1,0},{2,3},{3,2},{4,5},{5,4},{6,7},{7,6},{8,9},{9,8},{10,11... | collective-permute-start | bytes 7864328 | tf_op jit(solution)/shard_map/ppermute | solution.py:738
  1.1 23.0 %collective-permute-start.1 = (bf16[160,8192]{1,0:T(8,128)(2,1)}, bf16[160,8192]{1,0:T(8,128)(2,1)S(1)}, u32[]{:S(2)}, u32[]{:S(2)}) collective-permute-start(bf16[160,8192]{1,0:T(8,128)(2,1)} %refs_2_.3), channel_id=1, source_target_pairs={{0,1},{1,0},{2,3},{3,2},{4,5},{5,4},{6,7},{7,6},{8,9},{9,8},{10,11... | collective-permute-start | bytes 7864328 | tf_op jit(solution)/shard_map/ppermute | solution.py:738
  3.5 18.5 %collective-permute-start.8 = (bf16[160,2048]{1,0:T(8,128)(2,1)S(1)}, bf16[160,2048]{1,0:T(8,128)(2,1)S(1)}, u32[]{:S(2)}, u32[]{:S(2)}) collective-permute-start(bf16[160,2048]{1,0:T(8,128)(2,1)S(1)} %get-tuple-element.65), channel_id=1, source_target_pairs={{0,2},{1,3},{2,0},{3,1},{4,6},{5,7},{6,4},{7,5},{8,10},{9,11},{10,... | collective-permute-start | bytes 1966088 | tf_op jit(solution)/shard_map/ppermute | solution.py:738
  6.7 10.4 %collective-permute-start.4 = (bf16[160,512]{1,0:T(8,128)(2,1)S(1)}, bf16[160,512]{1,0:T(8,128)(2,1)S(1)}, u32[]{:S(2)}, u32[]{:S(2)}) collective-permute-start(bf16[160,512]{1,0:T(8,128)(2,1)S(1)} %get-tuple-element.75.refs_9_), channel_id=1, source_target_pairs={{0,16},{4,20},{8,24},{12,28},{16,0},{20,4},{24,8},{28,12},{1,17},{... | collective-permute-start | bytes 491528 | tf_op jit(solution)/shard_map/ppermute | solution.py:741
  9.4 8.6 %collective-permute-start.9 = (bf16[160,512]{1,0:T(8,128)(2,1)S(1)}, bf16[160,512]{1,0:T(8,128)(2,1)S(1)}, u32[]{:S(2)}, u32[]{:S(2)}) collective-permute-start(bf16[160,512]{1,0:T(8,128)(2,1)S(1)} %get-tuple-element.75.refs_9_), channel_id=1, source_target_pairs={{0,4},{4,0},{8,12},{12,8},{16,20},{20,16},{24,28},{28,24},{1,5},{5... | collective-permute-start | bytes 491528 | tf_op jit(solution)/shard_map/ppermute | solution.py:741
  17.1 18.6 %collective-permute-start.2 = (bf16[160,2048]{1,0:T(8,128)(2,1)S(1)}, bf16[160,2048]{1,0:T(8,128)(2,1)S(1)}, u32[]{:S(2)}, u32[]{:S(2)}) collective-permute-start(bf16[160,2048]{1,0:T(8,128)(2,1)S(1)} %get-tuple-element.68), channel_id=1, source_target_pairs={{0,3},{1,2},{2,1},{3,0},{4,7},{5,6},{6,5},{7,4},{8,11},{9,10},{10,... | collective-permute-start | bytes 1966088 | tf_op jit(solution)/shard_map/ppermute | solution.py:738
  17.1 7.1 %collective-permute-start.5 = (bf16[160,512]{1,0:T(8,128)(2,1)S(1)}, bf16[160,512]{1,0:T(8,128)(2,1)S(1)}, u32[]{:S(2)}, u32[]{:S(2)}) collective-permute-start(bf16[160,512]{1,0:T(8,128)(2,1)S(1)} %collective-permute-done.4.refs_13_), channel_id=1, source_target_pairs={{0,8},{4,12},{8,0},{12,4},{16,24},{20,28},{24,16},{28,20},{1,9},{5... | collective-permute-start | bytes 491528 | tf_op jit(solution)/shard_map/ppermute | solution.py:741
  18.0 9.8 %collective-permute-start.10 = (bf16[160,512]{1,0:T(8,128)(2,1)S(1)}, bf16[160,512]{1,0:T(8,128)(2,1)S(1)}, u32[]{:S(2)}, u32[]{:S(2)}) collective-permute-start(bf16[160,512]{1,0:T(8,128)(2,1)S(1)} %get-tuple-element.75.refs_9_), channel_id=1, source_target_pairs={{0,8},{4,12},{8,0},{12,4},{16,24},{20,28},{24,16},{28,20},{1,9},{5... | collective-permute-start | bytes 491528 | tf_op jit(solution)/shard_map/ppermute | solution.py:741
  22.0 6.5 %collective-permute-start.12 = (bf16[160,512]{1,0:T(8,128)(2,1)S(1)}, bf16[160,512]{1,0:T(8,128)(2,1)S(1)}, u32[]{:S(2)}, u32[]{:S(2)}) collective-permute-start(bf16[160,512]{1,0:T(8,128)(2,1)S(1)} %collective-permute-done.4.refs_13_), channel_id=1, source_target_pairs={{0,4},{4,0},{8,12},{12,8},{16,20},{20,16},{24,28},{28,24},{1,5},{5... | collective-permute-start | bytes 491528 | tf_op jit(solution)/shard_map/ppermute | solution.py:741
  24.2 6.7 %collective-permute-start.11 = (bf16[160,512]{1,0:T(8,128)(2,1)S(1)}, bf16[160,512]{1,0:T(8,128)(2,1)S(1)}, u32[]{:S(2)}, u32[]{:S(2)}) collective-permute-start(bf16[160,512]{1,0:T(8,128)(2,1)S(1)} %collective-permute-done.9.refs_10_), channel_id=1, source_target_pairs={{0,8},{4,12},{8,0},{12,4},{16,24},{20,28},{24,16},{28,20},{1,9},{5... | collective-permute-start | bytes 491528 | tf_op jit(solution)/shard_map/ppermute | solution.py:741
  27.8 46.2 %collective-permute-start.6 = (bf16[160,2048]{1,0:T(8,128)(2,1)S(1)}, bf16[160,2048]{1,0:T(8,128)(2,1)}, u32[]{:S(2)}, u32[]{:S(2)}) collective-permute-start(bf16[160,2048]{1,0:T(8,128)(2,1)S(1)} %get-tuple-element.73), channel_id=1, source_target_pairs={{0,2},{1,3},{2,0},{3,1},{4,6},{5,7},{6,4},{7,5},{8,10},{9,11},{10,... | collective-permute-start | bytes 1966088 | tf_op jit(solution)/shard_map/ppermute | solution.py:738
  28.6 45.4 %collective-permute-start.7 = (bf16[160,2048]{1,0:T(8,128)(2,1)S(1)}, bf16[160,2048]{1,0:T(8,128)(2,1)}, u32[]{:S(2)}, u32[]{:S(2)}) collective-permute-start(bf16[160,2048]{1,0:T(8,128)(2,1)S(1)} %get-tuple-element.74), channel_id=1, source_target_pairs={{0,3},{1,2},{2,1},{3,0},{4,7},{5,6},{6,5},{7,4},{8,11},{9,10},{10,... | collective-permute-start | bytes 1966088 | tf_op jit(solution)/shard_map/ppermute | solution.py:738
  74.0 37.1 %collective-permute-start.18 = (bf16[320,2048]{1,0:T(8,128)(2,1)}, bf16[320,2048]{1,0:T(8,128)(2,1)S(1)}, u32[]{:S(2)}, u32[]{:S(2)}) collective-permute-start(bf16[320,2048]{1,0:T(8,128)(2,1)} %get-tuple-element.90), channel_id=1, source_target_pairs={{0,1},{1,0},{2,3},{3,2},{4,5},{5,4},{6,7},{7,6},{8,9},{9,8},{10,11... | collective-permute-start | bytes 3932168 | tf_op jit(solution)/shard_map/ppermute | solution.py:738
  74.3 36.8 %collective-permute-start.17 = (bf16[160,2048]{1,0:T(8,128)(2,1)}, bf16[160,2048]{1,0:T(8,128)(2,1)S(1)}, u32[]{:S(2)}, u32[]{:S(2)}) collective-permute-start(bf16[160,2048]{1,0:T(8,128)(2,1)} %get-tuple-element.89), channel_id=1, source_target_pairs={{0,2},{1,3},{2,0},{3,1},{4,6},{5,7},{6,4},{7,5},{8,10},{9,11},{10,... | collective-permute-start | bytes 1966088 | tf_op jit(solution)/shard_map/ppermute | solution.py:738
  76.4 34.7 %collective-permute-start.19 = (bf16[160,2048]{1,0:T(8,128)(2,1)}, bf16[160,2048]{1,0:T(8,128)(2,1)S(1)}, u32[]{:S(2)}, u32[]{:S(2)}) collective-permute-start(bf16[160,2048]{1,0:T(8,128)(2,1)} %get-tuple-element.91), channel_id=1, source_target_pairs={{0,3},{1,2},{2,1},{3,0},{4,7},{5,6},{6,5},{7,4},{8,11},{9,10},{10,... | collective-permute-start | bytes 1966088 | tf_op jit(solution)/shard_map/ppermute | solution.py:738
  111.1 9.1 %collective-permute-start.20 = (bf16[320,2048]{1,0:T(8,128)(2,1)}, bf16[320,2048]{1,0:T(8,128)(2,1)S(1)}, u32[]{:S(2)}, u32[]{:S(2)}) collective-permute-start(bf16[320,2048]{1,0:T(8,128)(2,1)} %get-tuple-element.92), channel_id=1, source_target_pairs={{0,1},{1,0},{2,3},{3,2},{4,5},{5,4},{6,7},{7,6},{8,9},{9,8},{10,11... | collective-permute-start | bytes 3932168 | tf_op jit(solution)/shard_map/ppermute | solution.py:738
  111.3 8.8 %collective-permute-start.21 = (bf16[1120,512]{1,0:T(8,128)(2,1)}, bf16[1120,512]{1,0:T(8,128)(2,1)S(1)}, u32[]{:S(2)}, u32[]{:S(2)}) collective-permute-start(bf16[1120,512]{1,0:T(8,128)(2,1)} %get-tuple-element.94), channel_id=1, source_target_pairs={{0,1},{1,0},{2,3},{3,2},{4,5},{5,4},{6,7},{7,6},{8,9},{9,8},{10,11... | collective-permute-start | bytes 3440648 | tf_op jit(solution)/shard_map/ppermute | solution.py:738
  111.9 23.2 %collective-permute-start.29 = (bf16[160,2048]{1,0:T(8,128)(2,1)}, bf16[160,2048]{1,0:T(8,128)(2,1)S(1)}, u32[]{:S(2)}, u32[]{:S(2)}) collective-permute-start(bf16[160,2048]{1,0:T(8,128)(2,1)} %get-tuple-element.116), channel_id=1, source_target_pairs={{0,2},{1,3},{2,0},{3,1},{4,6},{5,7},{6,4},{7,5},{8,10},{9,11},{10,... | collective-permute-start | bytes 1966088 | tf_op jit(solution)/shard_map/ppermute | solution.py:738
  113.8 28.7 %collective-permute-start.26 = (bf16[160,2048]{1,0:T(8,128)(2,1)}, bf16[160,2048]{1,0:T(8,128)(2,1)S(1)}, u32[]{:S(2)}, u32[]{:S(2)}) collective-permute-start(bf16[160,2048]{1,0:T(8,128)(2,1)} %get-tuple-element.110), channel_id=1, source_target_pairs={{0,3},{1,2},{2,1},{3,0},{4,7},{5,6},{6,5},{7,4},{8,11},{9,10},{10,... | collective-permute-start | bytes 1966088 | tf_op jit(solution)/shard_map/ppermute | solution.py:738
  117.4 7.2 %collective-permute-start.24 = (bf16[168,512]{1,0:T(8,128)(2,1)S(1)}, bf16[168,512]{1,0:T(8,128)(2,1)S(1)}, u32[]{:S(2)}, u32[]{:S(2)}) collective-permute-start(bf16[168,512]{1,0:T(8,128)(2,1)S(1)} %get-tuple-element.98), channel_id=1, source_target_pairs={{0,4},{4,0},{8,12},{12,8},{16,20},{20,16},{24,28},{28,24},{1,5},{5... | collective-permute-start | bytes 516104 | tf_op jit(solution)/shard_map/ppermute | solution.py:741
  120.4 7.4 %collective-permute-start.23 = (bf16[168,512]{1,0:T(8,128)(2,1)S(1)}, bf16[168,512]{1,0:T(8,128)(2,1)S(1)}, u32[]{:S(2)}, u32[]{:S(2)}) collective-permute-start(bf16[168,512]{1,0:T(8,128)(2,1)S(1)} %get-tuple-element.103), channel_id=1, source_target_pairs={{0,4},{4,0},{8,12},{12,8},{16,20},{20,16},{24,28},{28,24},{1,5},{5... | collective-permute-start | bytes 516104 | tf_op jit(solution)/shard_map/ppermute | solution.py:741
  120.7 8.2 %collective-permute-start.27 = (bf16[168,512]{1,0:T(8,128)(2,1)S(1)}, bf16[168,512]{1,0:T(8,128)(2,1)S(1)}, u32[]{:S(2)}, u32[]{:S(2)}) collective-permute-start(bf16[168,512]{1,0:T(8,128)(2,1)S(1)} %get-tuple-element.113), channel_id=1, source_target_pairs={{0,8},{4,12},{8,0},{12,4},{16,24},{20,28},{24,16},{28,20},{1,9},{5... | collective-permute-start | bytes 516104 | tf_op jit(solution)/shard_map/ppermute | solution.py:741
  130.9 12.8 %collective-permute-start.31 = (bf16[168,512]{1,0:T(8,128)(2,1)S(1)}, bf16[168,512]{1,0:T(8,128)(2,1)S(1)}, u32[]{:S(2)}, u32[]{:S(2)}) collective-permute-start(bf16[168,512]{1,0:T(8,128)(2,1)S(1)} %pass_on.4), channel_id=1, source_target_pairs={{0,16},{4,20},{8,24},{12,28},{16,0},{20,4},{24,8},{28,12},{1,17},{... | collective-permute-start | bytes 516104 | tf_op jit(solution)/shard_map/ppermute | solution.py:741
  133.5 10.1 %collective-permute-start.30 = (bf16[168,512]{1,0:T(8,128)(2,1)S(1)}, bf16[168,512]{1,0:T(8,128)(2,1)S(1)}, u32[]{:S(2)}, u32[]{:S(2)}) collective-permute-start(bf16[168,512]{1,0:T(8,128)(2,1)S(1)} %get-tuple-element.122), channel_id=1, source_target_pairs={{0,8},{4,12},{8,0},{12,4},{16,24},{20,28},{24,16},{28,20},{1,9},{5... | collective-permute-start | bytes 516104 | tf_op jit(solution)/shard_map/ppermute | solution.py:741
  (32 other events, 262.4 us)

commit v7 on v6

--- a/solution.py
+++ b/solution.py
@@ -814,8 +814,8 @@
     s4 = pass_on(C, k4, r5, after(r6, grad))
     r4 = dp_move(s4, 4)
     end(CALLS - 1, True, s4, r1)
-    end(CALLS - 1, False, s4)
     weight_grad, bias_grad = total_sum(C, k0, r2, r1, after(r4, grad))
+    end(CALLS - 1, False, weight_grad)
     return (hid, grad, weight_grad, bias_grad)
 
 

time: 145 us -> 144 us (level)
    ppermute x18, waiting for transfers between devices: 16.9 us -> 10.6 us  [chan_move(): return lax.ppermute(v, 'chan', [(i, i ^ j) for i in range(chan)])]
    ppermute x14, waiting for transfers between devices: 12.5 us -> 17.8 us  [dp_move(): return lax.ppermute(v, 'dp', [(i, i ^ j) for i in range(parts)])]
  transfers between devices with their start and end apart: 32 -> 32, of which waited for: 11 -> 13; matrix products, arithmetic and copies ran while one was open for 0% -> 0% of each run, Pallas kernels for 52% -> 53%
where the time goes in v7:
time: 144 us
  Pallas kernels  76.6 us (53%)
  starting transfers between devices  33.3 us (23%)
  waiting for transfers between devices  28.4 us (20%)
  local copies, waits for them, and re-layouts  4.26 us (3%)
    pallas_call x2, Pallas kernels, layer(): pl.pallas_call(functools.partial(layer_kernel, k, calls, rows, parts, C,...  69.8 us
    ppermute x14, starting transfers between devices, dp_move(): return lax.ppermute(v, 'dp', [(i, i ^ j) for i in range(parts)])  22.6 us
    ppermute x14, waiting for transfers between devices, dp_move(): return lax.ppermute(v, 'dp', [(i, i ^ j) for i in range(parts)])  17.8 us
    ppermute x18, starting transfers between devices, chan_move(): return lax.ppermute(v, 'chan', [(i, i ^ j) for i in range(chan)])  10.7 us
    ppermute x18, waiting for transfers between devices, chan_move(): return lax.ppermute(v, 'chan', [(i, i ^ j) for i in range(chan)])  10.6 us
    unnamed x48, local copies, waits for them, and re-layouts  4.26 us
    pallas_call x4, Pallas kernels, finish(): pl.pallas_call(functools.partial(finish_kernel, k, rows, mine, C, n), out...  4.07 us
  transfers between devices with their start and end apart: 32, of which 13 were waited for; matrix products, arithmetic and copies ran while one was open for 0% of the time, Pallas kernels for 53%

profile of v7, /device:TPU:0, one launch (start us, length us, event | category | flops | bytes accessed | tf_op | source)
XLA Modules:
  0.0 143.8 jit_solution(13312771330936730318)
XLA Ops:
  1.2 1.7 %copy-done = bf16[160,8192]{1,0:T(8,128)(2,1)S(1)} copy-done((bf16[160,8192]{1,0:T(8,128)(2,1)S(1)}, bf16[160,8192]{1,0:T(8,128)(2,1)}, u32[]{:S(2)}) %copy-start) | copy-done | bytes 2621464
  3.5 3.0 %collective-permute-start.8 = (bf16[160,2048]{1,0:T(8,128)(2,1)S(1)}, bf16[160,2048]{1,0:T(8,128)(2,1)S(1)}, u32[]{:S(2)}, u32[]{:S(2)}) collective-permute-start(bf16[160,2048]{1,0:T(8,128)(2,1)S(1)} %get-tuple-element.65), channel_id=1, source_target_pairs={{0,2},{1,3},{2,0},{3,1},{4,6},{5,7},{6,4},{7,5},{8,10},{9,11},{10,... | collective-permute-start | bytes 1966088 | tf_op jit(solution)/shard_map/ppermute | solution.py:738
  6.7 2.7 %collective-permute-start.4 = (bf16[160,512]{1,0:T(8,128)(2,1)S(1)}, bf16[160,512]{1,0:T(8,128)(2,1)S(1)}, u32[]{:S(2)}, u32[]{:S(2)}) collective-permute-start(bf16[160,512]{1,0:T(8,128)(2,1)S(1)} %get-tuple-element.75.refs_9_), channel_id=1, source_target_pairs={{0,16},{4,20},{8,24},{12,28},{16,0},{20,4},{24,8},{28,12},{1,17},{... | collective-permute-start | bytes 491528 | tf_op jit(solution)/shard_map/ppermute | solution.py:741
  9.4 1.5 %collective-permute-start.9 = (bf16[160,512]{1,0:T(8,128)(2,1)S(1)}, bf16[160,512]{1,0:T(8,128)(2,1)S(1)}, u32[]{:S(2)}, u32[]{:S(2)}) collective-permute-start(bf16[160,512]{1,0:T(8,128)(2,1)S(1)} %get-tuple-element.75.refs_9_), channel_id=1, source_target_pairs={{0,4},{4,0},{8,12},{12,8},{16,20},{20,16},{24,28},{28,24},{1,5},{5... | collective-permute-start | bytes 491528 | tf_op jit(solution)/shard_map/ppermute | solution.py:741
  10.9 6.2 %collective-permute-done.4.refs_13_ = bf16[160,512]{1,0:T(8,128)(2,1)S(1)} collective-permute-done((bf16[160,512]{1,0:T(8,128)(2,1)S(1)}, bf16[160,512]{1,0:T(8,128)(2,1)S(1)}, u32[]{:S(2)}, u32[]{:S(2)}) %collective-permute-start.4) | collective-permute-done | bytes 163872 | tf_op jit(solution)/shard_map/ppermute | solution.py:741
  18.0 1.2 collective-permute-start.10
  19.2 2.8 %collective-permute-done.8.refs_7_ = bf16[160,2048]{1,0:T(8,128)(2,1)S(1)} collective-permute-done((bf16[160,2048]{1,0:T(8,128)(2,1)S(1)}, bf16[160,2048]{1,0:T(8,128)(2,1)S(1)}, u32[]{:S(2)}, u32[]{:S(2)}) %collective-permute-start.8) | collective-permute-done | bytes 655392 | tf_op jit(solution)/shard_map/ppermute | solution.py:738
  22.0 2.1 %collective-permute-start.12 = (bf16[160,512]{1,0:T(8,128)(2,1)S(1)}, bf16[160,512]{1,0:T(8,128)(2,1)S(1)}, u32[]{:S(2)}, u32[]{:S(2)}) collective-permute-start(bf16[160,512]{1,0:T(8,128)(2,1)S(1)} %collective-permute-done.4.refs_13_), channel_id=1, source_target_pairs={{0,4},{4,0},{8,12},{12,8},{16,20},{20,16},{24,28},{28,24},{1,5},{5... | collective-permute-start | bytes 491528 | tf_op jit(solution)/shard_map/ppermute | solution.py:741
  24.2 1.5 %collective-permute-start.11 = (bf16[160,512]{1,0:T(8,128)(2,1)S(1)}, bf16[160,512]{1,0:T(8,128)(2,1)S(1)}, u32[]{:S(2)}, u32[]{:S(2)}) collective-permute-start(bf16[160,512]{1,0:T(8,128)(2,1)S(1)} %collective-permute-done.9.refs_10_), channel_id=1, source_target_pairs={{0,8},{4,12},{8,0},{12,4},{16,24},{20,28},{24,16},{28,20},{1,9},{5... | collective-permute-start | bytes 491528 | tf_op jit(solution)/shard_map/ppermute | solution.py:741
  28.7 2.2 %collective-permute-done.11.refs_12_ = bf16[160,512]{1,0:T(8,128)(2,1)S(1)} collective-permute-done((bf16[160,512]{1,0:T(8,128)(2,1)S(1)}, bf16[160,512]{1,0:T(8,128)(2,1)S(1)}, u32[]{:S(2)}, u32[]{:S(2)}) %collective-permute-start.11) | collective-permute-done | bytes 163872 | tf_op jit(solution)/shard_map/ppermute | solution.py:741
  31.7 4.0 %collective-permute-done.2.refs_8_ = bf16[160,2048]{1,0:T(8,128)(2,1)S(1)} collective-permute-done((bf16[160,2048]{1,0:T(8,128)(2,1)S(1)}, bf16[160,2048]{1,0:T(8,128)(2,1)S(1)}, u32[]{:S(2)}, u32[]{:S(2)}) %collective-permute-start.2) | collective-permute-done | bytes 655392 | tf_op jit(solution)/shard_map/ppermute | solution.py:738
  38.8 35.1 %layer.2 = (bf16[160,8192]{1,0:T(8,128)(2,1)}, bf16[320,2048]{1,0:T(8,128)(2,1)}, bf16[160,2048]{1,0:T(8,128)(2,1)}, bf16[160,2048]{1,0:T(8,128)(2,1)}, bf16[160...) custom-call(bf16[160,8192]{1,0:T(8,128)(2,1)} %refs_0_.3, bf16[160,8192]{1,0:T(8,128)(2,1)} %copy-done.9, ...), custom_call_target="tpu_custom_call" | custom-call | flops 1 | bytes 1 | tf_op jit(solution)/shard_map/layer/pallas_call | solution.py:492
  74.3 2.1 %collective-permute-start.17 = (bf16[160,2048]{1,0:T(8,128)(2,1)}, bf16[160,2048]{1,0:T(8,128)(2,1)S(1)}, u32[]{:S(2)}, u32[]{:S(2)}) collective-permute-start(bf16[160,2048]{1,0:T(8,128)(2,1)} %get-tuple-element.89), channel_id=1, source_target_pairs={{0,2},{1,3},{2,0},{3,1},{4,6},{5,7},{6,4},{7,5},{8,10},{9,11},{10,... | collective-permute-start | bytes 1966088 | tf_op jit(solution)/shard_map/ppermute | solution.py:738
  76.4 34.7 %layer.3 = (bf16[160,8192]{1,0:T(8,128)(2,1)}, bf16[320,2048]{1,0:T(8,128)(2,1)}, bf16[160,2048]{1,0:T(8,128)(2,1)}, bf16[160,2048]{1,0:T(8,128)(2,1)}, bf16[160...) custom-call(bf16[160,8192]{1,0:T(8,128)(2,1)} %refs_0_.3, ...), custom_call_target="tpu_custom_call", output_to_operand_aliasing={{0}: (11, {})} | custom-call | flops 1 | bytes 1 | tf_op jit(solution)/shard_map/layer/pallas_call | solution.py:492
  111.9 2.0 %collective-permute-start.30 = (bf16[160,2048]{1,0:T(8,128)(2,1)}, bf16[160,2048]{1,0:T(8,128)(2,1)S(1)}, u32[]{:S(2)}, u32[]{:S(2)}) collective-permute-start(bf16[160,2048]{1,0:T(8,128)(2,1)} %get-tuple-element.117), channel_id=1, source_target_pairs={{0,2},{1,3},{2,0},{3,1},{4,6},{5,7},{6,4},{7,5},{8,10},{9,11},{10,... | collective-permute-start | bytes 1966088 | tf_op jit(solution)/shard_map/ppermute | solution.py:738
  113.8 2.5 %collective-permute-done.22.other = bf16[168,512]{1,0:T(8,128)(2,1)S(1)} collective-permute-done((bf16[168,512]{1,0:T(8,128)(2,1)}, bf16[168,512]{1,0:T(8,128)(2,1)S(1)}, u32[]{:S(2)}, u32[]{:S(2)}) %collective-permute-start.22) | collective-permute-done | bytes 172064 | tf_op jit(solution)/shard_map/ppermute | solution.py:738
  117.4 1.9 %collective-permute-start.25 = (bf16[168,512]{1,0:T(8,128)(2,1)S(1)}, bf16[168,512]{1,0:T(8,128)(2,1)S(1)}, u32[]{:S(2)}, u32[]{:S(2)}) collective-permute-start(bf16[168,512]{1,0:T(8,128)(2,1)S(1)} %get-tuple-element.98), channel_id=1, source_target_pairs={{0,4},{4,0},{8,12},{12,8},{16,20},{20,16},{24,28},{28,24},{1,5},{5... | collective-permute-start | bytes 516104 | tf_op jit(solution)/shard_map/ppermute | solution.py:741
  120.7 1.9 %collective-permute-start.23 = (bf16[168,512]{1,0:T(8,128)(2,1)S(1)}, bf16[168,512]{1,0:T(8,128)(2,1)S(1)}, u32[]{:S(2)}, u32[]{:S(2)}) collective-permute-start(bf16[168,512]{1,0:T(8,128)(2,1)S(1)} %get-tuple-element.104), channel_id=1, source_target_pairs={{0,8},{4,12},{8,0},{12,4},{16,24},{20,28},{24,16},{28,20},{1,9},{5... | collective-permute-start | bytes 516104 | tf_op jit(solution)/shard_map/ppermute | solution.py:741
  122.6 2.0 %collective-permute-done.25.refs_0_ = bf16[168,512]{1,0:T(8,128)(2,1)S(1)} collective-permute-done((bf16[168,512]{1,0:T(8,128)(2,1)S(1)}, bf16[168,512]{1,0:T(8,128)(2,1)S(1)}, u32[]{:S(2)}, u32[]{:S(2)}) %collective-permute-start.25) | collective-permute-done | bytes 172064 | tf_op jit(solution)/shard_map/ppermute | solution.py:741
  124.7 1.9 %collective-permute-start.28 = (bf16[168,512]{1,0:T(8,128)(2,1)S(1)}, bf16[168,512]{1,0:T(8,128)(2,1)S(1)}, u32[]{:S(2)}, u32[]{:S(2)}) collective-permute-start(bf16[168,512]{1,0:T(8,128)(2,1)S(1)} %pass_on.3), channel_id=1, source_target_pairs={{0,8},{4,12},{8,0},{12,4},{16,24},{20,28},{24,16},{28,20},{1,9},{5... | collective-permute-start | bytes 516104 | tf_op jit(solution)/shard_map/ppermute | solution.py:741
  129.0 1.8 %collective-permute-start.27 = (bf16[168,512]{1,0:T(8,128)(2,1)S(1)}, bf16[168,512]{1,0:T(8,128)(2,1)S(1)}, u32[]{:S(2)}, u32[]{:S(2)}) collective-permute-start(bf16[168,512]{1,0:T(8,128)(2,1)S(1)} %pass_on.4), channel_id=1, source_target_pairs={{0,4},{4,0},{8,12},{12,8},{16,20},{20,16},{24,28},{28,24},{1,5},{5... | collective-permute-start | bytes 516104 | tf_op jit(solution)/shard_map/ppermute | solution.py:741
  130.9 2.7 %collective-permute-start.29 = (bf16[168,512]{1,0:T(8,128)(2,1)S(1)}, bf16[168,512]{1,0:T(8,128)(2,1)S(1)}, u32[]{:S(2)}, u32[]{:S(2)}) collective-permute-start(bf16[168,512]{1,0:T(8,128)(2,1)S(1)} %pass_on.5), channel_id=1, source_target_pairs={{0,16},{4,20},{8,24},{12,28},{16,0},{20,4},{24,8},{28,12},{1,17},{... | collective-permute-start | bytes 516104 | tf_op jit(solution)/shard_map/ppermute | solution.py:741
  133.5 1.6 %collective-permute-start.24 = (bf16[168,512]{1,0:T(8,128)(2,1)S(1)}, bf16[168,512]{1,0:T(8,128)(2,1)S(1)}, u32[]{:S(2)}, u32[]{:S(2)}) collective-permute-start(bf16[168,512]{1,0:T(8,128)(2,1)S(1)} %get-tuple-element.105), channel_id=1, source_target_pairs={{0,8},{4,12},{8,0},{12,4},{16,24},{20,28},{24,16},{28,20},{1,9},{5... | collective-permute-start | bytes 516104 | tf_op jit(solution)/shard_map/ppermute | solution.py:741
  136.1 5.1 %collective-permute-done.29.r4 = bf16[168,512]{1,0:T(8,128)(2,1)S(1)} collective-permute-done((bf16[168,512]{1,0:T(8,128)(2,1)S(1)}, bf16[168,512]{1,0:T(8,128)(2,1)S(1)}, u32[]{:S(2)}, u32[]{:S(2)}) %collective-permute-start.29) | collective-permute-done | bytes 172064 | tf_op jit(solution)/shard_map/ppermute | solution.py:741
  (106 shorter events, 18.4 us)
Async XLA Ops:
  0.6 16.5 %collective-permute-start = (bf16[160,8192]{1,0:T(8,128)(2,1)}, bf16[160,8192]{1,0:T(8,128)(2,1)S(1)}, u32[]{:S(2)}, u32[]{:S(2)}) collective-permute-start(bf16[160,8192]{1,0:T(8,128)(2,1)} %refs_0_.3), channel_id=1, source_target_pairs={{0,1},{1,0},{2,3},{3,2},{4,5},{5,4},{6,7},{7,6},{8,9},{9,8},{10,11... | collective-permute-start | bytes 7864328 | tf_op jit(solution)/shard_map/ppermute | solution.py:738
  1.1 23.0 %collective-permute-start.1 = (bf16[160,8192]{1,0:T(8,128)(2,1)}, bf16[160,8192]{1,0:T(8,128)(2,1)S(1)}, u32[]{:S(2)}, u32[]{:S(2)}) collective-permute-start(bf16[160,8192]{1,0:T(8,128)(2,1)} %refs_2_.3), channel_id=1, source_target_pairs={{0,1},{1,0},{2,3},{3,2},{4,5},{5,4},{6,7},{7,6},{8,9},{9,8},{10,11... | collective-permute-start | bytes 7864328 | tf_op jit(solution)/shard_map/ppermute | solution.py:738
  3.5 18.5 %collective-permute-start.8 = (bf16[160,2048]{1,0:T(8,128)(2,1)S(1)}, bf16[160,2048]{1,0:T(8,128)(2,1)S(1)}, u32[]{:S(2)}, u32[]{:S(2)}) collective-permute-start(bf16[160,2048]{1,0:T(8,128)(2,1)S(1)} %get-tuple-element.65), channel_id=1, source_target_pairs={{0,2},{1,3},{2,0},{3,1},{4,6},{5,7},{6,4},{7,5},{8,10},{9,11},{10,... | collective-permute-start | bytes 1966088 | tf_op jit(solution)/shard_map/ppermute | solution.py:738
  6.7 10.4 %collective-permute-start.4 = (bf16[160,512]{1,0:T(8,128)(2,1)S(1)}, bf16[160,512]{1,0:T(8,128)(2,1)S(1)}, u32[]{:S(2)}, u32[]{:S(2)}) collective-permute-start(bf16[160,512]{1,0:T(8,128)(2,1)S(1)} %get-tuple-element.75.refs_9_), channel_id=1, source_target_pairs={{0,16},{4,20},{8,24},{12,28},{16,0},{20,4},{24,8},{28,12},{1,17},{... | collective-permute-start | bytes 491528 | tf_op jit(solution)/shard_map/ppermute | solution.py:741
  9.4 8.6 %collective-permute-start.9 = (bf16[160,512]{1,0:T(8,128)(2,1)S(1)}, bf16[160,512]{1,0:T(8,128)(2,1)S(1)}, u32[]{:S(2)}, u32[]{:S(2)}) collective-permute-start(bf16[160,512]{1,0:T(8,128)(2,1)S(1)} %get-tuple-element.75.refs_9_), channel_id=1, source_target_pairs={{0,4},{4,0},{8,12},{12,8},{16,20},{20,16},{24,28},{28,24},{1,5},{5... | collective-permute-start | bytes 491528 | tf_op jit(solution)/shard_map/ppermute | solution.py:741
  17.1 18.6 %collective-permute-start.2 = (bf16[160,2048]{1,0:T(8,128)(2,1)S(1)}, bf16[160,2048]{1,0:T(8,128)(2,1)S(1)}, u32[]{:S(2)}, u32[]{:S(2)}) collective-permute-start(bf16[160,2048]{1,0:T(8,128)(2,1)S(1)} %get-tuple-element.68), channel_id=1, source_target_pairs={{0,3},{1,2},{2,1},{3,0},{4,7},{5,6},{6,5},{7,4},{8,11},{9,10},{10,... | collective-permute-start | bytes 1966088 | tf_op jit(solution)/shard_map/ppermute | solution.py:738
  17.1 7.1 %collective-permute-start.5 = (bf16[160,512]{1,0:T(8,128)(2,1)S(1)}, bf16[160,512]{1,0:T(8,128)(2,1)S(1)}, u32[]{:S(2)}, u32[]{:S(2)}) collective-permute-start(bf16[160,512]{1,0:T(8,128)(2,1)S(1)} %collective-permute-done.4.refs_13_), channel_id=1, source_target_pairs={{0,8},{4,12},{8,0},{12,4},{16,24},{20,28},{24,16},{28,20},{1,9},{5... | collective-permute-start | bytes 491528 | tf_op jit(solution)/shard_map/ppermute | solution.py:741
  18.0 9.8 %collective-permute-start.10 = (bf16[160,512]{1,0:T(8,128)(2,1)S(1)}, bf16[160,512]{1,0:T(8,128)(2,1)S(1)}, u32[]{:S(2)}, u32[]{:S(2)}) collective-permute-start(bf16[160,512]{1,0:T(8,128)(2,1)S(1)} %get-tuple-element.75.refs_9_), channel_id=1, source_target_pairs={{0,8},{4,12},{8,0},{12,4},{16,24},{20,28},{24,16},{28,20},{1,9},{5... | collective-permute-start | bytes 491528 | tf_op jit(solution)/shard_map/ppermute | solution.py:741
  22.0 6.5 %collective-permute-start.12 = (bf16[160,512]{1,0:T(8,128)(2,1)S(1)}, bf16[160,512]{1,0:T(8,128)(2,1)S(1)}, u32[]{:S(2)}, u32[]{:S(2)}) collective-permute-start(bf16[160,512]{1,0:T(8,128)(2,1)S(1)} %collective-permute-done.4.refs_13_), channel_id=1, source_target_pairs={{0,4},{4,0},{8,12},{12,8},{16,20},{20,16},{24,28},{28,24},{1,5},{5... | collective-permute-start | bytes 491528 | tf_op jit(solution)/shard_map/ppermute | solution.py:741
  24.2 6.7 %collective-permute-start.11 = (bf16[160,512]{1,0:T(8,128)(2,1)S(1)}, bf16[160,512]{1,0:T(8,128)(2,1)S(1)}, u32[]{:S(2)}, u32[]{:S(2)}) collective-permute-start(bf16[160,512]{1,0:T(8,128)(2,1)S(1)} %collective-permute-done.9.refs_10_), channel_id=1, source_target_pairs={{0,8},{4,12},{8,0},{12,4},{16,24},{20,28},{24,16},{28,20},{1,9},{5... | collective-permute-start | bytes 491528 | tf_op jit(solution)/shard_map/ppermute | solution.py:741
  27.8 46.2 %collective-permute-start.6 = (bf16[160,2048]{1,0:T(8,128)(2,1)S(1)}, bf16[160,2048]{1,0:T(8,128)(2,1)}, u32[]{:S(2)}, u32[]{:S(2)}) collective-permute-start(bf16[160,2048]{1,0:T(8,128)(2,1)S(1)} %get-tuple-element.73), channel_id=1, source_target_pairs={{0,2},{1,3},{2,0},{3,1},{4,6},{5,7},{6,4},{7,5},{8,10},{9,11},{10,... | collective-permute-start | bytes 1966088 | tf_op jit(solution)/shard_map/ppermute | solution.py:738
  28.6 45.4 %collective-permute-start.7 = (bf16[160,2048]{1,0:T(8,128)(2,1)S(1)}, bf16[160,2048]{1,0:T(8,128)(2,1)}, u32[]{:S(2)}, u32[]{:S(2)}) collective-permute-start(bf16[160,2048]{1,0:T(8,128)(2,1)S(1)} %get-tuple-element.74), channel_id=1, source_target_pairs={{0,3},{1,2},{2,1},{3,0},{4,7},{5,6},{6,5},{7,4},{8,11},{9,10},{10,... | collective-permute-start | bytes 1966088 | tf_op jit(solution)/shard_map/ppermute | solution.py:738
  74.0 37.1 %collective-permute-start.18 = (bf16[320,2048]{1,0:T(8,128)(2,1)}, bf16[320,2048]{1,0:T(8,128)(2,1)S(1)}, u32[]{:S(2)}, u32[]{:S(2)}) collective-permute-start(bf16[320,2048]{1,0:T(8,128)(2,1)} %get-tuple-element.90), channel_id=1, source_target_pairs={{0,1},{1,0},{2,3},{3,2},{4,5},{5,4},{6,7},{7,6},{8,9},{9,8},{10,11... | collective-permute-start | bytes 3932168 | tf_op jit(solution)/shard_map/ppermute | solution.py:738
  74.3 36.8 %collective-permute-start.17 = (bf16[160,2048]{1,0:T(8,128)(2,1)}, bf16[160,2048]{1,0:T(8,128)(2,1)S(1)}, u32[]{:S(2)}, u32[]{:S(2)}) collective-permute-start(bf16[160,2048]{1,0:T(8,128)(2,1)} %get-tuple-element.89), channel_id=1, source_target_pairs={{0,2},{1,3},{2,0},{3,1},{4,6},{5,7},{6,4},{7,5},{8,10},{9,11},{10,... | collective-permute-start | bytes 1966088 | tf_op jit(solution)/shard_map/ppermute | solution.py:738
  76.4 34.7 %collective-permute-start.19 = (bf16[160,2048]{1,0:T(8,128)(2,1)}, bf16[160,2048]{1,0:T(8,128)(2,1)S(1)}, u32[]{:S(2)}, u32[]{:S(2)}) collective-permute-start(bf16[160,2048]{1,0:T(8,128)(2,1)} %get-tuple-element.91), channel_id=1, source_target_pairs={{0,3},{1,2},{2,1},{3,0},{4,7},{5,6},{6,5},{7,4},{8,11},{9,10},{10,... | collective-permute-start | bytes 1966088 | tf_op jit(solution)/shard_map/ppermute | solution.py:738
  111.1 9.1 %collective-permute-start.20 = (bf16[320,2048]{1,0:T(8,128)(2,1)}, bf16[320,2048]{1,0:T(8,128)(2,1)S(1)}, u32[]{:S(2)}, u32[]{:S(2)}) collective-permute-start(bf16[320,2048]{1,0:T(8,128)(2,1)} %get-tuple-element.92), channel_id=1, source_target_pairs={{0,1},{1,0},{2,3},{3,2},{4,5},{5,4},{6,7},{7,6},{8,9},{9,8},{10,11... | collective-permute-start | bytes 3932168 | tf_op jit(solution)/shard_map/ppermute | solution.py:738
  111.3 8.8 %collective-permute-start.21 = (bf16[1120,512]{1,0:T(8,128)(2,1)}, bf16[1120,512]{1,0:T(8,128)(2,1)S(1)}, u32[]{:S(2)}, u32[]{:S(2)}) collective-permute-start(bf16[1120,512]{1,0:T(8,128)(2,1)} %get-tuple-element.94), channel_id=1, source_target_pairs={{0,1},{1,0},{2,3},{3,2},{4,5},{5,4},{6,7},{7,6},{8,9},{9,8},{10,11... | collective-permute-start | bytes 3440648 | tf_op jit(solution)/shard_map/ppermute | solution.py:738
  111.9 23.2 %collective-permute-start.30 = (bf16[160,2048]{1,0:T(8,128)(2,1)}, bf16[160,2048]{1,0:T(8,128)(2,1)S(1)}, u32[]{:S(2)}, u32[]{:S(2)}) collective-permute-start(bf16[160,2048]{1,0:T(8,128)(2,1)} %get-tuple-element.117), channel_id=1, source_target_pairs={{0,2},{1,3},{2,0},{3,1},{4,6},{5,7},{6,4},{7,5},{8,10},{9,11},{10,... | collective-permute-start | bytes 1966088 | tf_op jit(solution)/shard_map/ppermute | solution.py:738
  113.8 28.7 %collective-permute-start.31 = (bf16[160,2048]{1,0:T(8,128)(2,1)}, bf16[160,2048]{1,0:T(8,128)(2,1)S(1)}, u32[]{:S(2)}, u32[]{:S(2)}) collective-permute-start(bf16[160,2048]{1,0:T(8,128)(2,1)} %get-tuple-element.121), channel_id=1, source_target_pairs={{0,3},{1,2},{2,1},{3,0},{4,7},{5,6},{6,5},{7,4},{8,11},{9,10},{10,... | collective-permute-start | bytes 1966088 | tf_op jit(solution)/shard_map/ppermute | solution.py:738
  117.4 7.2 %collective-permute-start.25 = (bf16[168,512]{1,0:T(8,128)(2,1)S(1)}, bf16[168,512]{1,0:T(8,128)(2,1)S(1)}, u32[]{:S(2)}, u32[]{:S(2)}) collective-permute-start(bf16[168,512]{1,0:T(8,128)(2,1)S(1)} %get-tuple-element.98), channel_id=1, source_target_pairs={{0,4},{4,0},{8,12},{12,8},{16,20},{20,16},{24,28},{28,24},{1,5},{5... | collective-permute-start | bytes 516104 | tf_op jit(solution)/shard_map/ppermute | solution.py:741
  120.4 7.4 %collective-permute-start.26 = (bf16[168,512]{1,0:T(8,128)(2,1)S(1)}, bf16[168,512]{1,0:T(8,128)(2,1)S(1)}, u32[]{:S(2)}, u32[]{:S(2)}) collective-permute-start(bf16[168,512]{1,0:T(8,128)(2,1)S(1)} %get-tuple-element.108), channel_id=1, source_target_pairs={{0,4},{4,0},{8,12},{12,8},{16,20},{20,16},{24,28},{28,24},{1,5},{5... | collective-permute-start | bytes 516104 | tf_op jit(solution)/shard_map/ppermute | solution.py:741
  120.7 8.2 %collective-permute-start.23 = (bf16[168,512]{1,0:T(8,128)(2,1)S(1)}, bf16[168,512]{1,0:T(8,128)(2,1)S(1)}, u32[]{:S(2)}, u32[]{:S(2)}) collective-permute-start(bf16[168,512]{1,0:T(8,128)(2,1)S(1)} %get-tuple-element.104), channel_id=1, source_target_pairs={{0,8},{4,12},{8,0},{12,4},{16,24},{20,28},{24,16},{28,20},{1,9},{5... | collective-permute-start | bytes 516104 | tf_op jit(solution)/shard_map/ppermute | solution.py:741
  130.9 10.3 %collective-permute-start.29 = (bf16[168,512]{1,0:T(8,128)(2,1)S(1)}, bf16[168,512]{1,0:T(8,128)(2,1)S(1)}, u32[]{:S(2)}, u32[]{:S(2)}) collective-permute-start(bf16[168,512]{1,0:T(8,128)(2,1)S(1)} %pass_on.5), channel_id=1, source_target_pairs={{0,16},{4,20},{8,24},{12,28},{16,0},{20,4},{24,8},{28,12},{1,17},{... | collective-permute-start | bytes 516104 | tf_op jit(solution)/shard_map/ppermute | solution.py:741
  133.5 7.9 %collective-permute-start.24 = (bf16[168,512]{1,0:T(8,128)(2,1)S(1)}, bf16[168,512]{1,0:T(8,128)(2,1)S(1)}, u32[]{:S(2)}, u32[]{:S(2)}) collective-permute-start(bf16[168,512]{1,0:T(8,128)(2,1)S(1)} %get-tuple-element.105), channel_id=1, source_target_pairs={{0,8},{4,12},{8,0},{12,4},{16,24},{20,28},{24,16},{28,20},{1,9},{5... | collective-permute-start | bytes 516104 | tf_op jit(solution)/shard_map/ppermute | solution.py:741
  (32 other events, 262.4 us)

commit v8 on v7

--- a/solution.py
+++ b/solution.py
@@ -18,7 +18,7 @@
 TILES = LEN // TILE
 CALLS = 2
 REST = (3, 5, 2, 6, 1, 4, 0)
-GROUPS = ((0, 1, 4), (2, 5, 6), (3, 7))
+GROUPS = ((0, 1, 4), (5, 6), (2, 3, 7))
 f32 = jnp.float32
 bf16 = jnp.bfloat16
 ANY = pl.BlockSpec(memory_space=pl.ANY)
@@ -496,7 +496,7 @@
         out_specs=[ANY] * len(outs),
         scratch_shapes=scratch,
         input_output_aliases=alias,
-        compiler_params=pltpu.CompilerParams(vmem_limit_bytes=60 << 20),
+        compiler_params=pltpu.CompilerParams(vmem_limit_bytes=54 << 20),
         cost_estimate=pl.CostEstimate(flops=1, bytes_accessed=1, transcendentals=0),
         name="layer",
     )(*ins)

time: 144 us -> 143 us (level)
  starting transfers between devices: 33.3 us -> 31.5 us
  waiting for transfers between devices: 28.4 us -> 30.1 us
    ppermute x14, waiting for transfers between devices: 17.8 us -> 20.4 us  [dp_move(): return lax.ppermute(v, 'dp', [(i, i ^ j) for i in range(parts)])]
    unnamed x48 -> x46, local copies, waits for them, and re-layouts: 4.26 us -> 3.45 us
  transfers between devices with their start and end apart: 32 -> 32, of which waited for: 13 -> 15; matrix products, arithmetic and copies ran while one was open for 0% -> 0% of each run, Pallas kernels for 53% -> 53%
where the time goes in v8:
time: 143 us
  Pallas kernels  76.7 us (54%)
  starting transfers between devices  31.5 us (22%)
  waiting for transfers between devices  30.1 us (21%)
  local copies, waits for them, and re-layouts  3.45 us (2%)
    pallas_call x2, Pallas kernels, layer(): pl.pallas_call(functools.partial(layer_kernel, k, calls, rows, parts, C,...  69.8 us
    ppermute x14, starting transfers between devices, dp_move(): return lax.ppermute(v, 'dp', [(i, i ^ j) for i in range(parts)])  21.3 us
    ppermute x14, waiting for transfers between devices, dp_move(): return lax.ppermute(v, 'dp', [(i, i ^ j) for i in range(parts)])  20.4 us
    ppermute x18, starting transfers between devices, chan_move(): return lax.ppermute(v, 'chan', [(i, i ^ j) for i in range(chan)])  10.2 us
    ppermute x18, waiting for transfers between devices, chan_move(): return lax.ppermute(v, 'chan', [(i, i ^ j) for i in range(chan)])  9.74 us
    pallas_call x4, Pallas kernels, finish(): pl.pallas_call(functools.partial(finish_kernel, k, rows, mine, C, n), out...  4.07 us
    unnamed x46, local copies, waits for them, and re-layouts  3.45 us
  transfers between devices with their start and end apart: 32, of which 15 were waited for; matrix products, arithmetic and copies ran while one was open for 0% of the time, Pallas kernels for 53%

profile of v8, /device:TPU:0, one launch (start us, length us, event | category | flops | bytes accessed | tf_op | source)
XLA Modules:
  0.0 143.0 jit_solution(3851131543468779171)
XLA Ops:
  1.2 1.7 %copy-done = bf16[160,8192]{1,0:T(8,128)(2,1)S(1)} copy-done((bf16[160,8192]{1,0:T(8,128)(2,1)S(1)}, bf16[160,8192]{1,0:T(8,128)(2,1)}, u32[]{:S(2)}) %copy-start) | copy-done | bytes 2621464
  3.5 3.0 %collective-permute-start.8 = (bf16[160,2048]{1,0:T(8,128)(2,1)S(1)}, bf16[160,2048]{1,0:T(8,128)(2,1)S(1)}, u32[]{:S(2)}, u32[]{:S(2)}) collective-permute-start(bf16[160,2048]{1,0:T(8,128)(2,1)S(1)} %get-tuple-element.65), channel_id=1, source_target_pairs={{0,2},{1,3},{2,0},{3,1},{4,6},{5,7},{6,4},{7,5},{8,10},{9,11},{10,... | collective-permute-start | bytes 1966088 | tf_op jit(solution)/shard_map/ppermute | solution.py:738
  6.7 2.7 %collective-permute-start.4 = (bf16[160,512]{1,0:T(8,128)(2,1)S(1)}, bf16[160,512]{1,0:T(8,128)(2,1)S(1)}, u32[]{:S(2)}, u32[]{:S(2)}) collective-permute-start(bf16[160,512]{1,0:T(8,128)(2,1)S(1)} %get-tuple-element.75.refs_9_), channel_id=1, source_target_pairs={{0,16},{4,20},{8,24},{12,28},{16,0},{20,4},{24,8},{28,12},{1,17},{... | collective-permute-start | bytes 491528 | tf_op jit(solution)/shard_map/ppermute | solution.py:741
  9.4 1.5 %collective-permute-start.9 = (bf16[160,512]{1,0:T(8,128)(2,1)S(1)}, bf16[160,512]{1,0:T(8,128)(2,1)S(1)}, u32[]{:S(2)}, u32[]{:S(2)}) collective-permute-start(bf16[160,512]{1,0:T(8,128)(2,1)S(1)} %get-tuple-element.75.refs_9_), channel_id=1, source_target_pairs={{0,4},{4,0},{8,12},{12,8},{16,20},{20,16},{24,28},{28,24},{1,5},{5... | collective-permute-start | bytes 491528 | tf_op jit(solution)/shard_map/ppermute | solution.py:741
  10.9 6.2 %collective-permute-done.4.refs_13_ = bf16[160,512]{1,0:T(8,128)(2,1)S(1)} collective-permute-done((bf16[160,512]{1,0:T(8,128)(2,1)S(1)}, bf16[160,512]{1,0:T(8,128)(2,1)S(1)}, u32[]{:S(2)}, u32[]{:S(2)}) %collective-permute-start.4) | collective-permute-done | bytes 163872 | tf_op jit(solution)/shard_map/ppermute | solution.py:741
  17.8 1.5 %collective-permute-start.10 = (bf16[160,512]{1,0:T(8,128)(2,1)S(1)}, bf16[160,512]{1,0:T(8,128)(2,1)S(1)}, u32[]{:S(2)}, u32[]{:S(2)}) collective-permute-start(bf16[160,512]{1,0:T(8,128)(2,1)S(1)} %get-tuple-element.75.refs_9_), channel_id=1, source_target_pairs={{0,8},{4,12},{8,0},{12,4},{16,24},{20,28},{24,16},{28,20},{1,9},{5... | collective-permute-start | bytes 491528 | tf_op jit(solution)/shard_map/ppermute | solution.py:741
  19.3 2.8 %collective-permute-done.8.refs_7_ = bf16[160,2048]{1,0:T(8,128)(2,1)S(1)} collective-permute-done((bf16[160,2048]{1,0:T(8,128)(2,1)S(1)}, bf16[160,2048]{1,0:T(8,128)(2,1)S(1)}, u32[]{:S(2)}, u32[]{:S(2)}) %collective-permute-start.8) | collective-permute-done | bytes 655392 | tf_op jit(solution)/shard_map/ppermute | solution.py:738
  22.0 1.9 %collective-permute-done.5.refs_15_ = bf16[160,512]{1,0:T(8,128)(2,1)S(1)} collective-permute-done((bf16[160,512]{1,0:T(8,128)(2,1)S(1)}, bf16[160,512]{1,0:T(8,128)(2,1)S(1)}, u32[]{:S(2)}, u32[]{:S(2)}) %collective-permute-start.5) | collective-permute-done | bytes 163872 | tf_op jit(solution)/shard_map/ppermute | solution.py:741
  24.8 1.5 %collective-permute-start.13 = (bf16[160,512]{1,0:T(8,128)(2,1)S(1)}, bf16[160,512]{1,0:T(8,128)(2,1)S(1)}, u32[]{:S(2)}, u32[]{:S(2)}) collective-permute-start(bf16[160,512]{1,0:T(8,128)(2,1)S(1)} %collective-permute-done.5.refs_15_), channel_id=1, source_target_pairs={{0,4},{4,0},{8,12},{12,8},{16,20},{20,16},{24,28},{28,24},{1,5},{5... | collective-permute-start | bytes 491528 | tf_op jit(solution)/shard_map/ppermute | solution.py:741
  30.7 1.7 %collective-permute-done.12.refs_14_ = bf16[160,512]{1,0:T(8,128)(2,1)S(1)} collective-permute-done((bf16[160,512]{1,0:T(8,128)(2,1)S(1)}, bf16[160,512]{1,0:T(8,128)(2,1)S(1)}, u32[]{:S(2)}, u32[]{:S(2)}) %collective-permute-start.12) | collective-permute-done | bytes 163872 | tf_op jit(solution)/shard_map/ppermute | solution.py:741
  32.5 3.2 %collective-permute-done.2.refs_8_ = bf16[160,2048]{1,0:T(8,128)(2,1)S(1)} collective-permute-done((bf16[160,2048]{1,0:T(8,128)(2,1)S(1)}, bf16[160,2048]{1,0:T(8,128)(2,1)S(1)}, u32[]{:S(2)}, u32[]{:S(2)}) %collective-permute-start.2) | collective-permute-done | bytes 655392 | tf_op jit(solution)/shard_map/ppermute | solution.py:738
  38.1 35.1 %layer.2 = (bf16[160,8192]{1,0:T(8,128)(2,1)}, bf16[320,2048]{1,0:T(8,128)(2,1)}, bf16[160,2048]{1,0:T(8,128)(2,1)}, bf16[160,2048]{1,0:T(8,128)(2,1)}, bf16[160...) custom-call(bf16[160,8192]{1,0:T(8,128)(2,1)} %refs_0_.3, bf16[160,8192]{1,0:T(8,128)(2,1)} %copy-done.9, ...), custom_call_target="tpu_custom_call" | custom-call | flops 1 | bytes 1 | tf_op jit(solution)/shard_map/layer/pallas_call | solution.py:492
  73.5 2.1 %collective-permute-start.17 = (bf16[160,2048]{1,0:T(8,128)(2,1)}, bf16[160,2048]{1,0:T(8,128)(2,1)S(1)}, u32[]{:S(2)}, u32[]{:S(2)}) collective-permute-start(bf16[160,2048]{1,0:T(8,128)(2,1)} %get-tuple-element.89), channel_id=1, source_target_pairs={{0,2},{1,3},{2,0},{3,1},{4,6},{5,7},{6,4},{7,5},{8,10},{9,11},{10,... | collective-permute-start | bytes 1966088 | tf_op jit(solution)/shard_map/ppermute | solution.py:738
  75.5 34.7 %layer.3 = (bf16[160,8192]{1,0:T(8,128)(2,1)}, bf16[320,2048]{1,0:T(8,128)(2,1)}, bf16[160,2048]{1,0:T(8,128)(2,1)}, bf16[160,2048]{1,0:T(8,128)(2,1)}, bf16[160...) custom-call(bf16[160,8192]{1,0:T(8,128)(2,1)} %refs_0_.3, ...), custom_call_target="tpu_custom_call", output_to_operand_aliasing={{0}: (11, {})} | custom-call | flops 1 | bytes 1 | tf_op jit(solution)/shard_map/layer/pallas_call | solution.py:492
  111.0 2.0 %collective-permute-start.30 = (bf16[160,2048]{1,0:T(8,128)(2,1)}, bf16[160,2048]{1,0:T(8,128)(2,1)S(1)}, u32[]{:S(2)}, u32[]{:S(2)}) collective-permute-start(bf16[160,2048]{1,0:T(8,128)(2,1)} %get-tuple-element.117), channel_id=1, source_target_pairs={{0,2},{1,3},{2,0},{3,1},{4,6},{5,7},{6,4},{7,5},{8,10},{9,11},{10,... | collective-permute-start | bytes 1966088 | tf_op jit(solution)/shard_map/ppermute | solution.py:738
  113.0 2.5 %collective-permute-done.22.other = bf16[168,512]{1,0:T(8,128)(2,1)S(1)} collective-permute-done((bf16[168,512]{1,0:T(8,128)(2,1)}, bf16[168,512]{1,0:T(8,128)(2,1)S(1)}, u32[]{:S(2)}, u32[]{:S(2)}) %collective-permute-start.22) | collective-permute-done | bytes 172064 | tf_op jit(solution)/shard_map/ppermute | solution.py:738
  116.5 1.9 %collective-permute-start.25 = (bf16[168,512]{1,0:T(8,128)(2,1)S(1)}, bf16[168,512]{1,0:T(8,128)(2,1)S(1)}, u32[]{:S(2)}, u32[]{:S(2)}) collective-permute-start(bf16[168,512]{1,0:T(8,128)(2,1)S(1)} %get-tuple-element.98), channel_id=1, source_target_pairs={{0,4},{4,0},{8,12},{12,8},{16,20},{20,16},{24,28},{28,24},{1,5},{5... | collective-permute-start | bytes 516104 | tf_op jit(solution)/shard_map/ppermute | solution.py:741
  120.0 1.9 %collective-permute-start.23 = (bf16[168,512]{1,0:T(8,128)(2,1)S(1)}, bf16[168,512]{1,0:T(8,128)(2,1)S(1)}, u32[]{:S(2)}, u32[]{:S(2)}) collective-permute-start(bf16[168,512]{1,0:T(8,128)(2,1)S(1)} %get-tuple-element.104), channel_id=1, source_target_pairs={{0,8},{4,12},{8,0},{12,4},{16,24},{20,28},{24,16},{28,20},{1,9},{5... | collective-permute-start | bytes 516104 | tf_op jit(solution)/shard_map/ppermute | solution.py:741
  121.9 1.9 %collective-permute-done.25.refs_0_ = bf16[168,512]{1,0:T(8,128)(2,1)S(1)} collective-permute-done((bf16[168,512]{1,0:T(8,128)(2,1)S(1)}, bf16[168,512]{1,0:T(8,128)(2,1)S(1)}, u32[]{:S(2)}, u32[]{:S(2)}) %collective-permute-start.25) | collective-permute-done | bytes 172064 | tf_op jit(solution)/shard_map/ppermute | solution.py:741
  123.8 1.9 %collective-permute-start.28 = (bf16[168,512]{1,0:T(8,128)(2,1)S(1)}, bf16[168,512]{1,0:T(8,128)(2,1)S(1)}, u32[]{:S(2)}, u32[]{:S(2)}) collective-permute-start(bf16[168,512]{1,0:T(8,128)(2,1)S(1)} %pass_on.3), channel_id=1, source_target_pairs={{0,8},{4,12},{8,0},{12,4},{16,24},{20,28},{24,16},{28,20},{1,9},{5... | collective-permute-start | bytes 516104 | tf_op jit(solution)/shard_map/ppermute | solution.py:741
  128.2 1.8 %collective-permute-start.27 = (bf16[168,512]{1,0:T(8,128)(2,1)S(1)}, bf16[168,512]{1,0:T(8,128)(2,1)S(1)}, u32[]{:S(2)}, u32[]{:S(2)}) collective-permute-start(bf16[168,512]{1,0:T(8,128)(2,1)S(1)} %pass_on.4), channel_id=1, source_target_pairs={{0,4},{4,0},{8,12},{12,8},{16,20},{20,16},{24,28},{28,24},{1,5},{5... | collective-permute-start | bytes 516104 | tf_op jit(solution)/shard_map/ppermute | solution.py:741
  130.1 2.6 %collective-permute-start.29 = (bf16[168,512]{1,0:T(8,128)(2,1)S(1)}, bf16[168,512]{1,0:T(8,128)(2,1)S(1)}, u32[]{:S(2)}, u32[]{:S(2)}) collective-permute-start(bf16[168,512]{1,0:T(8,128)(2,1)S(1)} %pass_on.5), channel_id=1, source_target_pairs={{0,16},{4,20},{8,24},{12,28},{16,0},{20,4},{24,8},{28,12},{1,17},{... | collective-permute-start | bytes 516104 | tf_op jit(solution)/shard_map/ppermute | solution.py:741
  132.6 1.7 %collective-permute-start.24 = (bf16[168,512]{1,0:T(8,128)(2,1)S(1)}, bf16[168,512]{1,0:T(8,128)(2,1)S(1)}, u32[]{:S(2)}, u32[]{:S(2)}) collective-permute-start(bf16[168,512]{1,0:T(8,128)(2,1)S(1)} %get-tuple-element.105), channel_id=1, source_target_pairs={{0,8},{4,12},{8,0},{12,4},{16,24},{20,28},{24,16},{28,20},{1,9},{5... | collective-permute-start | bytes 516104 | tf_op jit(solution)/shard_map/ppermute | solution.py:741
  135.3 5.0 %collective-permute-done.29.r4 = bf16[168,512]{1,0:T(8,128)(2,1)S(1)} collective-permute-done((bf16[168,512]{1,0:T(8,128)(2,1)S(1)}, bf16[168,512]{1,0:T(8,128)(2,1)S(1)}, u32[]{:S(2)}, u32[]{:S(2)}) %collective-permute-start.29) | collective-permute-done | bytes 172064 | tf_op jit(solution)/shard_map/ppermute | solution.py:741
  (104 shorter events, 19.1 us)
Async XLA Ops:
  0.6 16.5 %collective-permute-start = (bf16[160,8192]{1,0:T(8,128)(2,1)}, bf16[160,8192]{1,0:T(8,128)(2,1)S(1)}, u32[]{:S(2)}, u32[]{:S(2)}) collective-permute-start(bf16[160,8192]{1,0:T(8,128)(2,1)} %refs_0_.3), channel_id=1, source_target_pairs={{0,1},{1,0},{2,3},{3,2},{4,5},{5,4},{6,7},{7,6},{8,9},{9,8},{10,11... | collective-permute-start | bytes 7864328 | tf_op jit(solution)/shard_map/ppermute | solution.py:738
  1.1 20.9 %collective-permute-start.1 = (bf16[160,8192]{1,0:T(8,128)(2,1)}, bf16[160,8192]{1,0:T(8,128)(2,1)S(1)}, u32[]{:S(2)}, u32[]{:S(2)}) collective-permute-start(bf16[160,8192]{1,0:T(8,128)(2,1)} %refs_2_.3), channel_id=1, source_target_pairs={{0,1},{1,0},{2,3},{3,2},{4,5},{5,4},{6,7},{7,6},{8,9},{9,8},{10,11... | collective-permute-start | bytes 7864328 | tf_op jit(solution)/shard_map/ppermute | solution.py:738
  3.5 18.5 %collective-permute-start.8 = (bf16[160,2048]{1,0:T(8,128)(2,1)S(1)}, bf16[160,2048]{1,0:T(8,128)(2,1)S(1)}, u32[]{:S(2)}, u32[]{:S(2)}) collective-permute-start(bf16[160,2048]{1,0:T(8,128)(2,1)S(1)} %get-tuple-element.65), channel_id=1, source_target_pairs={{0,2},{1,3},{2,0},{3,1},{4,6},{5,7},{6,4},{7,5},{8,10},{9,11},{10,... | collective-permute-start | bytes 1966088 | tf_op jit(solution)/shard_map/ppermute | solution.py:738
  6.7 10.4 %collective-permute-start.4 = (bf16[160,512]{1,0:T(8,128)(2,1)S(1)}, bf16[160,512]{1,0:T(8,128)(2,1)S(1)}, u32[]{:S(2)}, u32[]{:S(2)}) collective-permute-start(bf16[160,512]{1,0:T(8,128)(2,1)S(1)} %get-tuple-element.75.refs_9_), channel_id=1, source_target_pairs={{0,16},{4,20},{8,24},{12,28},{16,0},{20,4},{24,8},{28,12},{1,17},{... | collective-permute-start | bytes 491528 | tf_op jit(solution)/shard_map/ppermute | solution.py:741
  9.4 8.4 %collective-permute-start.9 = (bf16[160,512]{1,0:T(8,128)(2,1)S(1)}, bf16[160,512]{1,0:T(8,128)(2,1)S(1)}, u32[]{:S(2)}, u32[]{:S(2)}) collective-permute-start(bf16[160,512]{1,0:T(8,128)(2,1)S(1)} %get-tuple-element.75.refs_9_), channel_id=1, source_target_pairs={{0,4},{4,0},{8,12},{12,8},{16,20},{20,16},{24,28},{28,24},{1,5},{5... | collective-permute-start | bytes 491528 | tf_op jit(solution)/shard_map/ppermute | solution.py:741
  17.1 6.9 %collective-permute-start.5 = (bf16[160,512]{1,0:T(8,128)(2,1)S(1)}, bf16[160,512]{1,0:T(8,128)(2,1)S(1)}, u32[]{:S(2)}, u32[]{:S(2)}) collective-permute-start(bf16[160,512]{1,0:T(8,128)(2,1)S(1)} %collective-permute-done.4.refs_13_), channel_id=1, source_target_pairs={{0,8},{4,12},{8,0},{12,4},{16,24},{20,28},{24,16},{28,20},{1,9},{5... | collective-permute-start | bytes 491528 | tf_op jit(solution)/shard_map/ppermute | solution.py:741
  17.8 17.9 %collective-permute-start.2 = (bf16[160,2048]{1,0:T(8,128)(2,1)S(1)}, bf16[160,2048]{1,0:T(8,128)(2,1)S(1)}, u32[]{:S(2)}, u32[]{:S(2)}) collective-permute-start(bf16[160,2048]{1,0:T(8,128)(2,1)S(1)} %get-tuple-element.68), channel_id=1, source_target_pairs={{0,3},{1,2},{2,1},{3,0},{4,7},{5,6},{6,5},{7,4},{8,11},{9,10},{10,... | collective-permute-start | bytes 1966088 | tf_op jit(solution)/shard_map/ppermute | solution.py:738
  17.8 9.7 %collective-permute-start.10 = (bf16[160,512]{1,0:T(8,128)(2,1)S(1)}, bf16[160,512]{1,0:T(8,128)(2,1)S(1)}, u32[]{:S(2)}, u32[]{:S(2)}) collective-permute-start(bf16[160,512]{1,0:T(8,128)(2,1)S(1)} %get-tuple-element.75.refs_9_), channel_id=1, source_target_pairs={{0,8},{4,12},{8,0},{12,4},{16,24},{20,28},{24,16},{28,20},{1,9},{5... | collective-permute-start | bytes 491528 | tf_op jit(solution)/shard_map/ppermute | solution.py:741
  27.5 45.7 %collective-permute-start.6 = (bf16[160,2048]{1,0:T(8,128)(2,1)S(1)}, bf16[160,2048]{1,0:T(8,128)(2,1)}, u32[]{:S(2)}, u32[]{:S(2)}) collective-permute-start(bf16[160,2048]{1,0:T(8,128)(2,1)S(1)} %get-tuple-element.73), channel_id=1, source_target_pairs={{0,2},{1,3},{2,0},{3,1},{4,6},{5,7},{6,4},{7,5},{8,10},{9,11},{10,... | collective-permute-start | bytes 1966088 | tf_op jit(solution)/shard_map/ppermute | solution.py:738
  29.5 43.7 %collective-permute-start.7 = (bf16[160,2048]{1,0:T(8,128)(2,1)S(1)}, bf16[160,2048]{1,0:T(8,128)(2,1)}, u32[]{:S(2)}, u32[]{:S(2)}) collective-permute-start(bf16[160,2048]{1,0:T(8,128)(2,1)S(1)} %get-tuple-element.74), channel_id=1, source_target_pairs={{0,3},{1,2},{2,1},{3,0},{4,7},{5,6},{6,5},{7,4},{8,11},{9,10},{10,... | collective-permute-start | bytes 1966088 | tf_op jit(solution)/shard_map/ppermute | solution.py:738
  73.2 37.1 %collective-permute-start.18 = (bf16[320,2048]{1,0:T(8,128)(2,1)}, bf16[320,2048]{1,0:T(8,128)(2,1)S(1)}, u32[]{:S(2)}, u32[]{:S(2)}) collective-permute-start(bf16[320,2048]{1,0:T(8,128)(2,1)} %get-tuple-element.90), channel_id=1, source_target_pairs={{0,1},{1,0},{2,3},{3,2},{4,5},{5,4},{6,7},{7,6},{8,9},{9,8},{10,11... | collective-permute-start | bytes 3932168 | tf_op jit(solution)/shard_map/ppermute | solution.py:738
  73.5 36.8 %collective-permute-start.17 = (bf16[160,2048]{1,0:T(8,128)(2,1)}, bf16[160,2048]{1,0:T(8,128)(2,1)S(1)}, u32[]{:S(2)}, u32[]{:S(2)}) collective-permute-start(bf16[160,2048]{1,0:T(8,128)(2,1)} %get-tuple-element.89), channel_id=1, source_target_pairs={{0,2},{1,3},{2,0},{3,1},{4,6},{5,7},{6,4},{7,5},{8,10},{9,11},{10,... | collective-permute-start | bytes 1966088 | tf_op jit(solution)/shard_map/ppermute | solution.py:738
  75.5 34.8 %collective-permute-start.19 = (bf16[160,2048]{1,0:T(8,128)(2,1)}, bf16[160,2048]{1,0:T(8,128)(2,1)S(1)}, u32[]{:S(2)}, u32[]{:S(2)}) collective-permute-start(bf16[160,2048]{1,0:T(8,128)(2,1)} %get-tuple-element.91), channel_id=1, source_target_pairs={{0,3},{1,2},{2,1},{3,0},{4,7},{5,6},{6,5},{7,4},{8,11},{9,10},{10,... | collective-permute-start | bytes 1966088 | tf_op jit(solution)/shard_map/ppermute | solution.py:738
  110.3 9.1 %collective-permute-start.20 = (bf16[320,2048]{1,0:T(8,128)(2,1)}, bf16[320,2048]{1,0:T(8,128)(2,1)S(1)}, u32[]{:S(2)}, u32[]{:S(2)}) collective-permute-start(bf16[320,2048]{1,0:T(8,128)(2,1)} %get-tuple-element.92), channel_id=1, source_target_pairs={{0,1},{1,0},{2,3},{3,2},{4,5},{5,4},{6,7},{7,6},{8,9},{9,8},{10,11... | collective-permute-start | bytes 3932168 | tf_op jit(solution)/shard_map/ppermute | solution.py:738
  110.5 8.9 %collective-permute-start.21 = (bf16[1120,512]{1,0:T(8,128)(2,1)}, bf16[1120,512]{1,0:T(8,128)(2,1)S(1)}, u32[]{:S(2)}, u32[]{:S(2)}) collective-permute-start(bf16[1120,512]{1,0:T(8,128)(2,1)} %get-tuple-element.94), channel_id=1, source_target_pairs={{0,1},{1,0},{2,3},{3,2},{4,5},{5,4},{6,7},{7,6},{8,9},{9,8},{10,11... | collective-permute-start | bytes 3440648 | tf_op jit(solution)/shard_map/ppermute | solution.py:738
  111.0 23.4 %collective-permute-start.30 = (bf16[160,2048]{1,0:T(8,128)(2,1)}, bf16[160,2048]{1,0:T(8,128)(2,1)S(1)}, u32[]{:S(2)}, u32[]{:S(2)}) collective-permute-start(bf16[160,2048]{1,0:T(8,128)(2,1)} %get-tuple-element.117), channel_id=1, source_target_pairs={{0,2},{1,3},{2,0},{3,1},{4,6},{5,7},{6,4},{7,5},{8,10},{9,11},{10,... | collective-permute-start | bytes 1966088 | tf_op jit(solution)/shard_map/ppermute | solution.py:738
  113.0 28.7 %collective-permute-start.31 = (bf16[160,2048]{1,0:T(8,128)(2,1)}, bf16[160,2048]{1,0:T(8,128)(2,1)S(1)}, u32[]{:S(2)}, u32[]{:S(2)}) collective-permute-start(bf16[160,2048]{1,0:T(8,128)(2,1)} %get-tuple-element.121), channel_id=1, source_target_pairs={{0,3},{1,2},{2,1},{3,0},{4,7},{5,6},{6,5},{7,4},{8,11},{9,10},{10,... | collective-permute-start | bytes 1966088 | tf_op jit(solution)/shard_map/ppermute | solution.py:738
  116.5 7.2 %collective-permute-start.25 = (bf16[168,512]{1,0:T(8,128)(2,1)S(1)}, bf16[168,512]{1,0:T(8,128)(2,1)S(1)}, u32[]{:S(2)}, u32[]{:S(2)}) collective-permute-start(bf16[168,512]{1,0:T(8,128)(2,1)S(1)} %get-tuple-element.98), channel_id=1, source_target_pairs={{0,4},{4,0},{8,12},{12,8},{16,20},{20,16},{24,28},{28,24},{1,5},{5... | collective-permute-start | bytes 516104 | tf_op jit(solution)/shard_map/ppermute | solution.py:741
  119.7 7.3 %collective-permute-start.26 = (bf16[168,512]{1,0:T(8,128)(2,1)S(1)}, bf16[168,512]{1,0:T(8,128)(2,1)S(1)}, u32[]{:S(2)}, u32[]{:S(2)}) collective-permute-start(bf16[168,512]{1,0:T(8,128)(2,1)S(1)} %get-tuple-element.108), channel_id=1, source_target_pairs={{0,4},{4,0},{8,12},{12,8},{16,20},{20,16},{24,28},{28,24},{1,5},{5... | collective-permute-start | bytes 516104 | tf_op jit(solution)/shard_map/ppermute | solution.py:741
  120.0 8.1 %collective-permute-start.23 = (bf16[168,512]{1,0:T(8,128)(2,1)S(1)}, bf16[168,512]{1,0:T(8,128)(2,1)S(1)}, u32[]{:S(2)}, u32[]{:S(2)}) collective-permute-start(bf16[168,512]{1,0:T(8,128)(2,1)S(1)} %get-tuple-element.104), channel_id=1, source_target_pairs={{0,8},{4,12},{8,0},{12,4},{16,24},{20,28},{24,16},{28,20},{1,9},{5... | collective-permute-start | bytes 516104 | tf_op jit(solution)/shard_map/ppermute | solution.py:741
  123.8 6.1 %collective-permute-start.28 = (bf16[168,512]{1,0:T(8,128)(2,1)S(1)}, bf16[168,512]{1,0:T(8,128)(2,1)S(1)}, u32[]{:S(2)}, u32[]{:S(2)}) collective-permute-start(bf16[168,512]{1,0:T(8,128)(2,1)S(1)} %pass_on.3), channel_id=1, source_target_pairs={{0,8},{4,12},{8,0},{12,4},{16,24},{20,28},{24,16},{28,20},{1,9},{5... | collective-permute-start | bytes 516104 | tf_op jit(solution)/shard_map/ppermute | solution.py:741
  128.2 6.2 %collective-permute-start.27 = (bf16[168,512]{1,0:T(8,128)(2,1)S(1)}, bf16[168,512]{1,0:T(8,128)(2,1)S(1)}, u32[]{:S(2)}, u32[]{:S(2)}) collective-permute-start(bf16[168,512]{1,0:T(8,128)(2,1)S(1)} %pass_on.4), channel_id=1, source_target_pairs={{0,4},{4,0},{8,12},{12,8},{16,20},{20,16},{24,28},{28,24},{1,5},{5... | collective-permute-start | bytes 516104 | tf_op jit(solution)/shard_map/ppermute | solution.py:741
  130.1 10.3 %collective-permute-start.29 = (bf16[168,512]{1,0:T(8,128)(2,1)S(1)}, bf16[168,512]{1,0:T(8,128)(2,1)S(1)}, u32[]{:S(2)}, u32[]{:S(2)}) collective-permute-start(bf16[168,512]{1,0:T(8,128)(2,1)S(1)} %pass_on.5), channel_id=1, source_target_pairs={{0,16},{4,20},{8,24},{12,28},{16,0},{20,4},{24,8},{28,12},{1,17},{... | collective-permute-start | bytes 516104 | tf_op jit(solution)/shard_map/ppermute | solution.py:741
  132.6 7.9 %collective-permute-start.24 = (bf16[168,512]{1,0:T(8,128)(2,1)S(1)}, bf16[168,512]{1,0:T(8,128)(2,1)S(1)}, u32[]{:S(2)}, u32[]{:S(2)}) collective-permute-start(bf16[168,512]{1,0:T(8,128)(2,1)S(1)} %get-tuple-element.105), channel_id=1, source_target_pairs={{0,8},{4,12},{8,0},{12,4},{16,24},{20,28},{24,16},{28,20},{1,9},{5... | collective-permute-start | bytes 516104 | tf_op jit(solution)/shard_map/ppermute | solution.py:741
  (31 other events, 273.0 us)
